TPU v7x, 1024 devices: a whole 4x8x16 slice. The times are simulated.
1024 devices in a mesh: ta: 64 (over z, x), xyz: 16 (over y, core).
Axes of the slice: x: 4, y: 8, z: 16, core: 2. Of those that a mesh axis runs over, the one named last changes fastest.
Arguments:
- right_side: bfloat16 [64, 16, 2, 2, 128], P('ta', 'xyz'), may hold values from -24 to 24
- self_block: bfloat16 [64, 16, 2, 2, 64, 128], P('ta', 'xyz'), may hold values from -1 to 4
- hop_blocks: bfloat16 [64, 16, 2, 2, 4, 64, 128], P('ta', 'xyz'), may hold values from -0.125 to 0.125
Outputs:
- solution: float32 [64, 16, 2, 2, 128], P('ta', 'xyz')
- final_residual: float32 [64, 16, 2, 2, 128], P('ta', 'xyz')
All inputs are finite; a program needn't handle non-finite values.
Results may differ from a plain program's by a relative error of at most 0.011.
Values may be sent and summed in bfloat16 or wider, within the bound.
No kernel may reach another device: no remote copies, remote signals or barrier semaphores. Data moves between devices by JAX's collectives and lax.ppermute only.
A program may use at most 32 MiB of HBM per device.

v0:
```python
import jax
import jax.numpy as jnp
from jax import lax
from jax.sharding import PartitionSpec as P

ITERS = 3


def shifted(block, axis, distance):
    devices = range(lax.axis_size(axis))
    route = [((i - distance) % len(devices), i) for i in devices]
    return lax.ppermute(block, axis, route)


def chirality_signs(full_width):
    half_width = full_width // 2
    quarter = full_width // 4
    column = jnp.arange(full_width) % half_width
    return jnp.where(column < quarter, 1.0, -1.0).astype(jnp.float32)


def time_rim(rim_piece, offset):
    return shifted(rim_piece, "ta", offset)


def space_rim(rim_piece, offset):
    return shifted(rim_piece, "xyz", offset)


def forward_sum(blocks, vectors):
    half_width = blocks.shape[-2]
    plain_order = jnp.concatenate([vectors[..., :half_width], -vectors[..., half_width:]], -1)
    turned = jnp.concatenate([vectors[..., half_width:], vectors[..., :half_width]], -1)
    real_out = jnp.einsum(
        "tzyxhab,tzyxhb->tzyxa", blocks, plain_order, preferred_element_type=jnp.float32
    )
    imag_out = jnp.einsum(
        "tzyxhab,tzyxhb->tzyxa", blocks, turned, preferred_element_type=jnp.float32
    )
    return jnp.concatenate([real_out, imag_out], -1)


def apply_operator(vector_field, self_block, hop_blocks):
    half_width = self_block.shape[-2]
    rounded = vector_field.astype(jnp.bfloat16)
    chiral_signs = chirality_signs(vector_field.shape[-1])
    flipped = rounded * chiral_signs.astype(jnp.bfloat16)
    from_real = jnp.einsum(
        "tzyxhab,tzyxa->tzyxhb",
        hop_blocks,
        flipped[..., :half_width],
        preferred_element_type=jnp.float32,
    )
    from_imag = jnp.einsum(
        "tzyxhab,tzyxa->tzyxhb",
        hop_blocks,
        flipped[..., half_width:],
        preferred_element_type=jnp.float32,
    )
    carried = jnp.concatenate(
        [
            from_real[..., :half_width] + from_imag[..., half_width:],
            from_imag[..., :half_width] - from_real[..., half_width:],
        ],
        -1,
    ).astype(jnp.bfloat16)
    ahead_x = jnp.roll(rounded, -1, 3)
    ahead_y = jnp.roll(rounded, -1, 2)
    ahead_z = jnp.concatenate([rounded[:, 1:], space_rim(rounded, -1)], 1)
    ahead_t = jnp.concatenate([rounded[1:], time_rim(rounded, -1)], 0)
    ahead_all = jnp.stack([ahead_x, ahead_y, ahead_z, ahead_t], 4)
    summed = forward_sum(self_block[..., None, :, :], rounded[..., None, :]) + forward_sum(
        hop_blocks, ahead_all
    )
    behind_x = jnp.roll(carried[:, :, :, :, 0], 1, 3)
    behind_y = jnp.roll(carried[:, :, :, :, 1], 1, 2)
    behind_z = jnp.concatenate(
        [space_rim(carried[:, -1:, :, :, 2], 1), carried[:, :-1, :, :, 2]], 1
    )
    behind_t = jnp.concatenate([time_rim(carried[-1:, :, :, :, 3], 1), carried[:-1, :, :, :, 3]], 0)
    behind_sum = (
        behind_x.astype(jnp.float32)
        + behind_y.astype(jnp.float32)
        + behind_z.astype(jnp.float32)
        + behind_t.astype(jnp.float32)
    )
    return summed + chiral_signs * behind_sum


def inner_pair(left_vec, right_vec):
    half_width = left_vec.shape[-1] // 2
    real_part = jnp.sum(
        left_vec[..., :half_width] * right_vec[..., :half_width]
        + left_vec[..., half_width:] * right_vec[..., half_width:]
    )
    imag_part = jnp.sum(
        left_vec[..., :half_width] * right_vec[..., half_width:]
        - left_vec[..., half_width:] * right_vec[..., :half_width]
    )
    return (real_part, imag_part)


def scale_complex(real_part, imag_part, vector):
    half_width = vector.shape[-1] // 2
    vec_re = vector[..., :half_width]
    vec_im = vector[..., half_width:]
    return jnp.concatenate(
        [real_part * vec_re - imag_part * vec_im, real_part * vec_im + imag_part * vec_re], -1
    )


def on_device(right_side, self_block, hop_blocks):
    local_rhs, local_self, local_hops = (right_side, self_block, hop_blocks)
    residual = local_rhs.astype(jnp.float32)
    solution = jnp.zeros_like(residual)
    basis_list = []
    direction_list = []
    for iteration in range(ITERS):
        mapped = apply_operator(residual, local_self, local_hops)
        partial_terms = []
        for basis_vec in basis_list:
            partial_terms.extend(inner_pair(basis_vec, mapped))
        partial_terms.append(inner_pair(mapped, mapped)[0])
        partial_terms.extend(inner_pair(mapped, residual))
        stacked = jnp.stack(partial_terms)
        totals = lax.psum(stacked, ("ta", "xyz"))
        count_prev = len(basis_list)
        squared = totals[2 * count_prev]
        along_re = totals[2 * count_prev + 1]
        along_im = totals[2 * count_prev + 2]
        orthogonal = mapped
        direction = residual
        for index_prev in range(count_prev):
            proj_re = totals[2 * index_prev]
            proj_im = totals[2 * index_prev + 1]
            squared = squared - (proj_re * proj_re + proj_im * proj_im)
            orthogonal = orthogonal - scale_complex(proj_re, proj_im, basis_list[index_prev])
            direction = direction - scale_complex(proj_re, proj_im, direction_list[index_prev])
        length = jnp.sqrt(squared)
        new_basis = orthogonal / length
        new_direction = direction / length
        step_re = along_re / length
        step_im = along_im / length
        solution = solution + scale_complex(step_re, step_im, new_direction)
        residual = residual - scale_complex(step_re, step_im, new_basis)
        basis_list.append(new_basis)
        direction_list.append(new_direction)
    return (solution, residual)


def solution(mesh):
    placed = (
        P("ta", "xyz", None, None, None),
        P("ta", "xyz", None, None, None, None),
        P("ta", "xyz", None, None, None, None, None),
    )
    return jax.shard_map(
        on_device,
        mesh=mesh,
        in_specs=placed,
        out_specs=(P("ta", "xyz", None, None, None), P("ta", "xyz", None, None, None)),
        check_vma=False,
    )
```

profile of v0, /device:TPU:1, one launch (start us, length us, event | category | flops | bytes accessed | tf_op | source)
XLA Modules:
  0.0 456.3 jit_solution(6779449023983785874)
XLA Ops:
  0.7 14.1 %collective-permute-start = (bf16[1,1,2,2,128]{4,3,2,1,0:T(2,128)(2,1)}, bf16[1,1,2,2,128]{4,3,2,1,0:T(2,128)(2,1)S(1)}, u32[]{:S(2)}, u32[]{:S(2)}) collective-permute-start(bf16[1,1,2,2,128]{4,3,2,1,0:T(2,128)(2,1)} %param.3), channel_id=1, source_target_pairs={{1,0},{2,1},{3,2},{4,3},{5,4},{6,5},{7,6},{8,7},{9,8},{10,9},{11,1... | collective-permute-start | bytes 3080 | tf_op jit(solution)/shard_map/ppermute | solution.py:12
  14.8 7.5 %collective-permute-start.1 = (bf16[1,1,2,2,128]{4,3,2,1,0:T(2,128)(2,1)}, bf16[1,1,2,2,128]{4,3,2,1,0:T(2,128)(2,1)S(1)}, u32[]{:S(2)}, u32[]{:S(2)}) collective-permute-start(bf16[1,1,2,2,128]{4,3,2,1,0:T(2,128)(2,1)} %param.3), channel_id=1, source_target_pairs={{16,0},{32,16},{48,32},{64,48},{80,64},{96,80},{112,96},{128,112},... | collective-permute-start | bytes 3080 | tf_op jit(solution)/shard_map/ppermute | solution.py:12
  22.4 0.1 fusion.16
  22.6 0.1 fusion.18
  22.7 0.1 fusion.41
  22.8 0.1 maximum_bitcast_fusion.13
  22.9 1.6 collective-permute-start.2
  24.5 1.9 collective-permute-start.3
  26.6 0.1 fusion.32
  26.8 0.1 fusion.34
  27.0 0.1 slice_negate_fusion.5
  27.1 0.1 maximum_bitcast_fusion
  27.2 0.2 fusion.22
  27.4 0.2 fusion.20
  27.5 4.6 %collective-permute-done.3 = bf16[1,1,2,2,128]{4,3,2,1,0:T(2,128)(2,1)S(1)} collective-permute-done((bf16[1,1,2,2,128]{4,3,2,1,0:T(2,128)(2,1)S(1)}, bf16[1,1,2,2,128]{4,3,2,1,0:T(2,128)(2,1)S(1)}, u32[]{:S(2)}, u32[]{:S(2)}) %collective-permute-start.3) | collective-permute-done | bytes 1056 | tf_op jit(solution)/shard_map/ppermute | solution.py:12
  32.2 0.7 add_reduce_fusion.7
  33.0 2.0 pad_maximum_fusion.6
  35.0 120.3 %psum.21 = f32[3]{0:T(128)S(1)} all-reduce(f32[3]{0:T(128)S(1)} %pad_maximum_fusion.6), channel_id=1, replica_groups=mesh['ta'=64,'xyz'=16] {'ta','xyz'}, use_global_device_ids=true, to_apply=%region_3.4 | all-reduce | flops 3 | bytes 24 | tf_op jit(solution)/shard_map/psum | solution.py:126
  155.3 0.6 fusion.88
  158.1 0.7 collective-permute-start.4
  158.8 5.1 %collective-permute-start.5 = (bf16[1,1,2,2,128]{4,3,2,1,0:T(2,128)(2,1)S(1)}, bf16[1,1,2,2,128]{4,3,2,1,0:T(2,128)(2,1)S(1)}, u32[]{:S(2)}, u32[]{:S(2)}) collective-permute-start(bf16[1,1,2,2,128]{4,3,2,1,0:T(2,128)(2,1)S(1)} %get-tuple-element.25), channel_id=1, source_target_pairs={{16,0},{32,16},{48,32},{64,48},{80,64},{96,80},{112,96},{128,112},... | collective-permute-start | bytes 3080 | tf_op jit(solution)/shard_map/ppermute | solution.py:12
  163.9 0.1 fusion.8
  164.1 0.1 fusion.10
  164.2 0.1 fusion.39
  164.3 0.1 maximum_bitcast_fusion.10
  164.4 1.4 collective-permute-start.6
  165.8 1.9 collective-permute-start.7
  167.9 0.1 fusion.30
  168.0 0.1 fusion.28
  168.2 0.1 slice_negate_fusion.4
  168.3 0.1 maximum_bitcast_fusion.2
  168.4 0.2 fusion.14
  168.6 0.2 fusion.12
  168.8 4.6 %collective-permute-done.7 = bf16[1,1,2,2,128]{4,3,2,1,0:T(2,128)(2,1)S(1)} collective-permute-done((bf16[1,1,2,2,128]{4,3,2,1,0:T(2,128)(2,1)S(1)}, bf16[1,1,2,2,128]{4,3,2,1,0:T(2,128)(2,1)S(1)}, u32[]{:S(2)}, u32[]{:S(2)}) %collective-permute-start.7) | collective-permute-done | bytes 1056 | tf_op jit(solution)/shard_map/ppermute | solution.py:12
  173.5 0.8 subtract_reduce_fusion.3
  174.3 3.2 stack.118
  177.5 117.7 %psum.22 = f32[5]{0:T(128)S(1)} all-reduce(f32[5]{0:T(128)S(1)} %stack.118), channel_id=1, replica_groups=mesh['ta'=64,'xyz'=16] {'ta','xyz'}, use_global_device_ids=true, to_apply=%region_9.10 | all-reduce | flops 5 | bytes 40 | tf_op jit(solution)/shard_map/psum | solution.py:126
  295.2 0.7 fusion.87
  297.0 1.3 multiply_subtract_fusion.7
  301.8 0.7 collective-permute-start.8
  302.5 5.1 %collective-permute-start.9 = (bf16[1,1,2,2,128]{4,3,2,1,0:T(2,128)(2,1)S(1)}, bf16[1,1,2,2,128]{4,3,2,1,0:T(2,128)(2,1)S(1)}, u32[]{:S(2)}, u32[]{:S(2)}) collective-permute-start(bf16[1,1,2,2,128]{4,3,2,1,0:T(2,128)(2,1)S(1)} %get-tuple-element.22), channel_id=1, source_target_pairs={{16,0},{32,16},{48,32},{64,48},{80,64},{96,80},{112,96},{128,112},... | collective-permute-start | bytes 3080 | tf_op jit(solution)/shard_map/ppermute | solution.py:12
  307.7 0.1 fusion
  307.8 0.1 fusion.2
  308.0 0.1 fusion.37
  308.1 0.1 maximum_bitcast_fusion.7
  308.1 1.4 collective-permute-start.10
  309.5 1.9 collective-permute-start.11
  311.6 0.1 fusion.26
  311.7 0.1 fusion.24
  312.0 0.1 slice_negate_fusion.3
  312.0 0.1 maximum_bitcast_fusion.4
  312.1 0.2 fusion.6
  312.3 0.2 fusion.4
  312.5 4.6 %collective-permute-done.11 = bf16[1,1,2,2,128]{4,3,2,1,0:T(2,128)(2,1)S(1)} collective-permute-done((bf16[1,1,2,2,128]{4,3,2,1,0:T(2,128)(2,1)S(1)}, bf16[1,1,2,2,128]{4,3,2,1,0:T(2,128)(2,1)S(1)}, u32[]{:S(2)}, u32[]{:S(2)}) %collective-permute-start.11) | collective-permute-done | bytes 1056 | tf_op jit(solution)/shard_map/ppermute | solution.py:12
  317.2 0.8 subtract_reduce_fusion
  318.0 4.6 stack.131
  322.5 117.7 %psum.23 = f32[7]{0:T(128)S(1)} all-reduce(f32[7]{0:T(128)S(1)} %stack.131), channel_id=1, replica_groups=mesh['ta'=64,'xyz'=16] {'ta','xyz'}, use_global_device_ids=true, to_apply=%region_17.18 | all-reduce | flops 7 | bytes 56 | tf_op jit(solution)/shard_map/psum | solution.py:126
  440.3 0.7 fusion.86
  443.6 1.4 multiply_subtract_fusion.1
  447.4 1.3 multiply_subtract_fusion.2
  450.7 2.5 multiply_subtract_fusion.5
  453.3 1.4 multiply_subtract_fusion.4
  454.9 0.7 maximum_subtract_fusion.6
  455.6 0.7 fusion.49
  (66 shorter events, 1.9 us)
Async XLA Ops:
  0.6 21.8 %copy-start = (bf16[1,1,2,2,4,64,128]{6,5,4,3,2,1,0:T(8,128)(2,1)S(1)}, bf16[1,1,2,2,4,64,128]{6,5,4,3,2,1,0:T(8,128)(2,1)}, u32[]{:S(2)}) copy-start(bf16[1,1,2,2,4,64,128]{6,5,4,3,2,1,0:T(8,128)(2,1)} %param.5) | copy-start | bytes 786436
  0.6 21.7 %copy-start.1 = (bf16[1,1,2,2,128]{4,3,2,1,0:T(2,128)(2,1)S(1)}, bf16[1,1,2,2,128]{4,3,2,1,0:T(2,128)(2,1)}, u32[]{:S(2)}) copy-start(bf16[1,1,2,2,128]{4,3,2,1,0:T(2,128)(2,1)} %param.3) | copy-start | bytes 3076
  0.7 26.3 %collective-permute-start = (bf16[1,1,2,2,128]{4,3,2,1,0:T(2,128)(2,1)}, bf16[1,1,2,2,128]{4,3,2,1,0:T(2,128)(2,1)S(1)}, u32[]{:S(2)}, u32[]{:S(2)}) collective-permute-start(bf16[1,1,2,2,128]{4,3,2,1,0:T(2,128)(2,1)} %param.3), channel_id=1, source_target_pairs={{1,0},{2,1},{3,2},{4,3},{5,4},{6,5},{7,6},{8,7},{9,8},{10,9},{11,1... | collective-permute-start | bytes 3080 | tf_op jit(solution)/shard_map/ppermute | solution.py:12
  14.8 12.2 %collective-permute-start.1 = (bf16[1,1,2,2,128]{4,3,2,1,0:T(2,128)(2,1)}, bf16[1,1,2,2,128]{4,3,2,1,0:T(2,128)(2,1)S(1)}, u32[]{:S(2)}, u32[]{:S(2)}) collective-permute-start(bf16[1,1,2,2,128]{4,3,2,1,0:T(2,128)(2,1)} %param.3), channel_id=1, source_target_pairs={{16,0},{32,16},{48,32},{64,48},{80,64},{96,80},{112,96},{128,112},... | collective-permute-start | bytes 3080 | tf_op jit(solution)/shard_map/ppermute | solution.py:12
  22.7 3.9 copy-start.2
  22.9 4.6 %collective-permute-start.2 = (bf16[1,1,2,2,128]{4,3,2,1,0:T(2,128)(2,1)S(1)}, bf16[1,1,2,2,128]{4,3,2,1,0:T(2,128)(2,1)S(1)}, u32[]{:S(2)}, u32[]{:S(2)}) collective-permute-start(bf16[1,1,2,2,128]{4,3,2,1,0:T(2,128)(2,1)S(1)} %get-tuple-element.44), channel_id=1, source_target_pairs={{15,0},{0,1},{1,2},{2,3},{3,4},{4,5},{5,6},{6,7},{7,8},{8,9},{9,10... | collective-permute-start | bytes 3080 | tf_op jit(solution)/shard_map/ppermute | solution.py:12
  24.5 7.6 %collective-permute-start.3 = (bf16[1,1,2,2,128]{4,3,2,1,0:T(2,128)(2,1)S(1)}, bf16[1,1,2,2,128]{4,3,2,1,0:T(2,128)(2,1)S(1)}, u32[]{:S(2)}, u32[]{:S(2)}) collective-permute-start(bf16[1,1,2,2,128]{4,3,2,1,0:T(2,128)(2,1)S(1)} %get-tuple-element.43), channel_id=1, source_target_pairs={{1008,0},{0,16},{16,32},{32,48},{48,64},{64,80},{80,96},{96,112},{... | collective-permute-start | bytes 3080 | tf_op jit(solution)/shard_map/ppermute | solution.py:12
  158.1 10.1 %collective-permute-start.4 = (bf16[1,1,2,2,128]{4,3,2,1,0:T(2,128)(2,1)S(1)}, bf16[1,1,2,2,128]{4,3,2,1,0:T(2,128)(2,1)S(1)}, u32[]{:S(2)}, u32[]{:S(2)}) collective-permute-start(bf16[1,1,2,2,128]{4,3,2,1,0:T(2,128)(2,1)S(1)} %get-tuple-element.25), channel_id=1, source_target_pairs={{1,0},{2,1},{3,2},{4,3},{5,4},{6,5},{7,6},{8,7},{9,8},{10,9},{11,1... | collective-permute-start | bytes 3080 | tf_op jit(solution)/shard_map/ppermute | solution.py:12
  158.8 9.5 %collective-permute-start.5 = (bf16[1,1,2,2,128]{4,3,2,1,0:T(2,128)(2,1)S(1)}, bf16[1,1,2,2,128]{4,3,2,1,0:T(2,128)(2,1)S(1)}, u32[]{:S(2)}, u32[]{:S(2)}) collective-permute-start(bf16[1,1,2,2,128]{4,3,2,1,0:T(2,128)(2,1)S(1)} %get-tuple-element.25), channel_id=1, source_target_pairs={{16,0},{32,16},{48,32},{64,48},{80,64},{96,80},{112,96},{128,112},... | collective-permute-start | bytes 3080 | tf_op jit(solution)/shard_map/ppermute | solution.py:12
  164.4 4.3 collective-permute-start.6
  165.8 7.6 %collective-permute-start.7 = (bf16[1,1,2,2,128]{4,3,2,1,0:T(2,128)(2,1)S(1)}, bf16[1,1,2,2,128]{4,3,2,1,0:T(2,128)(2,1)S(1)}, u32[]{:S(2)}, u32[]{:S(2)}) collective-permute-start(bf16[1,1,2,2,128]{4,3,2,1,0:T(2,128)(2,1)S(1)} %get-tuple-element.39), channel_id=1, source_target_pairs={{1008,0},{0,16},{16,32},{32,48},{48,64},{64,80},{80,96},{96,112},{... | collective-permute-start | bytes 3080 | tf_op jit(solution)/shard_map/ppermute | solution.py:12
  301.8 10.1 %collective-permute-start.8 = (bf16[1,1,2,2,128]{4,3,2,1,0:T(2,128)(2,1)S(1)}, bf16[1,1,2,2,128]{4,3,2,1,0:T(2,128)(2,1)S(1)}, u32[]{:S(2)}, u32[]{:S(2)}) collective-permute-start(bf16[1,1,2,2,128]{4,3,2,1,0:T(2,128)(2,1)S(1)} %get-tuple-element.22), channel_id=1, source_target_pairs={{1,0},{2,1},{3,2},{4,3},{5,4},{6,5},{7,6},{8,7},{9,8},{10,9},{11,1... | collective-permute-start | bytes 3080 | tf_op jit(solution)/shard_map/ppermute | solution.py:12
  302.5 9.5 %collective-permute-start.9 = (bf16[1,1,2,2,128]{4,3,2,1,0:T(2,128)(2,1)S(1)}, bf16[1,1,2,2,128]{4,3,2,1,0:T(2,128)(2,1)S(1)}, u32[]{:S(2)}, u32[]{:S(2)}) collective-permute-start(bf16[1,1,2,2,128]{4,3,2,1,0:T(2,128)(2,1)S(1)} %get-tuple-element.22), channel_id=1, source_target_pairs={{16,0},{32,16},{48,32},{64,48},{80,64},{96,80},{112,96},{128,112},... | collective-permute-start | bytes 3080 | tf_op jit(solution)/shard_map/ppermute | solution.py:12
  308.1 4.4 collective-permute-start.10
  309.5 7.6 %collective-permute-start.11 = (bf16[1,1,2,2,128]{4,3,2,1,0:T(2,128)(2,1)S(1)}, bf16[1,1,2,2,128]{4,3,2,1,0:T(2,128)(2,1)S(1)}, u32[]{:S(2)}, u32[]{:S(2)}) collective-permute-start(bf16[1,1,2,2,128]{4,3,2,1,0:T(2,128)(2,1)S(1)} %get-tuple-element.35), channel_id=1, source_target_pairs={{1008,0},{0,16},{16,32},{32,48},{48,64},{64,80},{80,96},{96,112},{... | collective-permute-start | bytes 3080 | tf_op jit(solution)/shard_map/ppermute | solution.py:12
where the time goes:
time: 457 us; the launch traced here: 456 us
  blocking collectives  356 us (78%)
  starting transfers between devices  43.3 us (9%)
  other arithmetic  16 us (4%)
  between operations  14.5 us (3%)
  waiting for transfers between devices  13.9 us (3%)
  local copies, waits for them, and re-layouts  10.1 us (2%)
    psum x3, blocking collectives, on_device(): totals = lax.psum(stacked, ('ta', 'xyz'))  356 us
    ppermute x12, starting transfers between devices, shifted(): return lax.ppermute(block, axis, route)  43.3 us
    ppermute x12, waiting for transfers between devices, shifted(): return lax.ppermute(block, axis, route)  13.9 us
  transfers between devices with their start and end apart: 12, of which 3 were waited for; matrix products, arithmetic and copies ran while one was open for 1% of the time, Pallas kernels for 0%

commit v1 on v0

v1 whole, which is shorter than its diff:
```python
import jax
import jax.numpy as jnp
from jax import lax
from jax.experimental import pallas as pl
from jax.experimental.pallas import tpu as pltpu
from jax.sharding import Mesh
from jax.sharding import PartitionSpec as P

ITERS = 3
T_AXES = ("tz", "tx")
Z_AXES = ("sy", "sc")
DIAGONAL = (1, 2, 3)
PAIRS = ((0, 1), (0, 2), (0, 3), (1, 2), (1, 3), (2, 3))


def shifted(block, axes, distance):
    count = lax.axis_size(axes)
    route = [((i - distance) % count, i) for i in range(count)]
    return lax.ppermute(block, axes, route)


def chirality_signs(full_width):
    half_width = full_width // 2
    column = jnp.arange(full_width) % half_width
    return jnp.where(column < half_width // 2, 1.0, -1.0).astype(jnp.float32)


def forward_sum(blocks, vectors):
    half = blocks.shape[-2]
    plain = jnp.concatenate([vectors[..., :half], -vectors[..., half:]], -1)
    turned = jnp.concatenate([vectors[..., half:], vectors[..., :half]], -1)
    wide = blocks.astype(jnp.float32)
    real_out = jnp.sum(wide * plain[..., None, :], (-3, -1))
    imag_out = jnp.sum(wide * turned[..., None, :], (-3, -1))
    return jnp.concatenate([real_out, imag_out], -1)


def adjoint(blocks, vector):
    half = blocks.shape[-2]
    wide = blocks.astype(jnp.float32)
    from_real = jnp.sum(wide * vector[..., None, :half, None], -2)
    from_imag = jnp.sum(wide * vector[..., None, half:, None], -2)
    return jnp.concatenate(
        [
            from_real[..., :half] + from_imag[..., half:],
            from_imag[..., :half] - from_real[..., half:],
        ],
        -1,
    )


def apply_operator(field, self_block, hop_blocks):
    signs = chirality_signs(field.shape[-1])
    ahead_z = shifted(field, Z_AXES, -1)
    ahead_t = shifted(field, T_AXES, -1)
    carried = adjoint(hop_blocks, field * signs)
    behind_z = shifted(carried[:, :, 2], Z_AXES, 1)
    behind_t = shifted(carried[:, :, 3], T_AXES, 1)
    near = forward_sum(self_block[:, :, None], field[:, :, None])
    near_hops = jnp.stack([jnp.roll(field, -1, 1), jnp.roll(field, -1, 0)], 2)
    near = near + forward_sum(hop_blocks[:, :, :2], near_hops)
    near_back = jnp.roll(carried[:, :, 0], 1, 1) + jnp.roll(carried[:, :, 1], 1, 0)
    far = forward_sum(hop_blocks[:, :, 2:], jnp.stack([ahead_z, ahead_t], 2))
    return near + far + signs * (near_back + behind_z + behind_t)


def gram_body(v0, v1, v2, v3, out):
    vectors = [v0[...], v1[...], v2[...], v3[...]]
    half = vectors[0].shape[-1] // 2
    lane = lax.broadcasted_iota(jnp.int32, vectors[0].shape, 1)
    sign = jnp.where(lane < half, 1.0, -1.0)
    turned = [pltpu.roll(v, half, 1) * sign for v in vectors]
    rows = [jnp.sum(vectors[i] * vectors[i], 0, keepdims=True) for i in DIAGONAL]
    for i, j in PAIRS:
        rows.append(jnp.sum(vectors[i] * vectors[j], 0, keepdims=True))
        rows.append(jnp.sum(vectors[i] * turned[j], 0, keepdims=True))
    rows.append(jnp.zeros_like(rows[0]))
    stacked = jnp.concatenate(rows, 0)
    totals = jnp.sum(stacked, 1, keepdims=True)
    row = lax.broadcasted_iota(jnp.int32, stacked.shape, 0)
    column = lax.broadcasted_iota(jnp.int32, stacked.shape, 1)
    out[...] = jnp.sum(jnp.where(row == column, totals, 0.0), 0, keepdims=True)


def cmul(a, b):
    return (a[0] * b[0] - a[1] * b[1], a[0] * b[1] + a[1] * b[0])


def cmulc(a, b):
    return (a[0] * b[0] + a[1] * b[1], a[0] * b[1] - a[1] * b[0])


def cadd(a, b):
    return (a[0] + b[0], a[1] + b[1])


def csub(a, b):
    return (a[0] - b[0], a[1] - b[1])


def gram_image(gram, vec):
    image = {}
    for i in range(4):
        total = None
        for j, value in vec.items():
            if (i, j) not in gram:
                continue
            term = cmul(gram[i, j], value)
            total = term if total is None else cadd(total, term)
        image[i] = total
    return image


def inner(left, image):
    total = None
    for i, value in left.items():
        term = cmulc(value, image[i])
        total = term if total is None else cadd(total, term)
    return total


def combine(base, scale, vec):
    out = dict(base)
    for i, value in vec.items():
        term = cmul(scale, value)
        out[i] = csub(out[i], term) if i in out else (-term[0], -term[1])
    return out


def cycle_coefficients(gram, one):
    zero = jnp.zeros_like(one)
    residual = {0: (one, zero)}
    answer = {}
    basis_list = []
    direction_list = []
    for _ in range(ITERS):
        mapped = {i + 1: value for i, value in residual.items()}
        image = gram_image(gram, mapped)
        norm = inner(mapped, image)[0]
        along = inner(residual, image)
        along = (along[0], -along[1])
        orthogonal = mapped
        direction = residual
        squared = norm
        for basis, previous in zip(basis_list, direction_list):
            proj = inner(basis, image)
            squared = squared - (proj[0] * proj[0] + proj[1] * proj[1])
            orthogonal = combine(orthogonal, proj, basis)
            direction = combine(direction, proj, previous)
        scale = 1.0 / jnp.sqrt(squared)
        new_basis = {i: (v[0] * scale, v[1] * scale) for i, v in orthogonal.items()}
        new_direction = {i: (v[0] * scale, v[1] * scale) for i, v in direction.items()}
        step = (along[0] * scale, along[1] * scale)
        minus = (-step[0], -step[1])
        answer = combine(answer, minus, new_direction)
        residual = combine(residual, step, new_basis)
        basis_list.append(new_basis)
        direction_list.append(new_direction)
    return answer, residual


def gram_of(totals):
    gram = {}
    for k, i in enumerate(DIAGONAL):
        gram[i, i] = (totals[k], jnp.zeros_like(totals[k]))
    for k, (i, j) in enumerate(PAIRS):
        real, imag = totals[3 + 2 * k], totals[4 + 2 * k]
        gram[i, j] = (real, imag)
        gram[j, i] = (real, -imag)
    return gram


def finish_body(packed, v0, v1, v2, v3, answer_out, residual_out):
    vectors = [v0[...], v1[...], v2[...], v3[...]]
    half = vectors[0].shape[-1] // 2
    spread = jnp.broadcast_to(packed[...], (16, 2 * half))
    row = lax.broadcasted_iota(jnp.int32, spread.shape, 0)
    column = lax.broadcasted_iota(jnp.int32, spread.shape, 1)
    totals = jnp.sum(jnp.where(row == column, spread, 0.0), 1, keepdims=True)
    entries = [totals[k : k + 1, :] for k in range(15)]
    answer, residual = cycle_coefficients(gram_of(entries), jnp.ones_like(entries[0]))
    lane = lax.broadcasted_iota(jnp.int32, vectors[0].shape, 1)
    sign = jnp.where(lane < half, -1.0, 1.0)
    turned = [pltpu.roll(v, half, 1) * sign for v in vectors]
    for coefficients, out in ((answer, answer_out), (residual, residual_out)):
        total = None
        for i, (real, imag) in coefficients.items():
            term = real * vectors[i] + imag * turned[i]
            total = term if total is None else total + term
        out[...] = total


def whole_sum(packed):
    for axes in (("sy", "sc"), "tx", "tz"):
        packed = lax.psum(packed, axes)
    return packed


def on_device(right_side, self_block, hop_blocks):
    shape = right_side.shape
    sites = shape[2:]
    rows = (sites[0] * sites[1], sites[2])
    local_self = self_block[0, 0]
    local_hops = hop_blocks[0, 0]
    vectors = [right_side[0, 0].astype(jnp.float32)]
    for _ in range(ITERS):
        vectors.append(apply_operator(vectors[-1], local_self, local_hops))
    flat = [v.reshape(rows) for v in vectors]
    space = pl.BlockSpec(memory_space=pltpu.VMEM)
    packed = pl.pallas_call(
        gram_body,
        out_shape=jax.ShapeDtypeStruct((1, rows[1]), jnp.float32),
        in_specs=[space] * 4,
        out_specs=space,
    )(*flat)
    packed = whole_sum(packed)
    result = jax.ShapeDtypeStruct(rows, jnp.float32)
    answer, residual = pl.pallas_call(
        finish_body,
        out_shape=(result, result),
        in_specs=[space] * 5,
        out_specs=(space, space),
    )(packed, *flat)
    return answer.reshape(shape), residual.reshape(shape)


def solution(mesh):
    chips = mesh.devices.reshape(16, 4, 8, 2)
    fine = Mesh(chips, (*T_AXES, *Z_AXES))
    lead = (T_AXES, Z_AXES)
    placed = (P(*lead), P(*lead), P(*lead))
    return jax.shard_map(
        on_device,
        mesh=fine,
        in_specs=placed,
        out_specs=(P(*lead), P(*lead)),
        check_vma=False,
    )
```

time: 457 us -> 128 us (0.28)
  the two profiles are of different devices: /device:TPU:1 before, /device:TPU:2 now
where the time goes in v1:
time: 128 us
  blocking collectives  65.8 us (51%)
  starting transfers between devices  34.7 us (27%)
  waiting for transfers between devices  16.7 us (13%)
  other arithmetic  6.36 us (5%)
  Pallas kernels  2.85 us (2%)
    psum x3, blocking collectives, whole_sum(): packed = lax.psum(packed, axes)  65.8 us
    ppermute x12, starting transfers between devices, shifted(): return lax.ppermute(block, axes, route)  34.7 us
    ppermute x12, waiting for transfers between devices, shifted(): return lax.ppermute(block, axes, route)  16.7 us
  transfers between devices with their start and end apart: 12, of which 5 were waited for; matrix products, arithmetic and copies ran while one was open for 4% of the time, Pallas kernels for 0%

profile of v1, /device:TPU:2, one launch (start us, length us, event | category | flops | bytes accessed | tf_op | source)
XLA Modules:
  0.0 128.0 jit_solution(17970356591903465050)
XLA Ops:
  0.6 0.7 convert_bitcast_fusion.1
  1.3 2.9 %collective-permute-start = (f32[2,2,128]{2,1,0:T(2,128)S(1)}, f32[2,2,128]{2,1,0:T(2,128)S(1)}, u32[]{:S(2)}, u32[]{:S(2)}) collective-permute-start(f32[2,2,128]{2,1,0:T(2,128)S(1)} %get-tuple-element.129), channel_id=1, source_target_pairs={{1,0},{2,1},{3,2},{4,3},{5,4},{6,5},{7,6},{8,7},{9,8},{10,9},{11,1... | collective-permute-start | bytes 6152 | tf_op jit(solution)/shard_map/ppermute | solution.py:19
  4.2 12.2 %collective-permute-start.1 = (f32[2,2,128]{2,1,0:T(2,128)S(1)}, f32[2,2,128]{2,1,0:T(2,128)S(1)}, u32[]{:S(2)}, u32[]{:S(2)}) collective-permute-start(f32[2,2,128]{2,1,0:T(2,128)S(1)} %get-tuple-element.129), channel_id=1, source_target_pairs={{16,0},{32,16},{48,32},{64,48},{80,64},{96,80},{112,96},{128,112},... | collective-permute-start | bytes 6152 | tf_op jit(solution)/shard_map/ppermute | solution.py:19
  16.4 0.1 fusion.86
  16.5 1.2 fusion.1
  17.7 0.1 slice_add_fusion
  17.8 0.1 fusion.29
  17.9 0.2 collective-permute-start.2
  18.1 1.9 %collective-permute-start.3 = (f32[2,2,128]{2,1,0:T(2,128)S(1)}, f32[2,2,128]{2,1,0:T(2,128)S(1)}, u32[]{:S(2)}, u32[]{:S(2)}) collective-permute-start(f32[2,2,128]{2,1,0:T(2,128)S(1)} %bitcast.121), channel_id=1, source_target_pairs={{1008,0},{0,16},{16,32},{32,48},{48,64},{64,80},{80,96},{96,112},{... | collective-permute-start | bytes 6152 | tf_op jit(solution)/shard_map/ppermute | solution.py:19
  20.1 0.1 fusion.83
  20.2 0.1 fusion.61
  20.3 0.1 pad_maximum_fusion.6
  20.3 0.1 maximum_bitcast_fusion.1
  20.4 0.2 fusion.18
  20.6 0.1 fusion.55
  20.7 0.1 pad_maximum_fusion.4
  20.8 0.1 pad_maximum_fusion.9
  20.9 0.2 fusion.12
  21.1 1.0 collective-permute-done.2
  22.1 8.0 %collective-permute-done.3 = f32[2,2,128]{2,1,0:T(2,128)S(1)} collective-permute-done((f32[2,2,128]{2,1,0:T(2,128)S(1)}, f32[2,2,128]{2,1,0:T(2,128)S(1)}, u32[]{:S(2)}, u32[]{:S(2)}) %collective-permute-start.3) | collective-permute-done | bytes 2080 | tf_op jit(solution)/shard_map/ppermute | solution.py:19
  30.2 0.1 broadcast_multiply_fusion.1
  30.3 2.1 %collective-permute-start.4 = (f32[2,2,128]{2,1,0:T(2,128)S(1)}, f32[2,2,128]{2,1,0:T(2,128)S(1)}, u32[]{:S(2)}, u32[]{:S(2)}) collective-permute-start(f32[2,2,128]{2,1,0:T(2,128)S(1)} %get-tuple-element.33), channel_id=1, source_target_pairs={{1,0},{2,1},{3,2},{4,3},{5,4},{6,5},{7,6},{8,7},{9,8},{10,9},{11,1... | collective-permute-start | bytes 6152 | tf_op jit(solution)/shard_map/ppermute | solution.py:19
  32.4 7.0 %collective-permute-start.5 = (f32[2,2,128]{2,1,0:T(2,128)S(1)}, f32[2,2,128]{2,1,0:T(2,128)S(1)}, u32[]{:S(2)}, u32[]{:S(2)}) collective-permute-start(f32[2,2,128]{2,1,0:T(2,128)S(1)} %get-tuple-element.33), channel_id=1, source_target_pairs={{16,0},{32,16},{48,32},{64,48},{80,64},{96,80},{112,96},{128,112},... | collective-permute-start | bytes 6152 | tf_op jit(solution)/shard_map/ppermute | solution.py:19
  39.3 0.1 fusion.78
  39.5 0.2 fusion.3
  39.7 0.1 fusion.71
  39.8 0.1 fusion.72
  39.9 0.1 fusion.47
  39.9 1.9 %collective-permute-start.7 = (f32[2,2,128]{2,1,0:T(2,128)S(1)}, f32[2,2,128]{2,1,0:T(2,128)S(1)}, u32[]{:S(2)}, u32[]{:S(2)}) collective-permute-start(f32[2,2,128]{2,1,0:T(2,128)S(1)} %get-tuple-element.40), channel_id=1, source_target_pairs={{1008,0},{0,16},{16,32},{32,48},{48,64},{64,80},{80,96},{96,112},{... | collective-permute-start | bytes 6152 | tf_op jit(solution)/shard_map/ppermute | solution.py:19
  41.9 0.1 maximum_bitcast_fusion.5
  41.9 0.2 fusion.20
  42.1 0.1 fusion.63
  42.2 0.1 pad_maximum_fusion.10
  42.3 0.1 fusion.58
  42.4 0.1 pad_maximum_fusion.2
  42.5 0.1 pad_maximum_fusion.13
  42.6 0.2 fusion.14
  42.8 3.8 %collective-permute-done.6 = f32[2,2,128]{2,1,0:T(2,128)S(1)} collective-permute-done((f32[2,2,128]{2,1,0:T(2,128)S(1)}, f32[2,2,128]{2,1,0:T(2,128)S(1)}, u32[]{:S(2)}, u32[]{:S(2)}) %collective-permute-start.6) | collective-permute-done | bytes 2080 | tf_op jit(solution)/shard_map/ppermute | solution.py:19
  46.6 0.1 broadcast_multiply_fusion
  46.7 0.1 fusion.74
  46.8 0.2 fusion.5
  47.0 0.1 fusion.69
  47.1 0.1 fusion.70
  47.2 0.1 fusion.60
  47.2 0.1 fusion.49
  47.4 4.4 %collective-permute-start.9 = (f32[2,2,128]{2,1,0:T(2,128)S(1)}, f32[2,2,128]{2,1,0:T(2,128)S(1)}, u32[]{:S(2)}, u32[]{:S(2)}) collective-permute-start(f32[2,2,128]{2,1,0:T(2,128)S(1)} %get-tuple-element.31), channel_id=1, source_target_pairs={{16,0},{32,16},{48,32},{64,48},{80,64},{96,80},{112,96},{128,112},... | collective-permute-start | bytes 6152 | tf_op jit(solution)/shard_map/ppermute | solution.py:19
  51.8 0.2 collective-permute-start.10
  52.0 1.9 %collective-permute-start.11 = (f32[2,2,128]{2,1,0:T(2,128)S(1)}, f32[2,2,128]{2,1,0:T(2,128)S(1)}, u32[]{:S(2)}, u32[]{:S(2)}) collective-permute-start(f32[2,2,128]{2,1,0:T(2,128)S(1)} %get-tuple-element.37), channel_id=1, source_target_pairs={{1008,0},{0,16},{16,32},{32,48},{48,64},{64,80},{80,96},{96,112},{... | collective-permute-start | bytes 6152 | tf_op jit(solution)/shard_map/ppermute | solution.py:19
  54.0 0.1 fusion.77
  54.1 0.1 fusion.65
  54.1 0.1 maximum_bitcast_fusion.9
  54.2 0.2 fusion.22
  54.4 0.1 pad_maximum_fusion.14
  54.5 0.1 pad_maximum_fusion
  54.6 0.1 pad_maximum_fusion.17
  54.7 0.2 fusion.16
  54.9 1.1 collective-permute-done.10
  56.0 2.7 %collective-permute-done.11 = f32[2,2,128]{2,1,0:T(2,128)S(1)} collective-permute-done((f32[2,2,128]{2,1,0:T(2,128)S(1)}, f32[2,2,128]{2,1,0:T(2,128)S(1)}, u32[]{:S(2)}, u32[]{:S(2)}) %collective-permute-start.11) | collective-permute-done | bytes 2080 | tf_op jit(solution)/shard_map/ppermute | solution.py:19
  58.7 0.7 fusion.43
  59.3 1.4 %shard_map.50 = f32[1,128]{1,0:T(1,128)} custom-call(f32[4,128]{1,0:T(4,128)} %bitcast.113, f32[4,128]{1,0:T(4,128)} %bitcast.108, f32[4,128]{1,0:T(4,128)} %bitcast.111, f32[4,128]{1,0:T(4,128)} %bitcast.115), custom_call_target="tpu_custom_call" | custom-call | tf_op jit(solution)/shard_map/pallas_call | solution.py:210
  60.7 25.5 %psum.21 = f32[1,128]{1,0:T(1,128)S(1)} all-reduce(f32[1,128]{1,0:T(1,128)} %shard_map.50), channel_id=1, replica_groups=mesh['tz'=16,'tx'=4,'sy'=8,'sc'=2] {'sy','sc'}, use_global_device_ids=true, to_apply=%region_24.25 | all-reduce | flops 128 | bytes 1024 | tf_op jit(solution)/shard_map/psum | solution.py:195
  86.2 12.8 %psum.22 = f32[1,128]{1,0:T(1,128)S(1)} all-reduce(f32[1,128]{1,0:T(1,128)S(1)} %psum.21), channel_id=1, replica_groups=mesh['tz'=16,'tx'=4,'sy'=8,'sc'=2] {'tx'}, use_global_device_ids=true, to_apply=%region_25.26 | all-reduce | flops 128 | bytes 1024 | tf_op jit(solution)/shard_map/psum | solution.py:195
  99.0 27.5 %psum.23.packed = f32[1,128]{1,0:T(1,128)} all-reduce(f32[1,128]{1,0:T(1,128)S(1)} %psum.22), channel_id=1, replica_groups=mesh['tz'=16,'tx'=4,'sy'=8,'sc'=2] {'tz'}, use_global_device_ids=true, to_apply=%region_26.27 | all-reduce | flops 128 | bytes 1024 | tf_op jit(solution)/shard_map/psum | solution.py:195
  126.5 1.5 %shard_map.51 = (f32[4,128]{1,0:T(4,128)}, f32[4,128]{1,0:T(4,128)}) custom-call(f32[1,128]{1,0:T(1,128)} %psum.23.packed, f32[4,128]{1,0:T(4,128)} %bitcast.114, f32[4,128]{1,0:T(4,128)} %bitcast.109, f32[4,128]{1,0:T(4,128)} %bitcast.112, f32[4,128]{1,0:T(4,128)} %bitcast.116), custom_call_target="tpu_custom_call" | custom-call | tf_op jit(solution)/shard_map/pallas_call | solution.py:218
  (54 shorter events, 0.3 us)
Async XLA Ops:
  1.3 18.8 %copy-start.4 = (f32[1,1,2,2,128]{4,3,2,1,0:T(2,128)}, f32[1,1,2,2,128]{4,3,2,1,0:T(2,128)S(1)}, u32[]{:S(2)}) copy-start(f32[1,1,2,2,128]{4,3,2,1,0:T(2,128)S(1)} %get-tuple-element.130) | copy-start | bytes 6148
  1.3 15.1 %copy-start.5 = (bf16[1,1,2,2,128]{4,3,2,1,0:T(2,128)(2,1)S(1)}, bf16[1,1,2,2,128]{4,3,2,1,0:T(2,128)(2,1)}, u32[]{:S(2)}) copy-start(bf16[1,1,2,2,128]{4,3,2,1,0:T(2,128)(2,1)} %param.3) | copy-start | bytes 3076
  1.3 19.3 %collective-permute-start = (f32[2,2,128]{2,1,0:T(2,128)S(1)}, f32[2,2,128]{2,1,0:T(2,128)S(1)}, u32[]{:S(2)}, u32[]{:S(2)}) collective-permute-start(f32[2,2,128]{2,1,0:T(2,128)S(1)} %get-tuple-element.129), channel_id=1, source_target_pairs={{1,0},{2,1},{3,2},{4,3},{5,4},{6,5},{7,6},{8,7},{9,8},{10,9},{11,1... | collective-permute-start | bytes 6152 | tf_op jit(solution)/shard_map/ppermute | solution.py:19
  4.2 16.4 %collective-permute-start.1 = (f32[2,2,128]{2,1,0:T(2,128)S(1)}, f32[2,2,128]{2,1,0:T(2,128)S(1)}, u32[]{:S(2)}, u32[]{:S(2)}) collective-permute-start(f32[2,2,128]{2,1,0:T(2,128)S(1)} %get-tuple-element.129), channel_id=1, source_target_pairs={{16,0},{32,16},{48,32},{64,48},{80,64},{96,80},{112,96},{128,112},... | collective-permute-start | bytes 6152 | tf_op jit(solution)/shard_map/ppermute | solution.py:19
  16.5 4.3 %copy-start = (bf16[1,1,2,2,4,64,128]{6,5,4,3,2,1,0:T(8,128)(2,1)S(1)}, bf16[1,1,2,2,4,64,128]{6,5,4,3,2,1,0:T(8,128)(2,1)}, u32[]{:S(2)}) copy-start(bf16[1,1,2,2,4,64,128]{6,5,4,3,2,1,0:T(8,128)(2,1)} %param.5) | copy-start | bytes 786436
  17.9 2.5 %copy-start.1 = (bf16[1,1,2,2,64,128]{5,4,3,2,1,0:T(8,128)(2,1)S(1)}, bf16[1,1,2,2,64,128]{5,4,3,2,1,0:T(8,128)(2,1)}, u32[]{:S(2)}) copy-start(bf16[1,1,2,2,64,128]{5,4,3,2,1,0:T(8,128)(2,1)} %param.4) | copy-start | bytes 196612
  17.9 4.2 %collective-permute-start.2 = (f32[2,2,128]{2,1,0:T(2,128)S(1)}, f32[2,2,128]{2,1,0:T(2,128)S(1)}, u32[]{:S(2)}, u32[]{:S(2)}) collective-permute-start(f32[2,2,128]{2,1,0:T(2,128)S(1)} %bitcast.124), channel_id=1, source_target_pairs={{15,0},{0,1},{1,2},{2,3},{3,4},{4,5},{5,6},{6,7},{7,8},{8,9},{9,10... | collective-permute-start | bytes 6152 | tf_op jit(solution)/shard_map/ppermute | solution.py:19
  18.1 12.0 %collective-permute-start.3 = (f32[2,2,128]{2,1,0:T(2,128)S(1)}, f32[2,2,128]{2,1,0:T(2,128)S(1)}, u32[]{:S(2)}, u32[]{:S(2)}) collective-permute-start(f32[2,2,128]{2,1,0:T(2,128)S(1)} %bitcast.121), channel_id=1, source_target_pairs={{1008,0},{0,16},{16,32},{32,48},{48,64},{64,80},{80,96},{96,112},{... | collective-permute-start | bytes 6152 | tf_op jit(solution)/shard_map/ppermute | solution.py:19
  30.3 9.1 %copy-start.2 = (f32[2,2,128]{2,1,0:T(2,128)}, f32[2,2,128]{2,1,0:T(2,128)S(1)}, u32[]{:S(2)}) copy-start(f32[2,2,128]{2,1,0:T(2,128)S(1)} %get-tuple-element.33) | copy-start | bytes 6148
  30.3 12.1 %collective-permute-start.4 = (f32[2,2,128]{2,1,0:T(2,128)S(1)}, f32[2,2,128]{2,1,0:T(2,128)S(1)}, u32[]{:S(2)}, u32[]{:S(2)}) collective-permute-start(f32[2,2,128]{2,1,0:T(2,128)S(1)} %get-tuple-element.33), channel_id=1, source_target_pairs={{1,0},{2,1},{3,2},{4,3},{5,4},{6,5},{7,6},{8,7},{9,8},{10,9},{11,1... | collective-permute-start | bytes 6152 | tf_op jit(solution)/shard_map/ppermute | solution.py:19
  32.4 10.1 %collective-permute-start.5 = (f32[2,2,128]{2,1,0:T(2,128)S(1)}, f32[2,2,128]{2,1,0:T(2,128)S(1)}, u32[]{:S(2)}, u32[]{:S(2)}) collective-permute-start(f32[2,2,128]{2,1,0:T(2,128)S(1)} %get-tuple-element.33), channel_id=1, source_target_pairs={{16,0},{32,16},{48,32},{64,48},{80,64},{96,80},{112,96},{128,112},... | collective-permute-start | bytes 6152 | tf_op jit(solution)/shard_map/ppermute | solution.py:19
  39.9 6.7 %collective-permute-start.7 = (f32[2,2,128]{2,1,0:T(2,128)S(1)}, f32[2,2,128]{2,1,0:T(2,128)S(1)}, u32[]{:S(2)}, u32[]{:S(2)}) collective-permute-start(f32[2,2,128]{2,1,0:T(2,128)S(1)} %get-tuple-element.40), channel_id=1, source_target_pairs={{1008,0},{0,16},{16,32},{32,48},{48,64},{64,80},{80,96},{96,112},{... | collective-permute-start | bytes 6152 | tf_op jit(solution)/shard_map/ppermute | solution.py:19
  42.4 4.2 %collective-permute-start.6 = (f32[2,2,128]{2,1,0:T(2,128)S(1)}, f32[2,2,128]{2,1,0:T(2,128)S(1)}, u32[]{:S(2)}, u32[]{:S(2)}) collective-permute-start(f32[2,2,128]{2,1,0:T(2,128)S(1)} %get-tuple-element.41), channel_id=1, source_target_pairs={{15,0},{0,1},{1,2},{2,3},{3,4},{4,5},{5,6},{6,7},{7,8},{8,9},{9,10... | collective-permute-start | bytes 6152 | tf_op jit(solution)/shard_map/ppermute | solution.py:19
  46.7 7.3 %copy-start.3 = (f32[2,2,128]{2,1,0:T(2,128)}, f32[2,2,128]{2,1,0:T(2,128)S(1)}, u32[]{:S(2)}) copy-start(f32[2,2,128]{2,1,0:T(2,128)S(1)} %get-tuple-element.31) | copy-start | bytes 6148
  47.3 7.1 %collective-permute-start.8 = (f32[2,2,128]{2,1,0:T(2,128)S(1)}, f32[2,2,128]{2,1,0:T(2,128)S(1)}, u32[]{:S(2)}, u32[]{:S(2)}) collective-permute-start(f32[2,2,128]{2,1,0:T(2,128)S(1)} %get-tuple-element.31), channel_id=1, source_target_pairs={{1,0},{2,1},{3,2},{4,3},{5,4},{6,5},{7,6},{8,7},{9,8},{10,9},{11,1... | collective-permute-start | bytes 6152 | tf_op jit(solution)/shard_map/ppermute | solution.py:19
  47.4 7.1 %collective-permute-start.9 = (f32[2,2,128]{2,1,0:T(2,128)S(1)}, f32[2,2,128]{2,1,0:T(2,128)S(1)}, u32[]{:S(2)}, u32[]{:S(2)}) collective-permute-start(f32[2,2,128]{2,1,0:T(2,128)S(1)} %get-tuple-element.31), channel_id=1, source_target_pairs={{16,0},{32,16},{48,32},{64,48},{80,64},{96,80},{112,96},{128,112},... | collective-permute-start | bytes 6152 | tf_op jit(solution)/shard_map/ppermute | solution.py:19
  51.8 4.2 %collective-permute-start.10 = (f32[2,2,128]{2,1,0:T(2,128)S(1)}, f32[2,2,128]{2,1,0:T(2,128)S(1)}, u32[]{:S(2)}, u32[]{:S(2)}) collective-permute-start(f32[2,2,128]{2,1,0:T(2,128)S(1)} %get-tuple-element.38), channel_id=1, source_target_pairs={{15,0},{0,1},{1,2},{2,3},{3,4},{4,5},{5,6},{6,7},{7,8},{8,9},{9,10... | collective-permute-start | bytes 6152 | tf_op jit(solution)/shard_map/ppermute | solution.py:19
  52.0 6.7 %collective-permute-start.11 = (f32[2,2,128]{2,1,0:T(2,128)S(1)}, f32[2,2,128]{2,1,0:T(2,128)S(1)}, u32[]{:S(2)}, u32[]{:S(2)}) collective-permute-start(f32[2,2,128]{2,1,0:T(2,128)S(1)} %get-tuple-element.37), channel_id=1, source_target_pairs={{1008,0},{0,16},{16,32},{32,48},{48,64},{64,80},{80,96},{96,112},{... | collective-permute-start | bytes 6152 | tf_op jit(solution)/shard_map/ppermute | solution.py:19

commit v2 on v1

--- a/solution.py
+++ b/solution.py
@@ -192,7 +192,10 @@
 
 def whole_sum(packed):
     for axes in (("sy", "sc"), "tx", "tz"):
-        packed = lax.psum(packed, axes)
+        count = lax.axis_size(axes)
+        copies = jnp.broadcast_to(packed, (count, packed.shape[1]))
+        got = lax.all_to_all(copies, axes, 0, 0, tiled=True)
+        packed = jnp.sum(got, 0, keepdims=True)
     return packed
 
 

time: 128 us -> 103 us (0.80)
  the two profiles are of different devices: /device:TPU:2 before, /device:TPU:1 now
where the time goes in v2:
time: 103 us; the launch traced here: 101 us
  starting transfers between devices  43.3 us (42%)
  blocking collectives  33.1 us (32%)
  waiting for transfers between devices  12.7 us (12%)
  other arithmetic  6.96 us (7%)
  Pallas kernels  2.85 us (3%)
  local copies, waits for them, and re-layouts  1.29 us (1%)
    ppermute x12, starting transfers between devices, shifted(): return lax.ppermute(block, axes, route)  43.3 us
    all_to_all x3, blocking collectives, whole_sum(): got = lax.all_to_all(copies, axes, 0, 0, tiled=True)  33.1 us
    ppermute x12, waiting for transfers between devices, shifted(): return lax.ppermute(block, axes, route)  12.7 us
  transfers between devices with their start and end apart: 12, of which 4 were waited for; matrix products, arithmetic and copies ran while one was open for 5% of the time, Pallas kernels for 0%

profile of v2, /device:TPU:1, one launch (start us, length us, event | category | flops | bytes accessed | tf_op | source)
XLA Modules:
  0.0 101.2 jit_solution(4511180854862552554)
XLA Ops:
  0.6 0.7 convert_bitcast_fusion.1
  1.3 14.1 %collective-permute-start = (f32[2,2,128]{2,1,0:T(2,128)S(1)}, f32[2,2,128]{2,1,0:T(2,128)S(1)}, u32[]{:S(2)}, u32[]{:S(2)}) collective-permute-start(f32[2,2,128]{2,1,0:T(2,128)S(1)} %get-tuple-element.129), channel_id=1, source_target_pairs={{1,0},{2,1},{3,2},{4,3},{5,4},{6,5},{7,6},{8,7},{9,8},{10,9},{11,1... | collective-permute-start | bytes 6152 | tf_op jit(solution)/shard_map/ppermute | solution.py:19
  15.4 7.5 %collective-permute-start.1 = (f32[2,2,128]{2,1,0:T(2,128)S(1)}, f32[2,2,128]{2,1,0:T(2,128)S(1)}, u32[]{:S(2)}, u32[]{:S(2)}) collective-permute-start(f32[2,2,128]{2,1,0:T(2,128)S(1)} %get-tuple-element.129), channel_id=1, source_target_pairs={{16,0},{32,16},{48,32},{64,48},{80,64},{96,80},{112,96},{128,112},... | collective-permute-start | bytes 6152 | tf_op jit(solution)/shard_map/ppermute | solution.py:19
  23.0 0.1 fusion.86
  23.1 1.2 %fusion.1 = (f32[2,2,4,128]{3,2,1,0:T(4,128)S(1)}, f32[2,2,4,128]{3,2,1,0:T(4,128)S(1)}) fusion(f32[2,2,64]{2,1,0:T(2,128)S(1)} %get-tuple-element.127, bf16[1,1,2,2,4,64,128]{6,5,4,3,2,1,0:T(8,128)(2,1)} %param.5, f32[2,2,64]{2,1,0:T(2,128)S(1)} %get-tuple-element.126), kind=kLoop, calls=%fused_computation.19 | loop fusion | flops 651264 | bytes 280576 | tf_op jit(solution)/shard_map/reduce_sum | solution.py:42
  24.3 0.1 slice_add_fusion
  24.4 0.1 fusion.29
  24.5 1.5 %collective-permute-start.2 = (f32[2,2,128]{2,1,0:T(2,128)S(1)}, f32[2,2,128]{2,1,0:T(2,128)S(1)}, u32[]{:S(2)}, u32[]{:S(2)}) collective-permute-start(f32[2,2,128]{2,1,0:T(2,128)S(1)} %bitcast.134), channel_id=1, source_target_pairs={{15,0},{0,1},{1,2},{2,3},{3,4},{4,5},{5,6},{6,7},{7,8},{8,9},{9,10... | collective-permute-start | bytes 6152 | tf_op jit(solution)/shard_map/ppermute | solution.py:19
  26.0 1.9 %collective-permute-start.3 = (f32[2,2,128]{2,1,0:T(2,128)S(1)}, f32[2,2,128]{2,1,0:T(2,128)S(1)}, u32[]{:S(2)}, u32[]{:S(2)}) collective-permute-start(f32[2,2,128]{2,1,0:T(2,128)S(1)} %bitcast.131), channel_id=1, source_target_pairs={{1008,0},{0,16},{16,32},{32,48},{48,64},{64,80},{80,96},{96,112},{... | collective-permute-start | bytes 6152 | tf_op jit(solution)/shard_map/ppermute | solution.py:19
  27.9 0.1 fusion.83
  28.0 0.1 fusion.61
  28.1 0.1 pad_maximum_fusion.6
  28.2 0.1 maximum_bitcast_fusion.1
  28.2 0.2 fusion.18
  28.4 0.1 fusion.55
  28.5 0.1 pad_maximum_fusion.4
  28.6 0.1 pad_maximum_fusion.9
  28.7 0.2 fusion.12
  28.9 4.7 %collective-permute-done.3 = f32[2,2,128]{2,1,0:T(2,128)S(1)} collective-permute-done((f32[2,2,128]{2,1,0:T(2,128)S(1)}, f32[2,2,128]{2,1,0:T(2,128)S(1)}, u32[]{:S(2)}, u32[]{:S(2)}) %collective-permute-start.3) | collective-permute-done | bytes 2080 | tf_op jit(solution)/shard_map/ppermute | solution.py:19
  33.6 0.1 broadcast_multiply_fusion.1
  33.7 2.9 %collective-permute-start.4 = (f32[2,2,128]{2,1,0:T(2,128)S(1)}, f32[2,2,128]{2,1,0:T(2,128)S(1)}, u32[]{:S(2)}, u32[]{:S(2)}) collective-permute-start(f32[2,2,128]{2,1,0:T(2,128)S(1)} %get-tuple-element.33), channel_id=1, source_target_pairs={{1,0},{2,1},{3,2},{4,3},{5,4},{6,5},{7,6},{8,7},{9,8},{10,9},{11,1... | collective-permute-start | bytes 6152 | tf_op jit(solution)/shard_map/ppermute | solution.py:19
  36.6 1.9 %collective-permute-start.5 = (f32[2,2,128]{2,1,0:T(2,128)S(1)}, f32[2,2,128]{2,1,0:T(2,128)S(1)}, u32[]{:S(2)}, u32[]{:S(2)}) collective-permute-start(f32[2,2,128]{2,1,0:T(2,128)S(1)} %get-tuple-element.33), channel_id=1, source_target_pairs={{16,0},{32,16},{48,32},{64,48},{80,64},{96,80},{112,96},{128,112},... | collective-permute-start | bytes 6152 | tf_op jit(solution)/shard_map/ppermute | solution.py:19
  38.5 0.1 fusion.78
  38.7 0.2 fusion.3
  38.9 0.1 fusion.71
  39.1 0.1 fusion.47
  39.1 3.4 %collective-permute-start.7 = (f32[2,2,128]{2,1,0:T(2,128)S(1)}, f32[2,2,128]{2,1,0:T(2,128)S(1)}, u32[]{:S(2)}, u32[]{:S(2)}) collective-permute-start(f32[2,2,128]{2,1,0:T(2,128)S(1)} %get-tuple-element.40), channel_id=1, source_target_pairs={{1008,0},{0,16},{16,32},{32,48},{48,64},{64,80},{80,96},{96,112},{... | collective-permute-start | bytes 6152 | tf_op jit(solution)/shard_map/ppermute | solution.py:19
  42.5 0.1 maximum_bitcast_fusion.5
  42.6 0.2 fusion.20
  42.8 0.1 fusion.63
  42.8 0.1 pad_maximum_fusion.10
  42.9 0.1 fusion.58
  43.1 0.1 pad_maximum_fusion.2
  43.1 0.1 pad_maximum_fusion.13
  43.2 0.2 fusion.14
  43.5 2.6 %collective-permute-done.6 = f32[2,2,128]{2,1,0:T(2,128)S(1)} collective-permute-done((f32[2,2,128]{2,1,0:T(2,128)S(1)}, f32[2,2,128]{2,1,0:T(2,128)S(1)}, u32[]{:S(2)}, u32[]{:S(2)}) %collective-permute-start.6) | collective-permute-done | bytes 2080 | tf_op jit(solution)/shard_map/ppermute | solution.py:19
  46.0 0.7 collective-permute-done.7
  46.8 0.1 broadcast_multiply_fusion
  46.9 0.1 fusion.74
  46.9 0.2 fusion.5
  47.1 0.1 fusion.69
  47.2 0.1 fusion.70
  47.3 0.1 fusion.60
  47.4 0.1 fusion.49
  47.5 3.3 %collective-permute-start.8 = (f32[2,2,128]{2,1,0:T(2,128)S(1)}, f32[2,2,128]{2,1,0:T(2,128)S(1)}, u32[]{:S(2)}, u32[]{:S(2)}) collective-permute-start(f32[2,2,128]{2,1,0:T(2,128)S(1)} %get-tuple-element.31), channel_id=1, source_target_pairs={{1,0},{2,1},{3,2},{4,3},{5,4},{6,5},{7,6},{8,7},{9,8},{10,9},{11,1... | collective-permute-start | bytes 6152 | tf_op jit(solution)/shard_map/ppermute | solution.py:19
  50.8 4.8 %collective-permute-start.9 = (f32[2,2,128]{2,1,0:T(2,128)S(1)}, f32[2,2,128]{2,1,0:T(2,128)S(1)}, u32[]{:S(2)}, u32[]{:S(2)}) collective-permute-start(f32[2,2,128]{2,1,0:T(2,128)S(1)} %get-tuple-element.31), channel_id=1, source_target_pairs={{16,0},{32,16},{48,32},{64,48},{80,64},{96,80},{112,96},{128,112},... | collective-permute-start | bytes 6152 | tf_op jit(solution)/shard_map/ppermute | solution.py:19
  55.7 1.9 %collective-permute-start.11 = (f32[2,2,128]{2,1,0:T(2,128)S(1)}, f32[2,2,128]{2,1,0:T(2,128)S(1)}, u32[]{:S(2)}, u32[]{:S(2)}) collective-permute-start(f32[2,2,128]{2,1,0:T(2,128)S(1)} %get-tuple-element.37), channel_id=1, source_target_pairs={{1008,0},{0,16},{16,32},{32,48},{48,64},{64,80},{80,96},{96,112},{... | collective-permute-start | bytes 6152 | tf_op jit(solution)/shard_map/ppermute | solution.py:19
  57.7 0.1 fusion.77
  57.7 0.1 fusion.65
  57.8 0.1 maximum_bitcast_fusion.9
  57.9 0.2 fusion.22
  58.1 0.1 pad_maximum_fusion.14
  58.2 0.1 pad_maximum_fusion
  58.3 0.1 pad_maximum_fusion.17
  58.3 0.2 fusion.16
  58.6 4.7 %collective-permute-done.11 = f32[2,2,128]{2,1,0:T(2,128)S(1)} collective-permute-done((f32[2,2,128]{2,1,0:T(2,128)S(1)}, f32[2,2,128]{2,1,0:T(2,128)S(1)}, u32[]{:S(2)}, u32[]{:S(2)}) %collective-permute-start.11) | collective-permute-done | bytes 2080 | tf_op jit(solution)/shard_map/ppermute | solution.py:19
  63.4 0.7 fusion.43
  64.0 1.4 %shard_map.50 = f32[1,128]{1,0:T(1,128)} custom-call(f32[4,128]{1,0:T(4,128)} %bitcast.118, f32[4,128]{1,0:T(4,128)} %bitcast.113, f32[4,128]{1,0:T(4,128)} %bitcast.116, f32[4,128]{1,0:T(4,128)} %bitcast.122), custom_call_target="tpu_custom_call" | custom-call | tf_op jit(solution)/shard_map/pallas_call | solution.py:213
  65.4 0.7 copy-done.6
  66.0 12.7 %all_to_all.18 = f32[16,1,128]{2,1,0:T(1,128)S(1)} all-to-all(f32[16,1,128]{2,1,0:T(1,128)S(1)} %broadcast_in_dim.28), channel_id=1, replica_groups=mesh['tz'=16,'tx'=4,'sy'=8,'sc'=2] {'sy','sc'}, dimensions={0} | all-to-all | bytes 16384 | tf_op jit(solution)/shard_map/all_to_all | solution.py:197
  78.7 6.5 %all_to_all.19 = f32[4,1,128]{2,1,0:T(1,128)S(1)} all-to-all(f32[4,1,128]{2,1,0:T(1,128)S(1)} %broadcast_in_dim.29), channel_id=1, replica_groups=mesh['tz'=16,'tx'=4,'sy'=8,'sc'=2] {'tx'}, dimensions={0} | all-to-all | bytes 4096 | tf_op jit(solution)/shard_map/all_to_all | solution.py:197
  85.2 14.0 %all_to_all.20 = f32[16,1,128]{2,1,0:T(1,128)S(1)} all-to-all(f32[16,1,128]{2,1,0:T(1,128)S(1)} %broadcast_in_dim.30), channel_id=1, replica_groups=mesh['tz'=16,'tx'=4,'sy'=8,'sc'=2] {'tz'}, dimensions={0} | all-to-all | bytes 16384 | tf_op jit(solution)/shard_map/all_to_all | solution.py:197
  99.2 0.6 reduce_sum.269
  99.8 1.5 %shard_map.51 = (f32[4,128]{1,0:T(4,128)}, f32[4,128]{1,0:T(4,128)}) custom-call(f32[1,128]{1,0:T(1,128)} %bitcast.128, f32[4,128]{1,0:T(4,128)} %bitcast.119, f32[4,128]{1,0:T(4,128)} %bitcast.114, f32[4,128]{1,0:T(4,128)} %bitcast.117, f32[4,128]{1,0:T(4,128)} %bitcast.123), custom_call_target="tpu_custom_call" | custom-call | tf_op jit(solution)/shard_map/pallas_call | solution.py:221
  (62 shorter events, 0.4 us)
Async XLA Ops:
  1.3 26.6 %copy-start.4 = (f32[1,1,2,2,128]{4,3,2,1,0:T(2,128)}, f32[1,1,2,2,128]{4,3,2,1,0:T(2,128)S(1)}, u32[]{:S(2)}) copy-start(f32[1,1,2,2,128]{4,3,2,1,0:T(2,128)S(1)} %get-tuple-element.130) | copy-start | bytes 6148
  1.3 21.6 %copy-start.5 = (bf16[1,1,2,2,128]{4,3,2,1,0:T(2,128)(2,1)S(1)}, bf16[1,1,2,2,128]{4,3,2,1,0:T(2,128)(2,1)}, u32[]{:S(2)}) copy-start(bf16[1,1,2,2,128]{4,3,2,1,0:T(2,128)(2,1)} %param.3) | copy-start | bytes 3076
  1.3 27.2 %collective-permute-start = (f32[2,2,128]{2,1,0:T(2,128)S(1)}, f32[2,2,128]{2,1,0:T(2,128)S(1)}, u32[]{:S(2)}, u32[]{:S(2)}) collective-permute-start(f32[2,2,128]{2,1,0:T(2,128)S(1)} %get-tuple-element.129), channel_id=1, source_target_pairs={{1,0},{2,1},{3,2},{4,3},{5,4},{6,5},{7,6},{8,7},{9,8},{10,9},{11,1... | collective-permute-start | bytes 6152 | tf_op jit(solution)/shard_map/ppermute | solution.py:19
  15.4 13.1 %collective-permute-start.1 = (f32[2,2,128]{2,1,0:T(2,128)S(1)}, f32[2,2,128]{2,1,0:T(2,128)S(1)}, u32[]{:S(2)}, u32[]{:S(2)}) collective-permute-start(f32[2,2,128]{2,1,0:T(2,128)S(1)} %get-tuple-element.129), channel_id=1, source_target_pairs={{16,0},{32,16},{48,32},{64,48},{80,64},{96,80},{112,96},{128,112},... | collective-permute-start | bytes 6152 | tf_op jit(solution)/shard_map/ppermute | solution.py:19
  23.1 5.6 %copy-start = (bf16[1,1,2,2,4,64,128]{6,5,4,3,2,1,0:T(8,128)(2,1)S(1)}, bf16[1,1,2,2,4,64,128]{6,5,4,3,2,1,0:T(8,128)(2,1)}, u32[]{:S(2)}) copy-start(bf16[1,1,2,2,4,64,128]{6,5,4,3,2,1,0:T(8,128)(2,1)} %param.5) | copy-start | bytes 786436
  24.4 3.8 %copy-start.1 = (bf16[1,1,2,2,64,128]{5,4,3,2,1,0:T(8,128)(2,1)S(1)}, bf16[1,1,2,2,64,128]{5,4,3,2,1,0:T(8,128)(2,1)}, u32[]{:S(2)}) copy-start(bf16[1,1,2,2,64,128]{5,4,3,2,1,0:T(8,128)(2,1)} %param.4) | copy-start | bytes 196612
  24.5 4.5 %collective-permute-start.2 = (f32[2,2,128]{2,1,0:T(2,128)S(1)}, f32[2,2,128]{2,1,0:T(2,128)S(1)}, u32[]{:S(2)}, u32[]{:S(2)}) collective-permute-start(f32[2,2,128]{2,1,0:T(2,128)S(1)} %bitcast.134), channel_id=1, source_target_pairs={{15,0},{0,1},{1,2},{2,3},{3,4},{4,5},{5,6},{6,7},{7,8},{8,9},{9,10... | collective-permute-start | bytes 6152 | tf_op jit(solution)/shard_map/ppermute | solution.py:19
  26.0 7.6 %collective-permute-start.3 = (f32[2,2,128]{2,1,0:T(2,128)S(1)}, f32[2,2,128]{2,1,0:T(2,128)S(1)}, u32[]{:S(2)}, u32[]{:S(2)}) collective-permute-start(f32[2,2,128]{2,1,0:T(2,128)S(1)} %bitcast.131), channel_id=1, source_target_pairs={{1008,0},{0,16},{16,32},{32,48},{48,64},{64,80},{80,96},{96,112},{... | collective-permute-start | bytes 6152 | tf_op jit(solution)/shard_map/ppermute | solution.py:19
  33.7 4.8 %copy-start.2 = (f32[2,2,128]{2,1,0:T(2,128)}, f32[2,2,128]{2,1,0:T(2,128)S(1)}, u32[]{:S(2)}) copy-start(f32[2,2,128]{2,1,0:T(2,128)S(1)} %get-tuple-element.33) | copy-start | bytes 6148
  33.7 9.3 %collective-permute-start.4 = (f32[2,2,128]{2,1,0:T(2,128)S(1)}, f32[2,2,128]{2,1,0:T(2,128)S(1)}, u32[]{:S(2)}, u32[]{:S(2)}) collective-permute-start(f32[2,2,128]{2,1,0:T(2,128)S(1)} %get-tuple-element.33), channel_id=1, source_target_pairs={{1,0},{2,1},{3,2},{4,3},{5,4},{6,5},{7,6},{8,7},{9,8},{10,9},{11,1... | collective-permute-start | bytes 6152 | tf_op jit(solution)/shard_map/ppermute | solution.py:19
  36.6 6.5 %collective-permute-start.5 = (f32[2,2,128]{2,1,0:T(2,128)S(1)}, f32[2,2,128]{2,1,0:T(2,128)S(1)}, u32[]{:S(2)}, u32[]{:S(2)}) collective-permute-start(f32[2,2,128]{2,1,0:T(2,128)S(1)} %get-tuple-element.33), channel_id=1, source_target_pairs={{16,0},{32,16},{48,32},{64,48},{80,64},{96,80},{112,96},{128,112},... | collective-permute-start | bytes 6152 | tf_op jit(solution)/shard_map/ppermute | solution.py:19
  39.1 7.6 %collective-permute-start.7 = (f32[2,2,128]{2,1,0:T(2,128)S(1)}, f32[2,2,128]{2,1,0:T(2,128)S(1)}, u32[]{:S(2)}, u32[]{:S(2)}) collective-permute-start(f32[2,2,128]{2,1,0:T(2,128)S(1)} %get-tuple-element.40), channel_id=1, source_target_pairs={{1008,0},{0,16},{16,32},{32,48},{48,64},{64,80},{80,96},{96,112},{... | collective-permute-start | bytes 6152 | tf_op jit(solution)/shard_map/ppermute | solution.py:19
  43.0 3.0 %collective-permute-start.6 = (f32[2,2,128]{2,1,0:T(2,128)S(1)}, f32[2,2,128]{2,1,0:T(2,128)S(1)}, u32[]{:S(2)}, u32[]{:S(2)}) collective-permute-start(f32[2,2,128]{2,1,0:T(2,128)S(1)} %get-tuple-element.41), channel_id=1, source_target_pairs={{15,0},{0,1},{1,2},{2,3},{3,4},{4,5},{5,6},{6,7},{7,8},{8,9},{9,10... | collective-permute-start | bytes 6152 | tf_op jit(solution)/shard_map/ppermute | solution.py:19
  46.9 10.8 %copy-start.3 = (f32[2,2,128]{2,1,0:T(2,128)}, f32[2,2,128]{2,1,0:T(2,128)S(1)}, u32[]{:S(2)}) copy-start(f32[2,2,128]{2,1,0:T(2,128)S(1)} %get-tuple-element.31) | copy-start | bytes 6148
  47.5 10.7 %collective-permute-start.8 = (f32[2,2,128]{2,1,0:T(2,128)S(1)}, f32[2,2,128]{2,1,0:T(2,128)S(1)}, u32[]{:S(2)}, u32[]{:S(2)}) collective-permute-start(f32[2,2,128]{2,1,0:T(2,128)S(1)} %get-tuple-element.31), channel_id=1, source_target_pairs={{1,0},{2,1},{3,2},{4,3},{5,4},{6,5},{7,6},{8,7},{9,8},{10,9},{11,1... | collective-permute-start | bytes 6152 | tf_op jit(solution)/shard_map/ppermute | solution.py:19
  50.8 7.3 %collective-permute-start.9 = (f32[2,2,128]{2,1,0:T(2,128)S(1)}, f32[2,2,128]{2,1,0:T(2,128)S(1)}, u32[]{:S(2)}, u32[]{:S(2)}) collective-permute-start(f32[2,2,128]{2,1,0:T(2,128)S(1)} %get-tuple-element.31), channel_id=1, source_target_pairs={{16,0},{32,16},{48,32},{64,48},{80,64},{96,80},{112,96},{128,112},... | collective-permute-start | bytes 6152 | tf_op jit(solution)/shard_map/ppermute | solution.py:19
  55.7 2.9 %collective-permute-start.10 = (f32[2,2,128]{2,1,0:T(2,128)S(1)}, f32[2,2,128]{2,1,0:T(2,128)S(1)}, u32[]{:S(2)}, u32[]{:S(2)}) collective-permute-start(f32[2,2,128]{2,1,0:T(2,128)S(1)} %get-tuple-element.38), channel_id=1, source_target_pairs={{15,0},{0,1},{1,2},{2,3},{3,4},{4,5},{5,6},{6,7},{7,8},{8,9},{9,10... | collective-permute-start | bytes 6152 | tf_op jit(solution)/shard_map/ppermute | solution.py:19
  55.7 7.6 %collective-permute-start.11 = (f32[2,2,128]{2,1,0:T(2,128)S(1)}, f32[2,2,128]{2,1,0:T(2,128)S(1)}, u32[]{:S(2)}, u32[]{:S(2)}) collective-permute-start(f32[2,2,128]{2,1,0:T(2,128)S(1)} %get-tuple-element.37), channel_id=1, source_target_pairs={{1008,0},{0,16},{16,32},{32,48},{48,64},{64,80},{80,96},{96,112},{... | collective-permute-start | bytes 6152 | tf_op jit(solution)/shard_map/ppermute | solution.py:19
  65.4 0.7 copy-start.6

commit v3 on v2

--- a/solution.py
+++ b/solution.py
@@ -13,10 +13,18 @@
 PAIRS = ((0, 1), (0, 2), (0, 3), (1, 2), (1, 3), (2, 3))
 
 
-def shifted(block, axes, distance):
+def exchanged(field, carried, axes):
     count = lax.axis_size(axes)
-    route = [((i - distance) % count, i) for i in range(count)]
-    return lax.ppermute(block, axes, route)
+    even = lax.axis_index(axes) % 2 == 0
+    inside = lax.ppermute(
+        jnp.where(even, carried, field), axes, [(i, i ^ 1) for i in range(count)]
+    )
+    across = lax.ppermute(
+        jnp.where(even, field, carried),
+        axes,
+        [(i, (i + (1 if i % 2 else -1)) % count) for i in range(count)],
+    )
+    return jnp.where(even, inside, across), jnp.where(even, across, inside)
 
 
 def chirality_signs(full_width):
@@ -51,11 +59,9 @@
 
 def apply_operator(field, self_block, hop_blocks):
     signs = chirality_signs(field.shape[-1])
-    ahead_z = shifted(field, Z_AXES, -1)
-    ahead_t = shifted(field, T_AXES, -1)
     carried = adjoint(hop_blocks, field * signs)
-    behind_z = shifted(carried[:, :, 2], Z_AXES, 1)
-    behind_t = shifted(carried[:, :, 3], T_AXES, 1)
+    ahead_t, behind_t = exchanged(field, carried[:, :, 3], T_AXES)
+    ahead_z, behind_z = exchanged(field, carried[:, :, 2], Z_AXES)
     near = forward_sum(self_block[:, :, None], field[:, :, None])
     near_hops = jnp.stack([jnp.roll(field, -1, 1), jnp.roll(field, -1, 0)], 2)
     near = near + forward_sum(hop_blocks[:, :, :2], near_hops)
@@ -191,7 +197,7 @@
 
 
 def whole_sum(packed):
-    for axes in (("sy", "sc"), "tx", "tz"):
+    for axes in (("tx", "sy", "sc"), "tz"):
         count = lax.axis_size(axes)
         copies = jnp.broadcast_to(packed, (count, packed.shape[1]))
         got = lax.all_to_all(copies, axes, 0, 0, tiled=True)

time: 103 us -> 107 us (1.039)
  starting transfers between devices: 43.3 us -> 52.8 us
  blocking collectives: 33.1 us -> 30.2 us
  waiting for transfers between devices: 12.7 us -> 10.3 us
  local copies, waits for them, and re-layouts: 1.29 us -> 2.53 us
    ppermute x12, starting transfers between devices: 43.3 us -> 52.8 us  [the longest x6 32 us: exchanged(): lax.ppermute(jnp.where(even, carried, field), axes, [(i, i ^ 1) for i in...]
    all_to_all x3 -> x2, blocking collectives: 33.1 us -> 30.2 us  [whole_sum(): got = lax.all_to_all(copies, axes, 0, 0, tiled=True)]
    ppermute x12, waiting for transfers between devices: 12.7 us -> 10.3 us  [the longest x6 9.13 us: exchanged(): lax.ppermute(jnp.where(even, field, carried), axes, [(i, (i + (1 if i % 2...]
    unnamed x14, local copies, waits for them, and re-layouts: 0.68 us -> 1.92 us
  transfers between devices with their start and end apart: 12 -> 12, of which waited for: 4 -> 3; matrix products, arithmetic and copies ran while one was open for 5% -> 1% of each run, Pallas kernels for 0% -> 0%
where the time goes in v3:
time: 107 us; the launch traced here: 106 us
  starting transfers between devices  52.8 us (49%)
  blocking collectives  30.2 us (28%)
  waiting for transfers between devices  10.3 us (10%)
  other arithmetic  6.43 us (6%)
  Pallas kernels  2.85 us (3%)
  local copies, waits for them, and re-layouts  2.53 us (2%)
  between operations  1.09 us (1%)
    ppermute x6, starting transfers between devices, exchanged(): lax.ppermute(jnp.where(even, carried, field), axes, [(i, i ^ 1) for i in...  32 us
    all_to_all x2, blocking collectives, whole_sum(): got = lax.all_to_all(copies, axes, 0, 0, tiled=True)  30.2 us
    ppermute x6, starting transfers between devices, exchanged(): lax.ppermute(jnp.where(even, field, carried), axes, [(i, (i + (1 if i % 2...  20.8 us
    ppermute x6, waiting for transfers between devices, exchanged(): lax.ppermute(jnp.where(even, field, carried), axes, [(i, (i + (1 if i % 2...  9.13 us
  transfers between devices with their start and end apart: 12, of which 3 were waited for; matrix products, arithmetic and copies ran while one was open for 1% of the time, Pallas kernels for 0%

profile of v3, /device:TPU:1, one launch (start us, length us, event | category | flops | bytes accessed | tf_op | source)
XLA Modules:
  0.0 106.2 jit_solution(15798335114364084304)
XLA Ops:
  0.7 0.7 copy-done.5
  1.4 0.1 fusion.87
  1.4 1.2 %fusion = (f32[2,2,4,128]{3,2,1,0:T(4,128)S(1)}, f32[2,2,4,128]{3,2,1,0:T(4,128)S(1)}) fusion(f32[2,2,64]{2,1,0:T(2,128)S(1)} %get-tuple-element.141, bf16[1,1,2,2,4,64,128]{6,5,4,3,2,1,0:T(8,128)(2,1)} %param.5, f32[2,2,64]{2,1,0:T(2,128)S(1)} %get-tuple-element.140), kind=kLoop, calls=%fused_computation.18 | loop fusion | flops 651264 | bytes 280576 | tf_op jit(solution)/shard_map/reduce_sum | solution.py:49
  2.6 0.1 slice_subtract_fusion
  2.7 0.1 fusion.32
  2.8 16.0 %collective-permute-start = (f32[2,2,128]{2,1,0:T(2,128)S(1)}, f32[2,2,128]{2,1,0:T(2,128)S(1)}, u32[]{:S(2)}, u32[]{:S(2)}) collective-permute-start(f32[2,2,128]{2,1,0:T(2,128)S(1)} %get-tuple-element.95), channel_id=1, source_target_pairs={{0,1},{1,0},{2,3},{3,2},{4,5},{5,4},{6,7},{7,6},{8,9},{9,8},{10,11... | collective-permute-start | bytes 6152 | tf_op jit(solution)/shard_map/ppermute | solution.py:19
  18.9 1.9 %collective-permute-start.1 = (f32[2,2,128]{2,1,0:T(2,128)S(1)}, f32[2,2,128]{2,1,0:T(2,128)S(1)}, u32[]{:S(2)}, u32[]{:S(2)}) collective-permute-start(f32[2,2,128]{2,1,0:T(2,128)S(1)} %get-tuple-element.96), channel_id=1, source_target_pairs={{0,15},{1,2},{2,1},{3,4},{4,3},{5,6},{6,5},{7,8},{8,7},{9,10},{10,... | collective-permute-start | bytes 6152 | tf_op jit(solution)/shard_map/ppermute | solution.py:22
  20.8 8.7 %collective-permute-start.3 = (f32[2,2,128]{2,1,0:T(2,128)S(1)}, f32[2,2,128]{2,1,0:T(2,128)S(1)}, u32[]{:S(2)}, u32[]{:S(2)}) collective-permute-start(f32[2,2,128]{2,1,0:T(2,128)S(1)} %get-tuple-element.145), channel_id=1, source_target_pairs={{0,1008},{16,32},{32,16},{48,64},{64,48},{80,96},{96,80},{112,128}... | collective-permute-start | bytes 6152 | tf_op jit(solution)/shard_map/ppermute | solution.py:22
  29.5 1.9 %collective-permute-start.2 = (f32[2,2,128]{2,1,0:T(2,128)S(1)}, f32[2,2,128]{2,1,0:T(2,128)S(1)}, u32[]{:S(2)}, u32[]{:S(2)}) collective-permute-start(f32[2,2,128]{2,1,0:T(2,128)S(1)} %get-tuple-element.146), channel_id=1, source_target_pairs={{0,16},{16,0},{32,48},{48,32},{64,80},{80,64},{96,112},{112,96},{1... | collective-permute-start | bytes 6152 | tf_op jit(solution)/shard_map/ppermute | solution.py:19
  31.4 0.6 copy-done.4
  32.0 0.1 fusion.84
  32.1 0.1 fusion.58
  32.2 0.1 maximum_bitcast_fusion.1
  32.3 0.2 fusion.18
  32.4 0.1 pad_maximum_fusion.6
  32.5 0.1 fusion.52
  32.6 1.2 %collective-permute-done.2 = f32[2,2,128]{2,1,0:T(2,128)S(1)} collective-permute-done((f32[2,2,128]{2,1,0:T(2,128)S(1)}, f32[2,2,128]{2,1,0:T(2,128)S(1)}, u32[]{:S(2)}, u32[]{:S(2)}) %collective-permute-start.2) | collective-permute-done | bytes 2080 | tf_op jit(solution)/shard_map/ppermute | solution.py:19
  33.8 0.1 pad_maximum_fusion.4
  33.9 0.1 pad_maximum_fusion.9
  34.0 0.2 fusion.12
  34.2 0.1 broadcast_multiply_fusion.1
  34.3 0.1 fusion.83
  34.4 0.2 fusion.2
  34.6 0.1 fusion.72
  34.8 0.1 fusion.48
  34.9 0.1 bitcast_select_fusion.6
  35.0 0.1 fusion.79
  35.1 5.7 %collective-permute-start.4 = (f32[2,2,128]{2,1,0:T(2,128)S(1)}, f32[2,2,128]{2,1,0:T(2,128)S(1)}, u32[]{:S(2)}, u32[]{:S(2)}) collective-permute-start(f32[2,2,128]{2,1,0:T(2,128)S(1)} %get-tuple-element.125), channel_id=1, source_target_pairs={{0,1},{1,0},{2,3},{3,2},{4,5},{5,4},{6,7},{7,6},{8,9},{9,8},{10,11... | collective-permute-start | bytes 6152 | tf_op jit(solution)/shard_map/ppermute | solution.py:19
  40.8 1.9 %collective-permute-start.5 = (f32[2,2,128]{2,1,0:T(2,128)S(1)}, f32[2,2,128]{2,1,0:T(2,128)S(1)}, u32[]{:S(2)}, u32[]{:S(2)}) collective-permute-start(f32[2,2,128]{2,1,0:T(2,128)S(1)} %get-tuple-element.36), channel_id=1, source_target_pairs={{0,15},{1,2},{2,1},{3,4},{4,3},{5,6},{6,5},{7,8},{8,7},{9,10},{10,... | collective-permute-start | bytes 6152 | tf_op jit(solution)/shard_map/ppermute | solution.py:22
  42.8 0.1 maximum_bitcast_fusion.5
  42.8 0.2 fusion.20
  43.0 0.1 fusion.60
  43.1 0.1 pad_maximum_fusion.10
  43.1 0.1 fusion.56
  43.2 1.9 %collective-permute-start.6 = (f32[2,2,128]{2,1,0:T(2,128)S(1)}, f32[2,2,128]{2,1,0:T(2,128)S(1)}, u32[]{:S(2)}, u32[]{:S(2)}) collective-permute-start(f32[2,2,128]{2,1,0:T(2,128)S(1)} %get-tuple-element.126), channel_id=1, source_target_pairs={{0,16},{16,0},{32,48},{48,32},{64,80},{80,64},{96,112},{112,96},{1... | collective-permute-start | bytes 6152 | tf_op jit(solution)/shard_map/ppermute | solution.py:19
  45.2 3.0 %collective-permute-start.7 = (f32[2,2,128]{2,1,0:T(2,128)S(1)}, f32[2,2,128]{2,1,0:T(2,128)S(1)}, u32[]{:S(2)}, u32[]{:S(2)}) collective-permute-start(f32[2,2,128]{2,1,0:T(2,128)S(1)} %get-tuple-element.44), channel_id=1, source_target_pairs={{0,1008},{16,32},{32,16},{48,64},{64,48},{80,96},{96,80},{112,128}... | collective-permute-start | bytes 6152 | tf_op jit(solution)/shard_map/ppermute | solution.py:22
  48.2 4.6 %collective-permute-done.7 = f32[2,2,128]{2,1,0:T(2,128)S(1)} collective-permute-done((f32[2,2,128]{2,1,0:T(2,128)S(1)}, f32[2,2,128]{2,1,0:T(2,128)S(1)}, u32[]{:S(2)}, u32[]{:S(2)}) %collective-permute-start.7) | collective-permute-done | bytes 2080 | tf_op jit(solution)/shard_map/ppermute | solution.py:22
  52.8 0.1 pad_maximum_fusion.2
  52.9 0.1 pad_maximum_fusion.13
  53.0 0.2 fusion.14
  53.2 0.1 broadcast_multiply_fusion
  53.4 0.2 fusion.4
  53.8 0.1 fusion.49
  53.9 0.1 bitcast_select_fusion
  54.0 4.5 %collective-permute-start.8 = (f32[2,2,128]{2,1,0:T(2,128)S(1)}, f32[2,2,128]{2,1,0:T(2,128)S(1)}, u32[]{:S(2)}, u32[]{:S(2)}) collective-permute-start(f32[2,2,128]{2,1,0:T(2,128)S(1)} %get-tuple-element.105), channel_id=1, source_target_pairs={{0,1},{1,0},{2,3},{3,2},{4,5},{5,4},{6,7},{7,6},{8,9},{9,8},{10,11... | collective-permute-start | bytes 6152 | tf_op jit(solution)/shard_map/ppermute | solution.py:19
  58.6 2.2 %collective-permute-start.9 = (f32[2,2,128]{2,1,0:T(2,128)S(1)}, f32[2,2,128]{2,1,0:T(2,128)S(1)}, u32[]{:S(2)}, u32[]{:S(2)}) collective-permute-start(f32[2,2,128]{2,1,0:T(2,128)S(1)} %get-tuple-element.30), channel_id=1, source_target_pairs={{0,15},{1,2},{2,1},{3,4},{4,3},{5,6},{6,5},{7,8},{8,7},{9,10},{10,... | collective-permute-start | bytes 6152 | tf_op jit(solution)/shard_map/ppermute | solution.py:22
  60.8 0.1 maximum_bitcast_fusion.9
  60.9 0.2 fusion.22
  61.0 0.1 fusion.62
  61.1 0.1 pad_maximum_fusion.14
  61.2 0.1 fusion.57
  61.3 1.9 %collective-permute-start.10 = (f32[2,2,128]{2,1,0:T(2,128)S(1)}, f32[2,2,128]{2,1,0:T(2,128)S(1)}, u32[]{:S(2)}, u32[]{:S(2)}) collective-permute-start(f32[2,2,128]{2,1,0:T(2,128)S(1)} %get-tuple-element.106), channel_id=1, source_target_pairs={{0,16},{16,0},{32,48},{48,32},{64,80},{80,64},{96,112},{112,96},{1... | collective-permute-start | bytes 6152 | tf_op jit(solution)/shard_map/ppermute | solution.py:19
  63.2 3.0 %collective-permute-start.11 = (f32[2,2,128]{2,1,0:T(2,128)S(1)}, f32[2,2,128]{2,1,0:T(2,128)S(1)}, u32[]{:S(2)}, u32[]{:S(2)}) collective-permute-start(f32[2,2,128]{2,1,0:T(2,128)S(1)} %get-tuple-element.42), channel_id=1, source_target_pairs={{0,1008},{16,32},{32,16},{48,64},{64,48},{80,96},{96,80},{112,128}... | collective-permute-start | bytes 6152 | tf_op jit(solution)/shard_map/ppermute | solution.py:22
  66.3 4.6 %collective-permute-done.11 = f32[2,2,128]{2,1,0:T(2,128)S(1)} collective-permute-done((f32[2,2,128]{2,1,0:T(2,128)S(1)}, f32[2,2,128]{2,1,0:T(2,128)S(1)}, u32[]{:S(2)}, u32[]{:S(2)}) %collective-permute-start.11) | collective-permute-done | bytes 2080 | tf_op jit(solution)/shard_map/ppermute | solution.py:22
  70.9 0.1 pad_maximum_fusion
  70.9 0.1 pad_maximum_fusion.17
  71.0 0.2 fusion.16
  71.3 0.7 fusion.44
  71.9 1.4 %shard_map.50 = f32[1,128]{1,0:T(1,128)} custom-call(f32[4,128]{1,0:T(4,128)} %bitcast.130, f32[4,128]{1,0:T(4,128)} %bitcast.124, f32[4,128]{1,0:T(4,128)} %bitcast.127, f32[4,128]{1,0:T(4,128)} %bitcast.133), custom_call_target="tpu_custom_call" | custom-call | tf_op jit(solution)/shard_map/pallas_call | solution.py:219
  73.3 0.7 copy-done.6
  74.0 15.4 %all_to_all.12 = f32[64,1,128]{2,1,0:T(1,128)S(1)} all-to-all(f32[64,1,128]{2,1,0:T(1,128)S(1)} %broadcast_in_dim.26), channel_id=1, replica_groups=mesh['tz'=16,'tx'=4,'sy'=8,'sc'=2] {'tx','sy','sc'}, dimensions={0} | all-to-all | bytes 65536 | tf_op jit(solution)/shard_map/all_to_all | solution.py:203
  89.4 14.8 %all_to_all.13 = f32[16,1,128]{2,1,0:T(1,128)S(1)} all-to-all(f32[16,1,128]{2,1,0:T(1,128)S(1)} %broadcast_in_dim.27), channel_id=1, replica_groups=mesh['tz'=16,'tx'=4,'sy'=8,'sc'=2] {'tz'}, dimensions={0} | all-to-all | bytes 16384 | tf_op jit(solution)/shard_map/all_to_all | solution.py:203
  104.2 0.6 reduce_sum.259
  104.7 1.5 %shard_map.51 = (f32[4,128]{1,0:T(4,128)}, f32[4,128]{1,0:T(4,128)}) custom-call(f32[1,128]{1,0:T(1,128)} %bitcast.141, f32[4,128]{1,0:T(4,128)} %bitcast.131, f32[4,128]{1,0:T(4,128)} %bitcast.125, f32[4,128]{1,0:T(4,128)} %bitcast.128, f32[4,128]{1,0:T(4,128)} %bitcast.134), custom_call_target="tpu_custom_call" | custom-call | tf_op jit(solution)/shard_map/pallas_call | solution.py:227
  (70 shorter events, 0.7 us)
Async XLA Ops:
  0.7 0.7 copy-start.5
  1.4 30.8 %copy-start.1 = (bf16[1,1,2,2,64,128]{5,4,3,2,1,0:T(8,128)(2,1)S(1)}, bf16[1,1,2,2,64,128]{5,4,3,2,1,0:T(8,128)(2,1)}, u32[]{:S(2)}) copy-start(bf16[1,1,2,2,64,128]{5,4,3,2,1,0:T(8,128)(2,1)} %param.4) | copy-start | bytes 196612
  2.6 31.4 %copy-start = (bf16[1,1,2,2,4,64,128]{6,5,4,3,2,1,0:T(8,128)(2,1)S(1)}, bf16[1,1,2,2,4,64,128]{6,5,4,3,2,1,0:T(8,128)(2,1)}, u32[]{:S(2)}) copy-start(bf16[1,1,2,2,4,64,128]{6,5,4,3,2,1,0:T(8,128)(2,1)} %param.5) | copy-start | bytes 786436
  2.8 29.8 %collective-permute-start = (f32[2,2,128]{2,1,0:T(2,128)S(1)}, f32[2,2,128]{2,1,0:T(2,128)S(1)}, u32[]{:S(2)}, u32[]{:S(2)}) collective-permute-start(f32[2,2,128]{2,1,0:T(2,128)S(1)} %get-tuple-element.95), channel_id=1, source_target_pairs={{0,1},{1,0},{2,3},{3,2},{4,5},{5,4},{6,7},{7,6},{8,9},{9,8},{10,11... | collective-permute-start | bytes 6152 | tf_op jit(solution)/shard_map/ppermute | solution.py:19
  18.9 13.8 %collective-permute-start.1 = (f32[2,2,128]{2,1,0:T(2,128)S(1)}, f32[2,2,128]{2,1,0:T(2,128)S(1)}, u32[]{:S(2)}, u32[]{:S(2)}) collective-permute-start(f32[2,2,128]{2,1,0:T(2,128)S(1)} %get-tuple-element.96), channel_id=1, source_target_pairs={{0,15},{1,2},{2,1},{3,4},{4,3},{5,6},{6,5},{7,8},{8,7},{9,10},{10,... | collective-permute-start | bytes 6152 | tf_op jit(solution)/shard_map/ppermute | solution.py:22
  20.8 11.8 %collective-permute-start.3 = (f32[2,2,128]{2,1,0:T(2,128)S(1)}, f32[2,2,128]{2,1,0:T(2,128)S(1)}, u32[]{:S(2)}, u32[]{:S(2)}) collective-permute-start(f32[2,2,128]{2,1,0:T(2,128)S(1)} %get-tuple-element.145), channel_id=1, source_target_pairs={{0,1008},{16,32},{32,16},{48,64},{64,48},{80,96},{96,80},{112,128}... | collective-permute-start | bytes 6152 | tf_op jit(solution)/shard_map/ppermute | solution.py:22
  29.5 4.3 %collective-permute-start.2 = (f32[2,2,128]{2,1,0:T(2,128)S(1)}, f32[2,2,128]{2,1,0:T(2,128)S(1)}, u32[]{:S(2)}, u32[]{:S(2)}) collective-permute-start(f32[2,2,128]{2,1,0:T(2,128)S(1)} %get-tuple-element.146), channel_id=1, source_target_pairs={{0,16},{16,0},{32,48},{48,32},{64,80},{80,64},{96,112},{112,96},{1... | collective-permute-start | bytes 6152 | tf_op jit(solution)/shard_map/ppermute | solution.py:19
  31.4 0.6 copy-start.4
  34.3 0.7 copy-start.2
  35.1 13.1 %collective-permute-start.4 = (f32[2,2,128]{2,1,0:T(2,128)S(1)}, f32[2,2,128]{2,1,0:T(2,128)S(1)}, u32[]{:S(2)}, u32[]{:S(2)}) collective-permute-start(f32[2,2,128]{2,1,0:T(2,128)S(1)} %get-tuple-element.125), channel_id=1, source_target_pairs={{0,1},{1,0},{2,3},{3,2},{4,5},{5,4},{6,7},{7,6},{8,9},{9,8},{10,11... | collective-permute-start | bytes 6152 | tf_op jit(solution)/shard_map/ppermute | solution.py:19
  40.8 7.4 %collective-permute-start.5 = (f32[2,2,128]{2,1,0:T(2,128)S(1)}, f32[2,2,128]{2,1,0:T(2,128)S(1)}, u32[]{:S(2)}, u32[]{:S(2)}) collective-permute-start(f32[2,2,128]{2,1,0:T(2,128)S(1)} %get-tuple-element.36), channel_id=1, source_target_pairs={{0,15},{1,2},{2,1},{3,4},{4,3},{5,6},{6,5},{7,8},{8,7},{9,10},{10,... | collective-permute-start | bytes 6152 | tf_op jit(solution)/shard_map/ppermute | solution.py:22
  43.2 5.0 %collective-permute-start.6 = (f32[2,2,128]{2,1,0:T(2,128)S(1)}, f32[2,2,128]{2,1,0:T(2,128)S(1)}, u32[]{:S(2)}, u32[]{:S(2)}) collective-permute-start(f32[2,2,128]{2,1,0:T(2,128)S(1)} %get-tuple-element.126), channel_id=1, source_target_pairs={{0,16},{16,0},{32,48},{48,32},{64,80},{80,64},{96,112},{112,96},{1... | collective-permute-start | bytes 6152 | tf_op jit(solution)/shard_map/ppermute | solution.py:19
  45.2 7.6 %collective-permute-start.7 = (f32[2,2,128]{2,1,0:T(2,128)S(1)}, f32[2,2,128]{2,1,0:T(2,128)S(1)}, u32[]{:S(2)}, u32[]{:S(2)}) collective-permute-start(f32[2,2,128]{2,1,0:T(2,128)S(1)} %get-tuple-element.44), channel_id=1, source_target_pairs={{0,1008},{16,32},{32,16},{48,64},{64,48},{80,96},{96,80},{112,128}... | collective-permute-start | bytes 6152 | tf_op jit(solution)/shard_map/ppermute | solution.py:22
  53.3 0.7 copy-start.3
  54.0 12.2 %collective-permute-start.8 = (f32[2,2,128]{2,1,0:T(2,128)S(1)}, f32[2,2,128]{2,1,0:T(2,128)S(1)}, u32[]{:S(2)}, u32[]{:S(2)}) collective-permute-start(f32[2,2,128]{2,1,0:T(2,128)S(1)} %get-tuple-element.105), channel_id=1, source_target_pairs={{0,1},{1,0},{2,3},{3,2},{4,5},{5,4},{6,7},{7,6},{8,9},{9,8},{10,11... | collective-permute-start | bytes 6152 | tf_op jit(solution)/shard_map/ppermute | solution.py:19
  58.6 7.7 %collective-permute-start.9 = (f32[2,2,128]{2,1,0:T(2,128)S(1)}, f32[2,2,128]{2,1,0:T(2,128)S(1)}, u32[]{:S(2)}, u32[]{:S(2)}) collective-permute-start(f32[2,2,128]{2,1,0:T(2,128)S(1)} %get-tuple-element.30), channel_id=1, source_target_pairs={{0,15},{1,2},{2,1},{3,4},{4,3},{5,6},{6,5},{7,8},{8,7},{9,10},{10,... | collective-permute-start | bytes 6152 | tf_op jit(solution)/shard_map/ppermute | solution.py:22
  61.3 5.0 %collective-permute-start.10 = (f32[2,2,128]{2,1,0:T(2,128)S(1)}, f32[2,2,128]{2,1,0:T(2,128)S(1)}, u32[]{:S(2)}, u32[]{:S(2)}) collective-permute-start(f32[2,2,128]{2,1,0:T(2,128)S(1)} %get-tuple-element.106), channel_id=1, source_target_pairs={{0,16},{16,0},{32,48},{48,32},{64,80},{80,64},{96,112},{112,96},{1... | collective-permute-start | bytes 6152 | tf_op jit(solution)/shard_map/ppermute | solution.py:19
  63.2 7.6 %collective-permute-start.11 = (f32[2,2,128]{2,1,0:T(2,128)S(1)}, f32[2,2,128]{2,1,0:T(2,128)S(1)}, u32[]{:S(2)}, u32[]{:S(2)}) collective-permute-start(f32[2,2,128]{2,1,0:T(2,128)S(1)} %get-tuple-element.42), channel_id=1, source_target_pairs={{0,1008},{16,32},{32,16},{48,64},{64,48},{80,96},{96,80},{112,128}... | collective-permute-start | bytes 6152 | tf_op jit(solution)/shard_map/ppermute | solution.py:22
  73.3 0.7 copy-start.6

commit v4 on v2

--- a/solution.py
+++ b/solution.py
@@ -191,7 +191,7 @@
 
 
 def whole_sum(packed):
-    for axes in (("sy", "sc"), "tx", "tz"):
+    for axes in (("tx", "sy", "sc"), "tz"):
         count = lax.axis_size(axes)
         copies = jnp.broadcast_to(packed, (count, packed.shape[1]))
         got = lax.all_to_all(copies, axes, 0, 0, tiled=True)

time: 103 us -> 98 us (0.951); the launches traced: 101 us -> 97.5 us
  blocking collectives: 33.1 us -> 30.2 us
    all_to_all x3 -> x2, blocking collectives: 33.1 us -> 30.2 us  [whole_sum(): got = lax.all_to_all(copies, axes, 0, 0, tiled=True)]
  transfers between devices with their start and end apart: 12 -> 12, of which waited for: 4 -> 3; matrix products, arithmetic and copies ran while one was open for 5% -> 6% of each run, Pallas kernels for 0% -> 0%
where the time goes in v4:
time: 98 us; the launch traced here: 97.5 us
  starting transfers between devices  43.1 us (44%)
  blocking collectives  30.2 us (31%)
  waiting for transfers between devices  12.2 us (12%)
  other arithmetic  6.93 us (7%)
  Pallas kernels  2.85 us (3%)
  local copies, waits for them, and re-layouts  1.29 us (1%)
    ppermute x12, starting transfers between devices, shifted(): return lax.ppermute(block, axes, route)  43.1 us
    all_to_all x2, blocking collectives, whole_sum(): got = lax.all_to_all(copies, axes, 0, 0, tiled=True)  30.2 us
    ppermute x12, waiting for transfers between devices, shifted(): return lax.ppermute(block, axes, route)  12.2 us
  transfers between devices with their start and end apart: 12, of which 3 were waited for; matrix products, arithmetic and copies ran while one was open for 6% of the time, Pallas kernels for 0%

profile of v4, /device:TPU:1, one launch (start us, length us, event | category | flops | bytes accessed | tf_op | source)
XLA Modules:
  0.0 97.5 jit_solution(14341687051496821855)
XLA Ops:
  0.6 0.7 convert_bitcast_fusion.1
  1.3 14.1 %collective-permute-start = (f32[2,2,128]{2,1,0:T(2,128)S(1)}, f32[2,2,128]{2,1,0:T(2,128)S(1)}, u32[]{:S(2)}, u32[]{:S(2)}) collective-permute-start(f32[2,2,128]{2,1,0:T(2,128)S(1)} %get-tuple-element.129), channel_id=1, source_target_pairs={{1,0},{2,1},{3,2},{4,3},{5,4},{6,5},{7,6},{8,7},{9,8},{10,9},{11,1... | collective-permute-start | bytes 6152 | tf_op jit(solution)/shard_map/ppermute | solution.py:19
  15.4 7.5 %collective-permute-start.1 = (f32[2,2,128]{2,1,0:T(2,128)S(1)}, f32[2,2,128]{2,1,0:T(2,128)S(1)}, u32[]{:S(2)}, u32[]{:S(2)}) collective-permute-start(f32[2,2,128]{2,1,0:T(2,128)S(1)} %get-tuple-element.129), channel_id=1, source_target_pairs={{16,0},{32,16},{48,32},{64,48},{80,64},{96,80},{112,96},{128,112},... | collective-permute-start | bytes 6152 | tf_op jit(solution)/shard_map/ppermute | solution.py:19
  23.0 0.1 fusion.86
  23.1 1.2 %fusion.1 = (f32[2,2,4,128]{3,2,1,0:T(4,128)S(1)}, f32[2,2,4,128]{3,2,1,0:T(4,128)S(1)}) fusion(f32[2,2,64]{2,1,0:T(2,128)S(1)} %get-tuple-element.127, bf16[1,1,2,2,4,64,128]{6,5,4,3,2,1,0:T(8,128)(2,1)} %param.5, f32[2,2,64]{2,1,0:T(2,128)S(1)} %get-tuple-element.126), kind=kLoop, calls=%fused_computation.19 | loop fusion | flops 651264 | bytes 280576 | tf_op jit(solution)/shard_map/reduce_sum | solution.py:42
  24.3 0.1 slice_add_fusion
  24.4 0.1 fusion.29
  24.4 1.9 %collective-permute-start.3 = (f32[2,2,128]{2,1,0:T(2,128)S(1)}, f32[2,2,128]{2,1,0:T(2,128)S(1)}, u32[]{:S(2)}, u32[]{:S(2)}) collective-permute-start(f32[2,2,128]{2,1,0:T(2,128)S(1)} %bitcast.133), channel_id=1, source_target_pairs={{1008,0},{0,16},{16,32},{32,48},{48,64},{64,80},{80,96},{96,112},{... | collective-permute-start | bytes 6152 | tf_op jit(solution)/shard_map/ppermute | solution.py:19
  26.4 1.5 %collective-permute-start.2 = (f32[2,2,128]{2,1,0:T(2,128)S(1)}, f32[2,2,128]{2,1,0:T(2,128)S(1)}, u32[]{:S(2)}, u32[]{:S(2)}) collective-permute-start(f32[2,2,128]{2,1,0:T(2,128)S(1)} %bitcast.129), channel_id=1, source_target_pairs={{15,0},{0,1},{1,2},{2,3},{3,4},{4,5},{5,6},{6,7},{7,8},{8,9},{9,10... | collective-permute-start | bytes 6152 | tf_op jit(solution)/shard_map/ppermute | solution.py:19
  27.9 0.1 fusion.83
  28.0 0.1 fusion.61
  28.0 0.1 maximum_bitcast_fusion.1
  28.1 0.2 fusion.18
  28.3 0.1 pad_maximum_fusion.6
  28.4 0.1 fusion.55
  28.5 0.1 pad_maximum_fusion.4
  28.5 0.1 pad_maximum_fusion.9
  28.7 0.2 fusion.12
  28.9 3.2 %collective-permute-done.3 = f32[2,2,128]{2,1,0:T(2,128)S(1)} collective-permute-done((f32[2,2,128]{2,1,0:T(2,128)S(1)}, f32[2,2,128]{2,1,0:T(2,128)S(1)}, u32[]{:S(2)}, u32[]{:S(2)}) %collective-permute-start.3) | collective-permute-done | bytes 2080 | tf_op jit(solution)/shard_map/ppermute | solution.py:19
  32.1 0.1 broadcast_multiply_fusion.1
  32.2 5.1 %collective-permute-start.5 = (f32[2,2,128]{2,1,0:T(2,128)S(1)}, f32[2,2,128]{2,1,0:T(2,128)S(1)}, u32[]{:S(2)}, u32[]{:S(2)}) collective-permute-start(f32[2,2,128]{2,1,0:T(2,128)S(1)} %get-tuple-element.33), channel_id=1, source_target_pairs={{16,0},{32,16},{48,32},{64,48},{80,64},{96,80},{112,96},{128,112},... | collective-permute-start | bytes 6152 | tf_op jit(solution)/shard_map/ppermute | solution.py:19
  37.3 3.9 %collective-permute-start.4 = (f32[2,2,128]{2,1,0:T(2,128)S(1)}, f32[2,2,128]{2,1,0:T(2,128)S(1)}, u32[]{:S(2)}, u32[]{:S(2)}) collective-permute-start(f32[2,2,128]{2,1,0:T(2,128)S(1)} %get-tuple-element.33), channel_id=1, source_target_pairs={{1,0},{2,1},{3,2},{4,3},{5,4},{6,5},{7,6},{8,7},{9,8},{10,9},{11,1... | collective-permute-start | bytes 6152 | tf_op jit(solution)/shard_map/ppermute | solution.py:19
  41.2 0.1 fusion.82
  41.2 0.1 fusion.78
  41.3 0.2 fusion.3
  41.5 0.1 fusion.72
  41.6 0.1 fusion.71
  41.7 0.1 fusion.47
  41.8 0.1 maximum_bitcast_fusion.5
  41.9 0.2 fusion.20
  42.1 0.1 fusion.63
  42.1 0.1 pad_maximum_fusion.10
  42.2 0.1 fusion.58
  42.3 1.9 %collective-permute-start.7 = (f32[2,2,128]{2,1,0:T(2,128)S(1)}, f32[2,2,128]{2,1,0:T(2,128)S(1)}, u32[]{:S(2)}, u32[]{:S(2)}) collective-permute-start(f32[2,2,128]{2,1,0:T(2,128)S(1)} %get-tuple-element.40), channel_id=1, source_target_pairs={{1008,0},{0,16},{16,32},{32,48},{48,64},{64,80},{80,96},{96,112},{... | collective-permute-start | bytes 6152 | tf_op jit(solution)/shard_map/ppermute | solution.py:19
  44.2 0.1 pad_maximum_fusion.2
  44.3 0.1 pad_maximum_fusion.13
  44.4 0.2 fusion.14
  44.7 5.3 %collective-permute-done.7 = f32[2,2,128]{2,1,0:T(2,128)S(1)} collective-permute-done((f32[2,2,128]{2,1,0:T(2,128)S(1)}, f32[2,2,128]{2,1,0:T(2,128)S(1)}, u32[]{:S(2)}, u32[]{:S(2)}) %collective-permute-start.7) | collective-permute-done | bytes 2080 | tf_op jit(solution)/shard_map/ppermute | solution.py:19
  50.0 0.1 broadcast_multiply_fusion
  50.0 1.9 %collective-permute-start.9 = (f32[2,2,128]{2,1,0:T(2,128)S(1)}, f32[2,2,128]{2,1,0:T(2,128)S(1)}, u32[]{:S(2)}, u32[]{:S(2)}) collective-permute-start(f32[2,2,128]{2,1,0:T(2,128)S(1)} %get-tuple-element.31), channel_id=1, source_target_pairs={{16,0},{32,16},{48,32},{64,48},{80,64},{96,80},{112,96},{128,112},... | collective-permute-start | bytes 6152 | tf_op jit(solution)/shard_map/ppermute | solution.py:19
  52.0 1.7 %collective-permute-start.8 = (f32[2,2,128]{2,1,0:T(2,128)S(1)}, f32[2,2,128]{2,1,0:T(2,128)S(1)}, u32[]{:S(2)}, u32[]{:S(2)}) collective-permute-start(f32[2,2,128]{2,1,0:T(2,128)S(1)} %get-tuple-element.31), channel_id=1, source_target_pairs={{1,0},{2,1},{3,2},{4,3},{5,4},{6,5},{7,6},{8,7},{9,8},{10,9},{11,1... | collective-permute-start | bytes 6152 | tf_op jit(solution)/shard_map/ppermute | solution.py:19
  53.7 0.1 fusion.77
  53.8 0.2 fusion.5
  54.0 0.1 fusion.70
  54.1 0.1 fusion.69
  54.2 0.1 fusion.49
  54.3 0.1 collective-permute-start.10
  54.4 0.1 maximum_bitcast_fusion.9
  54.5 0.2 fusion.22
  54.6 0.1 fusion.65
  54.7 0.1 pad_maximum_fusion.14
  54.8 0.1 fusion.60
  54.9 3.6 %collective-permute-start.11 = (f32[2,2,128]{2,1,0:T(2,128)S(1)}, f32[2,2,128]{2,1,0:T(2,128)S(1)}, u32[]{:S(2)}, u32[]{:S(2)}) collective-permute-start(f32[2,2,128]{2,1,0:T(2,128)S(1)} %get-tuple-element.37), channel_id=1, source_target_pairs={{1008,0},{0,16},{16,32},{32,48},{48,64},{64,80},{80,96},{96,112},{... | collective-permute-start | bytes 6152 | tf_op jit(solution)/shard_map/ppermute | solution.py:19
  58.4 0.1 pad_maximum_fusion
  58.5 0.1 pad_maximum_fusion.17
  58.6 0.2 fusion.16
  58.9 3.6 %collective-permute-done.11 = f32[2,2,128]{2,1,0:T(2,128)S(1)} collective-permute-done((f32[2,2,128]{2,1,0:T(2,128)S(1)}, f32[2,2,128]{2,1,0:T(2,128)S(1)}, u32[]{:S(2)}, u32[]{:S(2)}) %collective-permute-start.11) | collective-permute-done | bytes 2080 | tf_op jit(solution)/shard_map/ppermute | solution.py:19
  62.5 0.7 fusion.43
  63.2 1.4 %shard_map.50 = f32[1,128]{1,0:T(1,128)} custom-call(f32[4,128]{1,0:T(4,128)} %bitcast.118, f32[4,128]{1,0:T(4,128)} %bitcast.113, f32[4,128]{1,0:T(4,128)} %bitcast.116, f32[4,128]{1,0:T(4,128)} %bitcast.121), custom_call_target="tpu_custom_call" | custom-call | tf_op jit(solution)/shard_map/pallas_call | solution.py:213
  64.5 0.7 copy-done.6
  65.2 16.3 %all_to_all.12 = f32[64,1,128]{2,1,0:T(1,128)S(1)} all-to-all(f32[64,1,128]{2,1,0:T(1,128)S(1)} %broadcast_in_dim.26), channel_id=1, replica_groups=mesh['tz'=16,'tx'=4,'sy'=8,'sc'=2] {'tx','sy','sc'}, dimensions={0} | all-to-all | bytes 65536 | tf_op jit(solution)/shard_map/all_to_all | solution.py:197
  81.5 14.0 %all_to_all.13 = f32[16,1,128]{2,1,0:T(1,128)S(1)} all-to-all(f32[16,1,128]{2,1,0:T(1,128)S(1)} %broadcast_in_dim.27), channel_id=1, replica_groups=mesh['tz'=16,'tx'=4,'sy'=8,'sc'=2] {'tz'}, dimensions={0} | all-to-all | bytes 16384 | tf_op jit(solution)/shard_map/all_to_all | solution.py:197
  95.5 0.6 reduce_sum.259
  96.0 1.5 %shard_map.51 = (f32[4,128]{1,0:T(4,128)}, f32[4,128]{1,0:T(4,128)}) custom-call(f32[1,128]{1,0:T(1,128)} %bitcast.127, f32[4,128]{1,0:T(4,128)} %bitcast.119, f32[4,128]{1,0:T(4,128)} %bitcast.114, f32[4,128]{1,0:T(4,128)} %bitcast.117, f32[4,128]{1,0:T(4,128)} %bitcast.122), custom_call_target="tpu_custom_call" | custom-call | tf_op jit(solution)/shard_map/pallas_call | solution.py:221
  (59 shorter events, 0.3 us)
Async XLA Ops:
  1.3 26.6 %copy-start.4 = (f32[1,1,2,2,128]{4,3,2,1,0:T(2,128)}, f32[1,1,2,2,128]{4,3,2,1,0:T(2,128)S(1)}, u32[]{:S(2)}) copy-start(f32[1,1,2,2,128]{4,3,2,1,0:T(2,128)S(1)} %get-tuple-element.130) | copy-start | bytes 6148
  1.3 21.6 %copy-start.5 = (bf16[1,1,2,2,128]{4,3,2,1,0:T(2,128)(2,1)S(1)}, bf16[1,1,2,2,128]{4,3,2,1,0:T(2,128)(2,1)}, u32[]{:S(2)}) copy-start(bf16[1,1,2,2,128]{4,3,2,1,0:T(2,128)(2,1)} %param.3) | copy-start | bytes 3076
  1.3 27.1 %collective-permute-start = (f32[2,2,128]{2,1,0:T(2,128)S(1)}, f32[2,2,128]{2,1,0:T(2,128)S(1)}, u32[]{:S(2)}, u32[]{:S(2)}) collective-permute-start(f32[2,2,128]{2,1,0:T(2,128)S(1)} %get-tuple-element.129), channel_id=1, source_target_pairs={{1,0},{2,1},{3,2},{4,3},{5,4},{6,5},{7,6},{8,7},{9,8},{10,9},{11,1... | collective-permute-start | bytes 6152 | tf_op jit(solution)/shard_map/ppermute | solution.py:19
  15.4 13.0 %collective-permute-start.1 = (f32[2,2,128]{2,1,0:T(2,128)S(1)}, f32[2,2,128]{2,1,0:T(2,128)S(1)}, u32[]{:S(2)}, u32[]{:S(2)}) collective-permute-start(f32[2,2,128]{2,1,0:T(2,128)S(1)} %get-tuple-element.129), channel_id=1, source_target_pairs={{16,0},{32,16},{48,32},{64,48},{80,64},{96,80},{112,96},{128,112},... | collective-permute-start | bytes 6152 | tf_op jit(solution)/shard_map/ppermute | solution.py:19
  23.1 5.6 %copy-start = (bf16[1,1,2,2,4,64,128]{6,5,4,3,2,1,0:T(8,128)(2,1)S(1)}, bf16[1,1,2,2,4,64,128]{6,5,4,3,2,1,0:T(8,128)(2,1)}, u32[]{:S(2)}) copy-start(bf16[1,1,2,2,4,64,128]{6,5,4,3,2,1,0:T(8,128)(2,1)} %param.5) | copy-start | bytes 786436
  24.4 3.8 %copy-start.1 = (bf16[1,1,2,2,64,128]{5,4,3,2,1,0:T(8,128)(2,1)S(1)}, bf16[1,1,2,2,64,128]{5,4,3,2,1,0:T(8,128)(2,1)}, u32[]{:S(2)}) copy-start(bf16[1,1,2,2,64,128]{5,4,3,2,1,0:T(8,128)(2,1)} %param.4) | copy-start | bytes 196612
  24.4 7.6 %collective-permute-start.3 = (f32[2,2,128]{2,1,0:T(2,128)S(1)}, f32[2,2,128]{2,1,0:T(2,128)S(1)}, u32[]{:S(2)}, u32[]{:S(2)}) collective-permute-start(f32[2,2,128]{2,1,0:T(2,128)S(1)} %bitcast.133), channel_id=1, source_target_pairs={{1008,0},{0,16},{16,32},{32,48},{48,64},{64,80},{80,96},{96,112},{... | collective-permute-start | bytes 6152 | tf_op jit(solution)/shard_map/ppermute | solution.py:19
  26.4 5.7 %collective-permute-start.2 = (f32[2,2,128]{2,1,0:T(2,128)S(1)}, f32[2,2,128]{2,1,0:T(2,128)S(1)}, u32[]{:S(2)}, u32[]{:S(2)}) collective-permute-start(f32[2,2,128]{2,1,0:T(2,128)S(1)} %bitcast.129), channel_id=1, source_target_pairs={{15,0},{0,1},{1,2},{2,3},{3,4},{4,5},{5,6},{6,7},{7,8},{8,9},{9,10... | collective-permute-start | bytes 6152 | tf_op jit(solution)/shard_map/ppermute | solution.py:19
  32.2 9.1 %copy-start.2 = (f32[2,2,128]{2,1,0:T(2,128)}, f32[2,2,128]{2,1,0:T(2,128)S(1)}, u32[]{:S(2)}) copy-start(f32[2,2,128]{2,1,0:T(2,128)S(1)} %get-tuple-element.33) | copy-start | bytes 6148
  32.2 12.0 %collective-permute-start.5 = (f32[2,2,128]{2,1,0:T(2,128)S(1)}, f32[2,2,128]{2,1,0:T(2,128)S(1)}, u32[]{:S(2)}, u32[]{:S(2)}) collective-permute-start(f32[2,2,128]{2,1,0:T(2,128)S(1)} %get-tuple-element.33), channel_id=1, source_target_pairs={{16,0},{32,16},{48,32},{64,48},{80,64},{96,80},{112,96},{128,112},... | collective-permute-start | bytes 6152 | tf_op jit(solution)/shard_map/ppermute | solution.py:19
  37.3 6.9 %collective-permute-start.4 = (f32[2,2,128]{2,1,0:T(2,128)S(1)}, f32[2,2,128]{2,1,0:T(2,128)S(1)}, u32[]{:S(2)}, u32[]{:S(2)}) collective-permute-start(f32[2,2,128]{2,1,0:T(2,128)S(1)} %get-tuple-element.33), channel_id=1, source_target_pairs={{1,0},{2,1},{3,2},{4,3},{5,4},{6,5},{7,6},{8,7},{9,8},{10,9},{11,1... | collective-permute-start | bytes 6152 | tf_op jit(solution)/shard_map/ppermute | solution.py:19
  41.8 8.2 %collective-permute-start.6 = (f32[2,2,128]{2,1,0:T(2,128)S(1)}, f32[2,2,128]{2,1,0:T(2,128)S(1)}, u32[]{:S(2)}, u32[]{:S(2)}) collective-permute-start(f32[2,2,128]{2,1,0:T(2,128)S(1)} %get-tuple-element.41), channel_id=1, source_target_pairs={{15,0},{0,1},{1,2},{2,3},{3,4},{4,5},{5,6},{6,7},{7,8},{8,9},{9,10... | collective-permute-start | bytes 6152 | tf_op jit(solution)/shard_map/ppermute | solution.py:19
  42.3 7.6 %collective-permute-start.7 = (f32[2,2,128]{2,1,0:T(2,128)S(1)}, f32[2,2,128]{2,1,0:T(2,128)S(1)}, u32[]{:S(2)}, u32[]{:S(2)}) collective-permute-start(f32[2,2,128]{2,1,0:T(2,128)S(1)} %get-tuple-element.40), channel_id=1, source_target_pairs={{1008,0},{0,16},{16,32},{32,48},{48,64},{64,80},{80,96},{96,112},{... | collective-permute-start | bytes 6152 | tf_op jit(solution)/shard_map/ppermute | solution.py:19
  50.0 3.7 %copy-start.3 = (f32[2,2,128]{2,1,0:T(2,128)}, f32[2,2,128]{2,1,0:T(2,128)S(1)}, u32[]{:S(2)}) copy-start(f32[2,2,128]{2,1,0:T(2,128)S(1)} %get-tuple-element.31) | copy-start | bytes 6148
  50.0 8.4 %collective-permute-start.9 = (f32[2,2,128]{2,1,0:T(2,128)S(1)}, f32[2,2,128]{2,1,0:T(2,128)S(1)}, u32[]{:S(2)}, u32[]{:S(2)}) collective-permute-start(f32[2,2,128]{2,1,0:T(2,128)S(1)} %get-tuple-element.31), channel_id=1, source_target_pairs={{16,0},{32,16},{48,32},{64,48},{80,64},{96,80},{112,96},{128,112},... | collective-permute-start | bytes 6152 | tf_op jit(solution)/shard_map/ppermute | solution.py:19
  52.0 6.5 %collective-permute-start.8 = (f32[2,2,128]{2,1,0:T(2,128)S(1)}, f32[2,2,128]{2,1,0:T(2,128)S(1)}, u32[]{:S(2)}, u32[]{:S(2)}) collective-permute-start(f32[2,2,128]{2,1,0:T(2,128)S(1)} %get-tuple-element.31), channel_id=1, source_target_pairs={{1,0},{2,1},{3,2},{4,3},{5,4},{6,5},{7,6},{8,7},{9,8},{10,9},{11,1... | collective-permute-start | bytes 6152 | tf_op jit(solution)/shard_map/ppermute | solution.py:19
  54.3 8.3 %collective-permute-start.10 = (f32[2,2,128]{2,1,0:T(2,128)S(1)}, f32[2,2,128]{2,1,0:T(2,128)S(1)}, u32[]{:S(2)}, u32[]{:S(2)}) collective-permute-start(f32[2,2,128]{2,1,0:T(2,128)S(1)} %get-tuple-element.38), channel_id=1, source_target_pairs={{15,0},{0,1},{1,2},{2,3},{3,4},{4,5},{5,6},{6,7},{7,8},{8,9},{9,10... | collective-permute-start | bytes 6152 | tf_op jit(solution)/shard_map/ppermute | solution.py:19
  54.9 7.6 %collective-permute-start.11 = (f32[2,2,128]{2,1,0:T(2,128)S(1)}, f32[2,2,128]{2,1,0:T(2,128)S(1)}, u32[]{:S(2)}, u32[]{:S(2)}) collective-permute-start(f32[2,2,128]{2,1,0:T(2,128)S(1)} %get-tuple-element.37), channel_id=1, source_target_pairs={{1008,0},{0,16},{16,32},{32,48},{48,64},{64,80},{80,96},{96,112},{... | collective-permute-start | bytes 6152 | tf_op jit(solution)/shard_map/ppermute | solution.py:19
  64.5 0.7 copy-start.6

commit v5 on v1

--- a/solution.py
+++ b/solution.py
@@ -5,6 +5,7 @@
 from jax.experimental.pallas import tpu as pltpu
 from jax.sharding import Mesh
 from jax.sharding import PartitionSpec as P
+
 
 ITERS = 3
 T_AXES = ("tz", "tx")
@@ -51,11 +52,11 @@
 
 def apply_operator(field, self_block, hop_blocks):
     signs = chirality_signs(field.shape[-1])
+    ahead_t = shifted(field, T_AXES, -1)
     ahead_z = shifted(field, Z_AXES, -1)
-    ahead_t = shifted(field, T_AXES, -1)
     carried = adjoint(hop_blocks, field * signs)
+    behind_t = shifted(carried[:, :, 3], T_AXES, 1)
     behind_z = shifted(carried[:, :, 2], Z_AXES, 1)
-    behind_t = shifted(carried[:, :, 3], T_AXES, 1)
     near = forward_sum(self_block[:, :, None], field[:, :, None])
     near_hops = jnp.stack([jnp.roll(field, -1, 1), jnp.roll(field, -1, 0)], 2)
     near = near + forward_sum(hop_blocks[:, :, :2], near_hops)
@@ -79,7 +80,8 @@
     totals = jnp.sum(stacked, 1, keepdims=True)
     row = lax.broadcasted_iota(jnp.int32, stacked.shape, 0)
     column = lax.broadcasted_iota(jnp.int32, stacked.shape, 1)
-    out[...] = jnp.sum(jnp.where(row == column, totals, 0.0), 0, keepdims=True)
+    packed = jnp.sum(jnp.where(row == column, totals, 0.0), 0, keepdims=True)
+    out[...] = jnp.broadcast_to(packed[None], out.shape)
 
 
 def cmul(a, b):
@@ -170,10 +172,10 @@
     return gram
 
 
-def finish_body(packed, v0, v1, v2, v3, answer_out, residual_out):
+def finish_body(gathered, v0, v1, v2, v3, answer_out, residual_out):
     vectors = [v0[...], v1[...], v2[...], v3[...]]
     half = vectors[0].shape[-1] // 2
-    spread = jnp.broadcast_to(packed[...], (16, 2 * half))
+    spread = jnp.broadcast_to(jnp.sum(gathered[...], 0), (16, 2 * half))
     row = lax.broadcasted_iota(jnp.int32, spread.shape, 0)
     column = lax.broadcasted_iota(jnp.int32, spread.shape, 1)
     totals = jnp.sum(jnp.where(row == column, spread, 0.0), 1, keepdims=True)
@@ -190,10 +192,8 @@
         out[...] = total
 
 
-def whole_sum(packed):
-    for axes in (("sy", "sc"), "tx", "tz"):
-        packed = lax.psum(packed, axes)
-    return packed
+def on_chip(array):
+    return pltpu.with_memory_space_constraint(array, pltpu.VMEM)
 
 
 def on_device(right_side, self_block, hop_blocks):
@@ -205,22 +205,26 @@
     vectors = [right_side[0, 0].astype(jnp.float32)]
     for _ in range(ITERS):
         vectors.append(apply_operator(vectors[-1], local_self, local_hops))
-    flat = [v.reshape(rows) for v in vectors]
+    flat = [on_chip(v.reshape(rows)) for v in vectors]
     space = pl.BlockSpec(memory_space=pltpu.VMEM)
-    packed = pl.pallas_call(
+    near_axes, far_axes = ("tx", "sy", "sc"), "tz"
+    copies = pl.pallas_call(
         gram_body,
-        out_shape=jax.ShapeDtypeStruct((1, rows[1]), jnp.float32),
+        out_shape=pltpu.VMEM((lax.axis_size(near_axes), 1, rows[1]), jnp.float32),
         in_specs=[space] * 4,
         out_specs=space,
     )(*flat)
-    packed = whole_sum(packed)
+    gathered = lax.all_to_all(copies, near_axes, 0, 0, tiled=True)
+    packed = jnp.sum(gathered, 0, keepdims=True)
+    copies = jnp.broadcast_to(packed, (lax.axis_size(far_axes), 1, rows[1]))
+    gathered = lax.all_to_all(copies, far_axes, 0, 0, tiled=True)
     result = jax.ShapeDtypeStruct(rows, jnp.float32)
     answer, residual = pl.pallas_call(
         finish_body,
         out_shape=(result, result),
         in_specs=[space] * 5,
         out_specs=(space, space),
-    )(packed, *flat)
+    )(on_chip(gathered), *flat)
     return answer.reshape(shape), residual.reshape(shape)
 
 

time: 128 us -> 94.4 us (0.74)
  the two profiles are of different devices: /device:TPU:2 before, /device:TPU:1 now
where the time goes in v5:
time: 94.4 us; the launch traced here: 94 us
  starting transfers between devices  43.3 us (46%)
  blocking collectives  30.3 us (32%)
  waiting for transfers between devices  12.1 us (13%)
  other arithmetic  5.85 us (6%)
  Pallas kernels  1 us (1%)
    ppermute x12, starting transfers between devices, shifted(): return lax.ppermute(block, axes, route)  43.3 us
    all_to_all x1, blocking collectives, on_device(): gathered = lax.all_to_all(copies, near_axes, 0, 0, tiled=True)  16.4 us
    all_to_all x1, blocking collectives, on_device(): gathered = lax.all_to_all(copies, far_axes, 0, 0, tiled=True)  14 us
    ppermute x12, waiting for transfers between devices, shifted(): return lax.ppermute(block, axes, route)  12.1 us
  transfers between devices with their start and end apart: 12, of which 3 were waited for; matrix products, arithmetic and copies ran while one was open for 6% of the time, Pallas kernels for 0%

profile of v5, /device:TPU:1, one launch (start us, length us, event | category | flops | bytes accessed | tf_op | source)
XLA Modules:
  0.0 94.0 jit_solution(14139587240861375463)
XLA Ops:
  0.6 0.7 convert_bitcast_fusion.1
  1.3 14.1 %collective-permute-start = (f32[2,2,128]{2,1,0:T(2,128)S(1)}, f32[2,2,128]{2,1,0:T(2,128)S(1)}, u32[]{:S(2)}, u32[]{:S(2)}) collective-permute-start(f32[2,2,128]{2,1,0:T(2,128)S(1)} %get-tuple-element.129), channel_id=1, source_target_pairs={{1,0},{2,1},{3,2},{4,3},{5,4},{6,5},{7,6},{8,7},{9,8},{10,9},{11,1... | collective-permute-start | bytes 6152 | tf_op jit(solution)/shard_map/ppermute | solution.py:20
  15.4 7.5 %collective-permute-start.1 = (f32[2,2,128]{2,1,0:T(2,128)S(1)}, f32[2,2,128]{2,1,0:T(2,128)S(1)}, u32[]{:S(2)}, u32[]{:S(2)}) collective-permute-start(f32[2,2,128]{2,1,0:T(2,128)S(1)} %get-tuple-element.129), channel_id=1, source_target_pairs={{16,0},{32,16},{48,32},{64,48},{80,64},{96,80},{112,96},{128,112},... | collective-permute-start | bytes 6152 | tf_op jit(solution)/shard_map/ppermute | solution.py:20
  23.0 0.1 fusion.86
  23.1 1.2 %fusion.1 = (f32[2,2,4,128]{3,2,1,0:T(4,128)S(1)}, f32[2,2,4,128]{3,2,1,0:T(4,128)S(1)}) fusion(f32[2,2,64]{2,1,0:T(2,128)S(1)} %get-tuple-element.127, bf16[1,1,2,2,4,64,128]{6,5,4,3,2,1,0:T(8,128)(2,1)} %param.5, f32[2,2,64]{2,1,0:T(2,128)S(1)} %get-tuple-element.126), kind=kLoop, calls=%fused_computation.19 | loop fusion | flops 651264 | bytes 280576 | tf_op jit(solution)/shard_map/reduce_sum | solution.py:43
  24.3 0.1 slice_add_fusion
  24.4 0.1 fusion.29
  24.4 1.9 %collective-permute-start.3 = (f32[2,2,128]{2,1,0:T(2,128)S(1)}, f32[2,2,128]{2,1,0:T(2,128)S(1)}, u32[]{:S(2)}, u32[]{:S(2)}) collective-permute-start(f32[2,2,128]{2,1,0:T(2,128)S(1)} %bitcast.125), channel_id=1, source_target_pairs={{1008,0},{0,16},{16,32},{32,48},{48,64},{64,80},{80,96},{96,112},{... | collective-permute-start | bytes 6152 | tf_op jit(solution)/shard_map/ppermute | solution.py:20
  26.4 1.6 %collective-permute-start.2 = (f32[2,2,128]{2,1,0:T(2,128)S(1)}, f32[2,2,128]{2,1,0:T(2,128)S(1)}, u32[]{:S(2)}, u32[]{:S(2)}) collective-permute-start(f32[2,2,128]{2,1,0:T(2,128)S(1)} %bitcast.121), channel_id=1, source_target_pairs={{15,0},{0,1},{1,2},{2,3},{3,4},{4,5},{5,6},{6,7},{7,8},{8,9},{9,10... | collective-permute-start | bytes 6152 | tf_op jit(solution)/shard_map/ppermute | solution.py:20
  28.0 0.1 fusion.83
  28.1 0.1 fusion.61
  28.2 0.1 maximum_bitcast_fusion.1
  28.2 0.2 fusion.18
  28.4 0.1 pad_maximum_fusion.6
  28.5 0.1 fusion.55
  28.6 0.1 pad_maximum_fusion.4
  28.7 0.1 pad_maximum_fusion.9
  28.8 0.2 fusion.12
  29.0 3.1 %collective-permute-done.3 = f32[2,2,128]{2,1,0:T(2,128)S(1)} collective-permute-done((f32[2,2,128]{2,1,0:T(2,128)S(1)}, f32[2,2,128]{2,1,0:T(2,128)S(1)}, u32[]{:S(2)}, u32[]{:S(2)}) %collective-permute-start.3) | collective-permute-done | bytes 2080 | tf_op jit(solution)/shard_map/ppermute | solution.py:20
  32.1 0.1 broadcast_multiply_fusion.1
  32.2 5.1 %collective-permute-start.5 = (f32[2,2,128]{2,1,0:T(2,128)S(1)}, f32[2,2,128]{2,1,0:T(2,128)S(1)}, u32[]{:S(2)}, u32[]{:S(2)}) collective-permute-start(f32[2,2,128]{2,1,0:T(2,128)S(1)} %get-tuple-element.33), channel_id=1, source_target_pairs={{16,0},{32,16},{48,32},{64,48},{80,64},{96,80},{112,96},{128,112},... | collective-permute-start | bytes 6152 | tf_op jit(solution)/shard_map/ppermute | solution.py:20
  37.3 3.9 %collective-permute-start.4 = (f32[2,2,128]{2,1,0:T(2,128)S(1)}, f32[2,2,128]{2,1,0:T(2,128)S(1)}, u32[]{:S(2)}, u32[]{:S(2)}) collective-permute-start(f32[2,2,128]{2,1,0:T(2,128)S(1)} %get-tuple-element.33), channel_id=1, source_target_pairs={{1,0},{2,1},{3,2},{4,3},{5,4},{6,5},{7,6},{8,7},{9,8},{10,9},{11,1... | collective-permute-start | bytes 6152 | tf_op jit(solution)/shard_map/ppermute | solution.py:20
  41.1 0.1 fusion.82
  41.2 0.1 fusion.78
  41.3 0.2 fusion.3
  41.5 0.1 fusion.72
  41.6 0.1 fusion.71
  41.7 0.1 fusion.47
  41.8 0.1 maximum_bitcast_fusion.5
  41.9 0.2 fusion.20
  42.0 0.1 fusion.63
  42.1 0.1 pad_maximum_fusion.10
  42.2 0.1 fusion.58
  42.3 1.9 %collective-permute-start.7 = (f32[2,2,128]{2,1,0:T(2,128)S(1)}, f32[2,2,128]{2,1,0:T(2,128)S(1)}, u32[]{:S(2)}, u32[]{:S(2)}) collective-permute-start(f32[2,2,128]{2,1,0:T(2,128)S(1)} %get-tuple-element.40), channel_id=1, source_target_pairs={{1008,0},{0,16},{16,32},{32,48},{48,64},{64,80},{80,96},{96,112},{... | collective-permute-start | bytes 6152 | tf_op jit(solution)/shard_map/ppermute | solution.py:20
  44.2 0.1 pad_maximum_fusion.2
  44.3 0.1 pad_maximum_fusion.13
  44.4 0.2 fusion.14
  44.6 5.3 %collective-permute-done.7 = f32[2,2,128]{2,1,0:T(2,128)S(1)} collective-permute-done((f32[2,2,128]{2,1,0:T(2,128)S(1)}, f32[2,2,128]{2,1,0:T(2,128)S(1)}, u32[]{:S(2)}, u32[]{:S(2)}) %collective-permute-start.7) | collective-permute-done | bytes 2080 | tf_op jit(solution)/shard_map/ppermute | solution.py:20
  49.9 0.1 broadcast_multiply_fusion
  50.0 1.9 %collective-permute-start.9 = (f32[2,2,128]{2,1,0:T(2,128)S(1)}, f32[2,2,128]{2,1,0:T(2,128)S(1)}, u32[]{:S(2)}, u32[]{:S(2)}) collective-permute-start(f32[2,2,128]{2,1,0:T(2,128)S(1)} %get-tuple-element.31), channel_id=1, source_target_pairs={{16,0},{32,16},{48,32},{64,48},{80,64},{96,80},{112,96},{128,112},... | collective-permute-start | bytes 6152 | tf_op jit(solution)/shard_map/ppermute | solution.py:20
  52.0 1.7 %collective-permute-start.8 = (f32[2,2,128]{2,1,0:T(2,128)S(1)}, f32[2,2,128]{2,1,0:T(2,128)S(1)}, u32[]{:S(2)}, u32[]{:S(2)}) collective-permute-start(f32[2,2,128]{2,1,0:T(2,128)S(1)} %get-tuple-element.31), channel_id=1, source_target_pairs={{1,0},{2,1},{3,2},{4,3},{5,4},{6,5},{7,6},{8,7},{9,8},{10,9},{11,1... | collective-permute-start | bytes 6152 | tf_op jit(solution)/shard_map/ppermute | solution.py:20
  53.6 0.1 fusion.74
  53.7 0.1 fusion.77
  53.8 0.2 fusion.5
  54.0 0.1 fusion.70
  54.0 0.1 fusion.69
  54.1 0.1 fusion.49
  54.2 0.1 collective-permute-start.10
  54.3 0.1 maximum_bitcast_fusion.9
  54.4 0.2 fusion.22
  54.6 0.1 fusion.65
  54.7 0.1 pad_maximum_fusion.14
  54.7 0.1 fusion.60
  54.8 3.6 %collective-permute-start.11 = (f32[2,2,128]{2,1,0:T(2,128)S(1)}, f32[2,2,128]{2,1,0:T(2,128)S(1)}, u32[]{:S(2)}, u32[]{:S(2)}) collective-permute-start(f32[2,2,128]{2,1,0:T(2,128)S(1)} %get-tuple-element.37), channel_id=1, source_target_pairs={{1008,0},{0,16},{16,32},{32,48},{48,64},{64,80},{80,96},{96,112},{... | collective-permute-start | bytes 6152 | tf_op jit(solution)/shard_map/ppermute | solution.py:20
  58.4 0.1 pad_maximum_fusion
  58.5 0.1 pad_maximum_fusion.17
  58.6 0.2 fusion.16
  58.8 3.6 %collective-permute-done.11 = f32[2,2,128]{2,1,0:T(2,128)S(1)} collective-permute-done((f32[2,2,128]{2,1,0:T(2,128)S(1)}, f32[2,2,128]{2,1,0:T(2,128)S(1)}, u32[]{:S(2)}, u32[]{:S(2)}) %collective-permute-start.11) | collective-permute-done | bytes 2080 | tf_op jit(solution)/shard_map/ppermute | solution.py:20
  62.5 0.1 fusion.43
  62.6 0.2 shard_map.50
  62.8 16.4 %all_to_all.10 = f32[64,1,128]{2,1,0:T(1,128)S(1)} all-to-all(f32[64,1,128]{2,1,0:T(1,128)S(1)} %shard_map.50), channel_id=1, replica_groups=mesh['tz'=16,'tx'=4,'sy'=8,'sc'=2] {'tx','sy','sc'}, dimensions={0} | all-to-all | bytes 65536 | tf_op jit(solution)/shard_map/all_to_all | solution.py:217
  79.1 0.1 reduce_sum.249
  79.2 14.0 %all_to_all.11.gathered = f32[16,1,128]{2,1,0:T(1,128)S(1)} all-to-all(f32[16,1,128]{2,1,0:T(1,128)S(1)} %broadcast_in_dim.22), channel_id=1, replica_groups=mesh['tz'=16,'tx'=4,'sy'=8,'sc'=2] {'tz'}, dimensions={0} | all-to-all | bytes 16384 | tf_op jit(solution)/shard_map/all_to_all | solution.py:220
  93.2 0.8 shard_map.51
  (49 shorter events, 0.2 us)
Async XLA Ops:
  1.3 21.6 %copy-start.2 = (bf16[1,1,2,2,128]{4,3,2,1,0:T(2,128)(2,1)S(1)}, bf16[1,1,2,2,128]{4,3,2,1,0:T(2,128)(2,1)}, u32[]{:S(2)}) copy-start(bf16[1,1,2,2,128]{4,3,2,1,0:T(2,128)(2,1)} %param.3) | copy-start | bytes 3076
  1.3 27.2 %collective-permute-start = (f32[2,2,128]{2,1,0:T(2,128)S(1)}, f32[2,2,128]{2,1,0:T(2,128)S(1)}, u32[]{:S(2)}, u32[]{:S(2)}) collective-permute-start(f32[2,2,128]{2,1,0:T(2,128)S(1)} %get-tuple-element.129), channel_id=1, source_target_pairs={{1,0},{2,1},{3,2},{4,3},{5,4},{6,5},{7,6},{8,7},{9,8},{10,9},{11,1... | collective-permute-start | bytes 6152 | tf_op jit(solution)/shard_map/ppermute | solution.py:20
  15.4 13.1 %collective-permute-start.1 = (f32[2,2,128]{2,1,0:T(2,128)S(1)}, f32[2,2,128]{2,1,0:T(2,128)S(1)}, u32[]{:S(2)}, u32[]{:S(2)}) collective-permute-start(f32[2,2,128]{2,1,0:T(2,128)S(1)} %get-tuple-element.129), channel_id=1, source_target_pairs={{16,0},{32,16},{48,32},{64,48},{80,64},{96,80},{112,96},{128,112},... | collective-permute-start | bytes 6152 | tf_op jit(solution)/shard_map/ppermute | solution.py:20
  23.1 5.7 %copy-start = (bf16[1,1,2,2,4,64,128]{6,5,4,3,2,1,0:T(8,128)(2,1)S(1)}, bf16[1,1,2,2,4,64,128]{6,5,4,3,2,1,0:T(8,128)(2,1)}, u32[]{:S(2)}) copy-start(bf16[1,1,2,2,4,64,128]{6,5,4,3,2,1,0:T(8,128)(2,1)} %param.5) | copy-start | bytes 786436
  24.4 3.9 %copy-start.1 = (bf16[1,1,2,2,64,128]{5,4,3,2,1,0:T(8,128)(2,1)S(1)}, bf16[1,1,2,2,64,128]{5,4,3,2,1,0:T(8,128)(2,1)}, u32[]{:S(2)}) copy-start(bf16[1,1,2,2,64,128]{5,4,3,2,1,0:T(8,128)(2,1)} %param.4) | copy-start | bytes 196612
  24.4 7.6 %collective-permute-start.3 = (f32[2,2,128]{2,1,0:T(2,128)S(1)}, f32[2,2,128]{2,1,0:T(2,128)S(1)}, u32[]{:S(2)}, u32[]{:S(2)}) collective-permute-start(f32[2,2,128]{2,1,0:T(2,128)S(1)} %bitcast.125), channel_id=1, source_target_pairs={{1008,0},{0,16},{16,32},{32,48},{48,64},{64,80},{80,96},{96,112},{... | collective-permute-start | bytes 6152 | tf_op jit(solution)/shard_map/ppermute | solution.py:20
  26.4 5.7 %collective-permute-start.2 = (f32[2,2,128]{2,1,0:T(2,128)S(1)}, f32[2,2,128]{2,1,0:T(2,128)S(1)}, u32[]{:S(2)}, u32[]{:S(2)}) collective-permute-start(f32[2,2,128]{2,1,0:T(2,128)S(1)} %bitcast.121), channel_id=1, source_target_pairs={{15,0},{0,1},{1,2},{2,3},{3,4},{4,5},{5,6},{6,7},{7,8},{8,9},{9,10... | collective-permute-start | bytes 6152 | tf_op jit(solution)/shard_map/ppermute | solution.py:20
  32.2 12.0 %collective-permute-start.5 = (f32[2,2,128]{2,1,0:T(2,128)S(1)}, f32[2,2,128]{2,1,0:T(2,128)S(1)}, u32[]{:S(2)}, u32[]{:S(2)}) collective-permute-start(f32[2,2,128]{2,1,0:T(2,128)S(1)} %get-tuple-element.33), channel_id=1, source_target_pairs={{16,0},{32,16},{48,32},{64,48},{80,64},{96,80},{112,96},{128,112},... | collective-permute-start | bytes 6152 | tf_op jit(solution)/shard_map/ppermute | solution.py:20
  37.3 6.9 %collective-permute-start.4 = (f32[2,2,128]{2,1,0:T(2,128)S(1)}, f32[2,2,128]{2,1,0:T(2,128)S(1)}, u32[]{:S(2)}, u32[]{:S(2)}) collective-permute-start(f32[2,2,128]{2,1,0:T(2,128)S(1)} %get-tuple-element.33), channel_id=1, source_target_pairs={{1,0},{2,1},{3,2},{4,3},{5,4},{6,5},{7,6},{8,7},{9,8},{10,9},{11,1... | collective-permute-start | bytes 6152 | tf_op jit(solution)/shard_map/ppermute | solution.py:20
  41.8 8.2 %collective-permute-start.6 = (f32[2,2,128]{2,1,0:T(2,128)S(1)}, f32[2,2,128]{2,1,0:T(2,128)S(1)}, u32[]{:S(2)}, u32[]{:S(2)}) collective-permute-start(f32[2,2,128]{2,1,0:T(2,128)S(1)} %get-tuple-element.41), channel_id=1, source_target_pairs={{15,0},{0,1},{1,2},{2,3},{3,4},{4,5},{5,6},{6,7},{7,8},{8,9},{9,10... | collective-permute-start | bytes 6152 | tf_op jit(solution)/shard_map/ppermute | solution.py:20
  42.3 7.6 %collective-permute-start.7 = (f32[2,2,128]{2,1,0:T(2,128)S(1)}, f32[2,2,128]{2,1,0:T(2,128)S(1)}, u32[]{:S(2)}, u32[]{:S(2)}) collective-permute-start(f32[2,2,128]{2,1,0:T(2,128)S(1)} %get-tuple-element.40), channel_id=1, source_target_pairs={{1008,0},{0,16},{16,32},{32,48},{48,64},{64,80},{80,96},{96,112},{... | collective-permute-start | bytes 6152 | tf_op jit(solution)/shard_map/ppermute | solution.py:20
  50.0 8.4 %collective-permute-start.9 = (f32[2,2,128]{2,1,0:T(2,128)S(1)}, f32[2,2,128]{2,1,0:T(2,128)S(1)}, u32[]{:S(2)}, u32[]{:S(2)}) collective-permute-start(f32[2,2,128]{2,1,0:T(2,128)S(1)} %get-tuple-element.31), channel_id=1, source_target_pairs={{16,0},{32,16},{48,32},{64,48},{80,64},{96,80},{112,96},{128,112},... | collective-permute-start | bytes 6152 | tf_op jit(solution)/shard_map/ppermute | solution.py:20
  52.0 6.4 %collective-permute-start.8 = (f32[2,2,128]{2,1,0:T(2,128)S(1)}, f32[2,2,128]{2,1,0:T(2,128)S(1)}, u32[]{:S(2)}, u32[]{:S(2)}) collective-permute-start(f32[2,2,128]{2,1,0:T(2,128)S(1)} %get-tuple-element.31), channel_id=1, source_target_pairs={{1,0},{2,1},{3,2},{4,3},{5,4},{6,5},{7,6},{8,7},{9,8},{10,9},{11,1... | collective-permute-start | bytes 6152 | tf_op jit(solution)/shard_map/ppermute | solution.py:20
  54.2 8.3 %collective-permute-start.10 = (f32[2,2,128]{2,1,0:T(2,128)S(1)}, f32[2,2,128]{2,1,0:T(2,128)S(1)}, u32[]{:S(2)}, u32[]{:S(2)}) collective-permute-start(f32[2,2,128]{2,1,0:T(2,128)S(1)} %get-tuple-element.38), channel_id=1, source_target_pairs={{15,0},{0,1},{1,2},{2,3},{3,4},{4,5},{5,6},{6,7},{7,8},{8,9},{9,10... | collective-permute-start | bytes 6152 | tf_op jit(solution)/shard_map/ppermute | solution.py:20
  54.8 7.6 %collective-permute-start.11 = (f32[2,2,128]{2,1,0:T(2,128)S(1)}, f32[2,2,128]{2,1,0:T(2,128)S(1)}, u32[]{:S(2)}, u32[]{:S(2)}) collective-permute-start(f32[2,2,128]{2,1,0:T(2,128)S(1)} %get-tuple-element.37), channel_id=1, source_target_pairs={{1008,0},{0,16},{16,32},{32,48},{48,64},{64,80},{80,96},{96,112},{... | collective-permute-start | bytes 6152 | tf_op jit(solution)/shard_map/ppermute | solution.py:20

commit v6 on v5

--- a/solution.py
+++ b/solution.py
@@ -18,6 +18,20 @@
     count = lax.axis_size(axes)
     route = [((i - distance) % count, i) for i in range(count)]
     return lax.ppermute(block, axes, route)
+
+
+def exchanged(field, carried, axes):
+    count = lax.axis_size(axes)
+    even = lax.axis_index(axes) % 2 == 0
+    across = lax.ppermute(
+        jnp.where(even, field, carried),
+        axes,
+        [(i, (i + (1 if i % 2 else -1)) % count) for i in range(count)],
+    )
+    inside = lax.ppermute(
+        jnp.where(even, carried, field), axes, [(i, i ^ 1) for i in range(count)]
+    )
+    return jnp.where(even, inside, across), jnp.where(even, across, inside)
 
 
 def chirality_signs(full_width):
@@ -52,10 +66,9 @@
 
 def apply_operator(field, self_block, hop_blocks):
     signs = chirality_signs(field.shape[-1])
-    ahead_t = shifted(field, T_AXES, -1)
+    carried = adjoint(hop_blocks, field * signs)
+    ahead_t, behind_t = exchanged(field, carried[:, :, 3], T_AXES)
     ahead_z = shifted(field, Z_AXES, -1)
-    carried = adjoint(hop_blocks, field * signs)
-    behind_t = shifted(carried[:, :, 3], T_AXES, 1)
     behind_z = shifted(carried[:, :, 2], Z_AXES, 1)
     near = forward_sum(self_block[:, :, None], field[:, :, None])
     near_hops = jnp.stack([jnp.roll(field, -1, 1), jnp.roll(field, -1, 0)], 2)

time: 94.4 us -> 91.7 us (0.971)
  waiting for transfers between devices: 12.1 us -> 6.13 us
  starting transfers between devices: 43.3 us -> 44.5 us
  blocking collectives: 30.3 us -> 31.5 us
    ppermute x0 -> x6, starting transfers between devices: none -> 23.3 us  [the longest x3 17.5 us: exchanged(): lax.ppermute(jnp.where(even, field, carried), axes, [(i, (i + (1 if i % 2...]
    ppermute x12 -> x6, starting transfers between devices: 43.3 us -> 21.2 us  [shifted(): return lax.ppermute(block, axes, route)]
    ppermute x12 -> x6, waiting for transfers between devices: 12.1 us -> 1.34 us  [shifted(): return lax.ppermute(block, axes, route)]
    ppermute x0 -> x6, waiting for transfers between devices: none -> 4.79 us  [the longest x3 4.78 us: exchanged(): lax.ppermute(jnp.where(even, field, carried), axes, [(i, (i + (1 if i % 2...]
    all_to_all x1, blocking collectives: 14 us -> 16.5 us  [on_device(): gathered = lax.all_to_all(copies, far_axes, 0, 0, tiled=True)]
    all_to_all x1, blocking collectives: 16.4 us -> 15 us  [on_device(): gathered = lax.all_to_all(copies, near_axes, 0, 0, tiled=True)]
where the time goes in v6:
time: 91.7 us; the launch traced here: 91.3 us
  starting transfers between devices  44.5 us (49%)
  blocking collectives  31.5 us (34%)
  waiting for transfers between devices  6.13 us (7%)
  other arithmetic  6 us (7%)
  local copies, waits for them, and re-layouts  1.28 us (1%)
  Pallas kernels  1 us (1%)
  between operations  0.93 us (1%)
    ppermute x6, starting transfers between devices, shifted(): return lax.ppermute(block, axes, route)  21.2 us
    ppermute x3, starting transfers between devices, exchanged(): lax.ppermute(jnp.where(even, field, carried), axes, [(i, (i + (1 if i % 2...  17.5 us
    all_to_all x1, blocking collectives, on_device(): gathered = lax.all_to_all(copies, far_axes, 0, 0, tiled=True)  16.5 us
    all_to_all x1, blocking collectives, on_device(): gathered = lax.all_to_all(copies, near_axes, 0, 0, tiled=True)  15 us
    ppermute x3, starting transfers between devices, exchanged(): lax.ppermute(jnp.where(even, carried, field), axes, [(i, i ^ 1) for i in...  5.76 us
    ppermute x3, waiting for transfers between devices, exchanged(): lax.ppermute(jnp.where(even, field, carried), axes, [(i, (i + (1 if i % 2...  4.78 us
  transfers between devices with their start and end apart: 12, of which 3 were waited for; matrix products, arithmetic and copies ran while one was open for 6% of the time, Pallas kernels for 0%

profile of v6, /device:TPU:1, one launch (start us, length us, event | category | flops | bytes accessed | tf_op | source)
XLA Modules:
  0.0 91.3 jit_solution(12569808511260053923)
XLA Ops:
  0.6 0.7 convert_bitcast_fusion.1
  1.3 14.1 %collective-permute-start = (f32[2,2,128]{2,1,0:T(2,128)S(1)}, f32[2,2,128]{2,1,0:T(2,128)S(1)}, u32[]{:S(2)}, u32[]{:S(2)}) collective-permute-start(f32[2,2,128]{2,1,0:T(2,128)S(1)} %get-tuple-element.133), channel_id=1, source_target_pairs={{1,0},{2,1},{3,2},{4,3},{5,4},{6,5},{7,6},{8,7},{9,8},{10,9},{11,1... | collective-permute-start | bytes 6152 | tf_op jit(solution)/shard_map/ppermute | solution.py:20
  15.4 0.7 copy-done.2
  16.1 0.1 fusion.87
  16.2 1.2 %fusion = (f32[2,2,4,128]{3,2,1,0:T(4,128)S(1)}, f32[2,2,4,128]{3,2,1,0:T(4,128)S(1)}) fusion(f32[2,2,64]{2,1,0:T(2,128)S(1)} %get-tuple-element.131, bf16[1,1,2,2,4,64,128]{6,5,4,3,2,1,0:T(8,128)(2,1)} %param.5, f32[2,2,64]{2,1,0:T(2,128)S(1)} %get-tuple-element.130), kind=kLoop, calls=%fused_computation.18 | loop fusion | flops 651264 | bytes 280576 | tf_op jit(solution)/shard_map/reduce_sum | solution.py:56
  17.4 0.1 slice_subtract_fusion
  17.5 0.1 fusion.29
  17.6 1.9 %collective-permute-start.1 = (f32[2,2,128]{2,1,0:T(2,128)S(1)}, f32[2,2,128]{2,1,0:T(2,128)S(1)}, u32[]{:S(2)}, u32[]{:S(2)}) collective-permute-start(f32[2,2,128]{2,1,0:T(2,128)S(1)} %get-tuple-element.91), channel_id=1, source_target_pairs={{0,16},{16,0},{32,48},{48,32},{64,80},{80,64},{96,112},{112,96},{1... | collective-permute-start | bytes 6152 | tf_op jit(solution)/shard_map/ppermute | solution.py:31
  19.5 8.1 %collective-permute-start.2 = (f32[2,2,128]{2,1,0:T(2,128)S(1)}, f32[2,2,128]{2,1,0:T(2,128)S(1)}, u32[]{:S(2)}, u32[]{:S(2)}) collective-permute-start(f32[2,2,128]{2,1,0:T(2,128)S(1)} %get-tuple-element.92), channel_id=1, source_target_pairs={{0,1008},{16,32},{32,16},{48,64},{64,48},{80,96},{96,80},{112,128}... | collective-permute-start | bytes 6152 | tf_op jit(solution)/shard_map/ppermute | solution.py:26
  27.6 1.8 %collective-permute-start.3 = (f32[2,2,128]{2,1,0:T(2,128)S(1)}, f32[2,2,128]{2,1,0:T(2,128)S(1)}, u32[]{:S(2)}, u32[]{:S(2)}) collective-permute-start(f32[2,2,128]{2,1,0:T(2,128)S(1)} %bitcast.131), channel_id=1, source_target_pairs={{15,0},{0,1},{1,2},{2,3},{3,4},{4,5},{5,6},{6,7},{7,8},{8,9},{9,10... | collective-permute-start | bytes 6152 | tf_op jit(solution)/shard_map/ppermute | solution.py:20
  29.3 0.1 fusion.84
  29.4 0.1 fusion.60
  29.5 0.1 maximum_bitcast_fusion.1
  29.6 0.2 fusion.18
  29.7 0.1 pad_maximum_fusion.6
  29.8 0.1 fusion.54
  30.0 0.1 pad_maximum_fusion.4
  30.0 0.1 pad_maximum_fusion.9
  30.1 0.2 fusion.12
  30.4 1.3 %collective-permute-done.3 = f32[2,2,128]{2,1,0:T(2,128)S(1)} collective-permute-done((f32[2,2,128]{2,1,0:T(2,128)S(1)}, f32[2,2,128]{2,1,0:T(2,128)S(1)}, u32[]{:S(2)}, u32[]{:S(2)}) %collective-permute-start.3) | collective-permute-done | bytes 2080 | tf_op jit(solution)/shard_map/ppermute | solution.py:20
  31.7 0.1 broadcast_multiply_fusion.1
  31.8 3.6 %collective-permute-start.4 = (f32[2,2,128]{2,1,0:T(2,128)S(1)}, f32[2,2,128]{2,1,0:T(2,128)S(1)}, u32[]{:S(2)}, u32[]{:S(2)}) collective-permute-start(f32[2,2,128]{2,1,0:T(2,128)S(1)} %get-tuple-element.37), channel_id=1, source_target_pairs={{1,0},{2,1},{3,2},{4,3},{5,4},{6,5},{7,6},{8,7},{9,8},{10,9},{11,1... | collective-permute-start | bytes 6152 | tf_op jit(solution)/shard_map/ppermute | solution.py:20
  35.4 0.1 fusion.83
  35.4 0.2 fusion.2
  35.7 0.1 fusion.72
  35.8 0.1 bitcast_select_fusion.2
  35.9 0.1 fusion.47
  36.0 0.1 fusion.79
  36.1 1.9 %collective-permute-start.5 = (f32[2,2,128]{2,1,0:T(2,128)S(1)}, f32[2,2,128]{2,1,0:T(2,128)S(1)}, u32[]{:S(2)}, u32[]{:S(2)}) collective-permute-start(f32[2,2,128]{2,1,0:T(2,128)S(1)} %bitcast_select_fusion.3), channel_id=1, source_target_pairs={{0,16},{16,0},{32,48},{48,32},{64,80},{80,64},{96,112},{112,96},{1... | collective-permute-start | bytes 6152 | tf_op jit(solution)/shard_map/ppermute | solution.py:31
  38.0 4.7 %collective-permute-start.6 = (f32[2,2,128]{2,1,0:T(2,128)S(1)}, f32[2,2,128]{2,1,0:T(2,128)S(1)}, u32[]{:S(2)}, u32[]{:S(2)}) collective-permute-start(f32[2,2,128]{2,1,0:T(2,128)S(1)} %get-tuple-element.34), channel_id=1, source_target_pairs={{0,1008},{16,32},{32,16},{48,64},{64,48},{80,96},{96,80},{112,128}... | collective-permute-start | bytes 6152 | tf_op jit(solution)/shard_map/ppermute | solution.py:26
  42.8 0.1 maximum_bitcast_fusion.5
  42.9 0.2 fusion.20
  43.0 0.1 fusion.62
  43.1 0.1 pad_maximum_fusion.10
  43.2 0.1 fusion.56
  43.3 2.4 %collective-permute-done.6 = f32[2,2,128]{2,1,0:T(2,128)S(1)} collective-permute-done((f32[2,2,128]{2,1,0:T(2,128)S(1)}, f32[2,2,128]{2,1,0:T(2,128)S(1)}, u32[]{:S(2)}, u32[]{:S(2)}) %collective-permute-start.6) | collective-permute-done | bytes 2080 | tf_op jit(solution)/shard_map/ppermute | solution.py:26
  45.7 0.1 pad_maximum_fusion.2
  45.7 0.1 pad_maximum_fusion.13
  45.8 0.2 fusion.14
  46.1 0.1 broadcast_multiply_fusion
  46.2 1.2 %collective-permute-start.8 = (f32[2,2,128]{2,1,0:T(2,128)S(1)}, f32[2,2,128]{2,1,0:T(2,128)S(1)}, u32[]{:S(2)}, u32[]{:S(2)}) collective-permute-start(f32[2,2,128]{2,1,0:T(2,128)S(1)} %get-tuple-element.33), channel_id=1, source_target_pairs={{1,0},{2,1},{3,2},{4,3},{5,4},{6,5},{7,6},{8,7},{9,8},{10,9},{11,1... | collective-permute-start | bytes 6152 | tf_op jit(solution)/shard_map/ppermute | solution.py:20
  47.4 0.2 fusion.4
  47.6 0.1 fusion.70
  47.8 0.1 fusion.48
  47.9 0.1 bitcast_select_fusion
  48.0 0.1 fusion.78
  48.1 1.9 %collective-permute-start.9 = (f32[2,2,128]{2,1,0:T(2,128)S(1)}, f32[2,2,128]{2,1,0:T(2,128)S(1)}, u32[]{:S(2)}, u32[]{:S(2)}) collective-permute-start(f32[2,2,128]{2,1,0:T(2,128)S(1)} %bitcast_select_fusion.1), channel_id=1, source_target_pairs={{0,16},{16,0},{32,48},{48,32},{64,80},{80,64},{96,112},{112,96},{1... | collective-permute-start | bytes 6152 | tf_op jit(solution)/shard_map/ppermute | solution.py:31
  50.0 0.6 collective-permute-start.11
  50.6 4.7 %collective-permute-start.10 = (f32[2,2,128]{2,1,0:T(2,128)S(1)}, f32[2,2,128]{2,1,0:T(2,128)S(1)}, u32[]{:S(2)}, u32[]{:S(2)}) collective-permute-start(f32[2,2,128]{2,1,0:T(2,128)S(1)} %get-tuple-element.30), channel_id=1, source_target_pairs={{0,1008},{16,32},{32,16},{48,64},{64,48},{80,96},{96,80},{112,128}... | collective-permute-start | bytes 6152 | tf_op jit(solution)/shard_map/ppermute | solution.py:26
  55.3 0.1 maximum_bitcast_fusion.9
  55.4 0.2 fusion.22
  55.6 0.1 fusion.64
  55.6 0.1 pad_maximum_fusion.14
  55.7 0.1 fusion.58
  55.8 2.4 %collective-permute-done.10 = f32[2,2,128]{2,1,0:T(2,128)S(1)} collective-permute-done((f32[2,2,128]{2,1,0:T(2,128)S(1)}, f32[2,2,128]{2,1,0:T(2,128)S(1)}, u32[]{:S(2)}, u32[]{:S(2)}) %collective-permute-start.10) | collective-permute-done | bytes 2080 | tf_op jit(solution)/shard_map/ppermute | solution.py:26
  58.2 0.1 pad_maximum_fusion
  58.3 0.1 pad_maximum_fusion.17
  58.4 0.2 fusion.16
  58.7 0.1 fusion.43
  58.7 0.2 shard_map.50
  58.9 15.0 %all_to_all.10 = f32[64,1,128]{2,1,0:T(1,128)S(1)} all-to-all(f32[64,1,128]{2,1,0:T(1,128)S(1)} %shard_map.50), channel_id=1, replica_groups=mesh['tz'=16,'tx'=4,'sy'=8,'sc'=2] {'tx','sy','sc'}, dimensions={0} | all-to-all | bytes 65536 | tf_op jit(solution)/shard_map/all_to_all | solution.py:230
  73.9 0.1 reduce_sum.249
  74.0 16.5 %all_to_all.11.gathered = f32[16,1,128]{2,1,0:T(1,128)S(1)} all-to-all(f32[16,1,128]{2,1,0:T(1,128)S(1)} %broadcast_in_dim.22), channel_id=1, replica_groups=mesh['tz'=16,'tx'=4,'sy'=8,'sc'=2] {'tz'}, dimensions={0} | all-to-all | bytes 16384 | tf_op jit(solution)/shard_map/all_to_all | solution.py:233
  90.5 0.8 shard_map.51
  (57 shorter events, 0.5 us)
Async XLA Ops:
  1.3 28.6 %collective-permute-start = (f32[2,2,128]{2,1,0:T(2,128)S(1)}, f32[2,2,128]{2,1,0:T(2,128)S(1)}, u32[]{:S(2)}, u32[]{:S(2)}) collective-permute-start(f32[2,2,128]{2,1,0:T(2,128)S(1)} %get-tuple-element.133), channel_id=1, source_target_pairs={{1,0},{2,1},{3,2},{4,3},{5,4},{6,5},{7,6},{8,7},{9,8},{10,9},{11,1... | collective-permute-start | bytes 6152 | tf_op jit(solution)/shard_map/ppermute | solution.py:20
  15.4 0.7 copy-start.2
  16.2 13.4 %copy-start.1 = (bf16[1,1,2,2,64,128]{5,4,3,2,1,0:T(8,128)(2,1)S(1)}, bf16[1,1,2,2,64,128]{5,4,3,2,1,0:T(8,128)(2,1)}, u32[]{:S(2)}) copy-start(bf16[1,1,2,2,64,128]{5,4,3,2,1,0:T(8,128)(2,1)} %param.4) | copy-start | bytes 196612
  17.4 12.7 %copy-start = (bf16[1,1,2,2,4,64,128]{6,5,4,3,2,1,0:T(8,128)(2,1)S(1)}, bf16[1,1,2,2,4,64,128]{6,5,4,3,2,1,0:T(8,128)(2,1)}, u32[]{:S(2)}) copy-start(bf16[1,1,2,2,4,64,128]{6,5,4,3,2,1,0:T(8,128)(2,1)} %param.5) | copy-start | bytes 786436
  17.6 12.3 %collective-permute-start.1 = (f32[2,2,128]{2,1,0:T(2,128)S(1)}, f32[2,2,128]{2,1,0:T(2,128)S(1)}, u32[]{:S(2)}, u32[]{:S(2)}) collective-permute-start(f32[2,2,128]{2,1,0:T(2,128)S(1)} %get-tuple-element.91), channel_id=1, source_target_pairs={{0,16},{16,0},{32,48},{48,32},{64,80},{80,64},{96,112},{112,96},{1... | collective-permute-start | bytes 6152 | tf_op jit(solution)/shard_map/ppermute | solution.py:31
  19.5 10.4 %collective-permute-start.2 = (f32[2,2,128]{2,1,0:T(2,128)S(1)}, f32[2,2,128]{2,1,0:T(2,128)S(1)}, u32[]{:S(2)}, u32[]{:S(2)}) collective-permute-start(f32[2,2,128]{2,1,0:T(2,128)S(1)} %get-tuple-element.92), channel_id=1, source_target_pairs={{0,1008},{16,32},{32,16},{48,64},{64,48},{80,96},{96,80},{112,128}... | collective-permute-start | bytes 6152 | tf_op jit(solution)/shard_map/ppermute | solution.py:26
  27.6 4.1 %collective-permute-start.3 = (f32[2,2,128]{2,1,0:T(2,128)S(1)}, f32[2,2,128]{2,1,0:T(2,128)S(1)}, u32[]{:S(2)}, u32[]{:S(2)}) collective-permute-start(f32[2,2,128]{2,1,0:T(2,128)S(1)} %bitcast.131), channel_id=1, source_target_pairs={{15,0},{0,1},{1,2},{2,3},{3,4},{4,5},{5,6},{6,7},{7,8},{8,9},{9,10... | collective-permute-start | bytes 6152 | tf_op jit(solution)/shard_map/ppermute | solution.py:20
  31.8 13.9 %collective-permute-start.4 = (f32[2,2,128]{2,1,0:T(2,128)S(1)}, f32[2,2,128]{2,1,0:T(2,128)S(1)}, u32[]{:S(2)}, u32[]{:S(2)}) collective-permute-start(f32[2,2,128]{2,1,0:T(2,128)S(1)} %get-tuple-element.37), channel_id=1, source_target_pairs={{1,0},{2,1},{3,2},{4,3},{5,4},{6,5},{7,6},{8,7},{9,8},{10,9},{11,1... | collective-permute-start | bytes 6152 | tf_op jit(solution)/shard_map/ppermute | solution.py:20
  36.1 7.2 %collective-permute-start.5 = (f32[2,2,128]{2,1,0:T(2,128)S(1)}, f32[2,2,128]{2,1,0:T(2,128)S(1)}, u32[]{:S(2)}, u32[]{:S(2)}) collective-permute-start(f32[2,2,128]{2,1,0:T(2,128)S(1)} %bitcast_select_fusion.3), channel_id=1, source_target_pairs={{0,16},{16,0},{32,48},{48,32},{64,80},{80,64},{96,112},{112,96},{1... | collective-permute-start | bytes 6152 | tf_op jit(solution)/shard_map/ppermute | solution.py:31
  38.0 7.6 %collective-permute-start.6 = (f32[2,2,128]{2,1,0:T(2,128)S(1)}, f32[2,2,128]{2,1,0:T(2,128)S(1)}, u32[]{:S(2)}, u32[]{:S(2)}) collective-permute-start(f32[2,2,128]{2,1,0:T(2,128)S(1)} %get-tuple-element.34), channel_id=1, source_target_pairs={{0,1008},{16,32},{32,16},{48,64},{64,48},{80,96},{96,80},{112,128}... | collective-permute-start | bytes 6152 | tf_op jit(solution)/shard_map/ppermute | solution.py:26
  42.7 3.3 %collective-permute-start.7 = (f32[2,2,128]{2,1,0:T(2,128)S(1)}, f32[2,2,128]{2,1,0:T(2,128)S(1)}, u32[]{:S(2)}, u32[]{:S(2)}) collective-permute-start(f32[2,2,128]{2,1,0:T(2,128)S(1)} %get-tuple-element.43), channel_id=1, source_target_pairs={{15,0},{0,1},{1,2},{2,3},{3,4},{4,5},{5,6},{6,7},{7,8},{8,9},{9,10... | collective-permute-start | bytes 6152 | tf_op jit(solution)/shard_map/ppermute | solution.py:20
  46.2 12.0 %collective-permute-start.8 = (f32[2,2,128]{2,1,0:T(2,128)S(1)}, f32[2,2,128]{2,1,0:T(2,128)S(1)}, u32[]{:S(2)}, u32[]{:S(2)}) collective-permute-start(f32[2,2,128]{2,1,0:T(2,128)S(1)} %get-tuple-element.33), channel_id=1, source_target_pairs={{1,0},{2,1},{3,2},{4,3},{5,4},{6,5},{7,6},{8,7},{9,8},{10,9},{11,1... | collective-permute-start | bytes 6152 | tf_op jit(solution)/shard_map/ppermute | solution.py:20
  48.1 7.7 %collective-permute-start.9 = (f32[2,2,128]{2,1,0:T(2,128)S(1)}, f32[2,2,128]{2,1,0:T(2,128)S(1)}, u32[]{:S(2)}, u32[]{:S(2)}) collective-permute-start(f32[2,2,128]{2,1,0:T(2,128)S(1)} %bitcast_select_fusion.1), channel_id=1, source_target_pairs={{0,16},{16,0},{32,48},{48,32},{64,80},{80,64},{96,112},{112,96},{1... | collective-permute-start | bytes 6152 | tf_op jit(solution)/shard_map/ppermute | solution.py:31
  50.0 8.7 %collective-permute-start.11 = (f32[2,2,128]{2,1,0:T(2,128)S(1)}, f32[2,2,128]{2,1,0:T(2,128)S(1)}, u32[]{:S(2)}, u32[]{:S(2)}) collective-permute-start(f32[2,2,128]{2,1,0:T(2,128)S(1)} %get-tuple-element.41), channel_id=1, source_target_pairs={{15,0},{0,1},{1,2},{2,3},{3,4},{4,5},{5,6},{6,7},{7,8},{8,9},{9,10... | collective-permute-start | bytes 6152 | tf_op jit(solution)/shard_map/ppermute | solution.py:20
  50.6 7.6 %collective-permute-start.10 = (f32[2,2,128]{2,1,0:T(2,128)S(1)}, f32[2,2,128]{2,1,0:T(2,128)S(1)}, u32[]{:S(2)}, u32[]{:S(2)}) collective-permute-start(f32[2,2,128]{2,1,0:T(2,128)S(1)} %get-tuple-element.30), channel_id=1, source_target_pairs={{0,1008},{16,32},{32,16},{48,64},{64,48},{80,96},{96,80},{112,128}... | collective-permute-start | bytes 6152 | tf_op jit(solution)/shard_map/ppermute | solution.py:26

commit v7 on v6

--- a/solution.py
+++ b/solution.py
@@ -53,8 +53,8 @@
 def adjoint(blocks, vector):
     half = blocks.shape[-2]
     wide = blocks.astype(jnp.float32)
-    from_real = jnp.sum(wide * vector[..., None, :half, None], -2)
-    from_imag = jnp.sum(wide * vector[..., None, half:, None], -2)
+    from_real = jnp.sum(wide * vector[..., :half, None], -2)
+    from_imag = jnp.sum(wide * vector[..., half:, None], -2)
     return jnp.concatenate(
         [
             from_real[..., :half] + from_imag[..., half:],
@@ -64,18 +64,40 @@
     )
 
 
-def apply_operator(field, self_block, hop_blocks):
+def turned_blocks(blocks):
+    half = blocks.shape[-2]
+    real, imag = blocks[..., :half], blocks[..., half:]
+    return jnp.concatenate([real, -imag], -1), jnp.concatenate([imag, real], -1)
+
+
+def adjoint_turned(pair, hop, vector):
+    real_blocks, imag_blocks = (part[:, :, hop].astype(jnp.float32) for part in pair)
+    half = real_blocks.shape[-2]
+    terms = real_blocks * vector[..., :half, None] + imag_blocks * vector[..., half:, None]
+    return jnp.sum(terms, -2)
+
+
+def apply_operator(field, self_block, hop_blocks, pair):
     signs = chirality_signs(field.shape[-1])
-    carried = adjoint(hop_blocks, field * signs)
-    ahead_t, behind_t = exchanged(field, carried[:, :, 3], T_AXES)
+    flipped = field * signs
+    if pair is None:
+        carried = lambda hop: adjoint(hop_blocks[:, :, hop], flipped)
+    else:
+        carried = lambda hop: adjoint_turned(pair, hop, flipped)
+    carried_t = carried(3)
+    ahead_t, behind_t = exchanged(field, carried_t, T_AXES)
     ahead_z = shifted(field, Z_AXES, -1)
-    behind_z = shifted(carried[:, :, 2], Z_AXES, 1)
+    carried_z = carried(2)
+    behind_z = shifted(carried_z, Z_AXES, 1)
+    if pair is None:
+        pair = lax.optimization_barrier(turned_blocks(hop_blocks))
     near = forward_sum(self_block[:, :, None], field[:, :, None])
     near_hops = jnp.stack([jnp.roll(field, -1, 1), jnp.roll(field, -1, 0)], 2)
     near = near + forward_sum(hop_blocks[:, :, :2], near_hops)
-    near_back = jnp.roll(carried[:, :, 0], 1, 1) + jnp.roll(carried[:, :, 1], 1, 0)
+    near_back = jnp.roll(carried(0), 1, 1) + jnp.roll(carried(1), 1, 0)
+    near = near + signs * near_back
     far = forward_sum(hop_blocks[:, :, 2:], jnp.stack([ahead_z, ahead_t], 2))
-    return near + far + signs * (near_back + behind_z + behind_t)
+    return near + far + signs * (behind_z + behind_t), pair
 
 
 def gram_body(v0, v1, v2, v3, out):
@@ -215,9 +237,11 @@
     rows = (sites[0] * sites[1], sites[2])
     local_self = self_block[0, 0]
     local_hops = hop_blocks[0, 0]
-    vectors = [right_side[0, 0].astype(jnp.float32)]
+    vectors = [lax.optimization_barrier(right_side[0, 0].astype(jnp.float32))]
+    pair = None
     for _ in range(ITERS):
-        vectors.append(apply_operator(vectors[-1], local_self, local_hops))
+        field, pair = apply_operator(vectors[-1], local_self, local_hops, pair)
+        vectors.append(field)
     flat = [on_chip(v.reshape(rows)) for v in vectors]
     space = pl.BlockSpec(memory_space=pltpu.VMEM)
     near_axes, far_axes = ("tx", "sy", "sc"), "tz"

time: 91.7 us -> 91 us (level)
  blocking collectives: 31.5 us -> 33.8 us
  starting transfers between devices: 44.5 us -> 43 us
  waiting for transfers between devices: 6.13 us -> 4.74 us
    all_to_all x1, blocking collectives: 15 us -> 17.4 us  [on_device(): gathered = lax.all_to_all(copies, near_axes, 0, 0, tiled=True)]
    ppermute x6, waiting for transfers between devices: 1.34 us -> 0.02 us  [shifted(): return lax.ppermute(block, axes, route)]
    ppermute x6, starting transfers between devices: 21.2 us -> 20.3 us  [shifted(): return lax.ppermute(block, axes, route)]
where the time goes in v7:
time: 91 us; the launch traced here: 90.5 us
  starting transfers between devices  43 us (47%)
  blocking collectives  33.8 us (37%)
  other arithmetic  6.06 us (7%)
  waiting for transfers between devices  4.74 us (5%)
  Pallas kernels  1 us (1%)
  between operations  0.95 us (1%)
    ppermute x6, starting transfers between devices, shifted(): return lax.ppermute(block, axes, route)  20.3 us
    all_to_all x1, blocking collectives, on_device(): gathered = lax.all_to_all(copies, near_axes, 0, 0, tiled=True)  17.4 us
    ppermute x3, starting transfers between devices, exchanged(): lax.ppermute(jnp.where(even, field, carried), axes, [(i, (i + (1 if i % 2...  17 us
    all_to_all x1, blocking collectives, on_device(): gathered = lax.all_to_all(copies, far_axes, 0, 0, tiled=True)  16.5 us
    ppermute x3, starting transfers between devices, exchanged(): lax.ppermute(jnp.where(even, carried, field), axes, [(i, i ^ 1) for i in...  5.76 us
    ppermute x3, waiting for transfers between devices, exchanged(): lax.ppermute(jnp.where(even, field, carried), axes, [(i, (i + (1 if i % 2...  4.02 us
  transfers between devices with their start and end apart: 12, of which 3 were waited for; matrix products, arithmetic and copies ran while one was open for 6% of the time, Pallas kernels for 0%

profile of v7, /device:TPU:1, one launch (start us, length us, event | category | flops | bytes accessed | tf_op | source)
XLA Modules:
  0.0 90.5 jit_solution(13279091217524747906)
XLA Ops:
  0.6 0.0 copy-start
  0.6 0.7 bitcast_convert_fusion
  1.4 14.1 %collective-permute-start = (f32[2,2,128]{2,1,0:T(2,128)S(1)}, f32[2,2,128]{2,1,0:T(2,128)S(1)}, u32[]{:S(2)}, u32[]{:S(2)}) collective-permute-start(f32[2,2,128]{2,1,0:T(2,128)S(1)} %bitcast_convert_fusion), channel_id=1, source_target_pairs={{1,0},{2,1},{3,2},{4,3},{5,4},{6,5},{7,6},{8,7},{9,8},{10,9},{11,1... | collective-permute-start | bytes 6152 | tf_op jit(solution)/shard_map/ppermute | solution.py:20
  15.5 0.1 fusion.81
  15.6 1.1 %fusion.13 = (f32[2,2,128]{2,1,0:T(2,128)S(1)}, f32[2,2,128]{2,1,0:T(2,128)S(1)}, f32[2,2,128]{2,1,0:T(2,128)S(1)}, f32[2,2,128]{2,1,0:T(2,128)S(1)}, f32[2,2,12...) fusion(f32[2,2,64]{2,1,0:T(2,128)S(1)} %get-tuple-element.138, ...), kind=kLoop, calls=%fused_computation.58 | loop fusion | flops 651264 | bytes 280576 | tf_op jit(solution)/shard_map/reduce_sum | solution.py:57
  16.7 0.1 slice_add_fusion
  16.8 0.1 pad_maximum_fusion.23
  16.9 0.1 broadcast_select_fusion.5
  17.0 8.7 %collective-permute-start.2 = (f32[2,2,128]{2,1,0:T(2,128)S(1)}, f32[2,2,128]{2,1,0:T(2,128)S(1)}, u32[]{:S(2)}, u32[]{:S(2)}) collective-permute-start(f32[2,2,128]{2,1,0:T(2,128)S(1)} %get-tuple-element.55), channel_id=1, source_target_pairs={{0,1008},{16,32},{32,16},{48,64},{64,48},{80,96},{96,80},{112,128}... | collective-permute-start | bytes 6152 | tf_op jit(solution)/shard_map/ppermute | solution.py:26
  25.7 1.9 %collective-permute-start.1 = (f32[2,2,128]{2,1,0:T(2,128)S(1)}, f32[2,2,128]{2,1,0:T(2,128)S(1)}, u32[]{:S(2)}, u32[]{:S(2)}) collective-permute-start(f32[2,2,128]{2,1,0:T(2,128)S(1)} %get-tuple-element.54), channel_id=1, source_target_pairs={{0,16},{16,0},{32,48},{48,32},{64,80},{80,64},{96,112},{112,96},{1... | collective-permute-start | bytes 6152 | tf_op jit(solution)/shard_map/ppermute | solution.py:31
  27.6 0.1 fusion.65
  27.8 0.1 fusion.78
  27.9 0.2 pad_maximum_fusion.1
  28.0 0.2 pad_maximum_fusion
  28.2 0.1 pad_maximum_fusion.7
  28.3 0.1 slice_add_fusion.2
  28.4 0.1 fusion.56
  28.5 0.1 pad_maximum_fusion.9
  28.5 0.1 maximum_bitcast_fusion.1
  28.6 0.4 copy-done.1
  29.0 0.1 fusion.36
  29.2 0.1 fusion.57
  29.3 0.7 collective-permute-done.1
  30.0 0.1 fusion.59
  30.1 0.1 pad_maximum_fusion.10
  30.2 0.2 fusion
  30.4 0.1 broadcast_multiply_fusion
  30.5 3.2 %collective-permute-start.4 = (f32[2,2,128]{2,1,0:T(2,128)S(1)}, f32[2,2,128]{2,1,0:T(2,128)S(1)}, u32[]{:S(2)}, u32[]{:S(2)}) collective-permute-start(f32[2,2,128]{2,1,0:T(2,128)S(1)} %get-tuple-element.51), channel_id=1, source_target_pairs={{1,0},{2,1},{3,2},{4,3},{5,4},{6,5},{7,6},{8,7},{9,8},{10,9},{11,1... | collective-permute-start | bytes 6152 | tf_op jit(solution)/shard_map/ppermute | solution.py:20
  33.7 0.1 fusion.77
  33.7 0.2 fusion.29
  33.9 0.0 collective-permute-start.7
  34.0 3.0 %collective-permute-start.6 = (f32[2,2,128]{2,1,0:T(2,128)S(1)}, f32[2,2,128]{2,1,0:T(2,128)S(1)}, u32[]{:S(2)}, u32[]{:S(2)}) collective-permute-start(f32[2,2,128]{2,1,0:T(2,128)S(1)} %get-tuple-element.79), channel_id=1, source_target_pairs={{0,1008},{16,32},{32,16},{48,64},{64,48},{80,96},{96,80},{112,128}... | collective-permute-start | bytes 6152 | tf_op jit(solution)/shard_map/ppermute | solution.py:26
  37.0 1.9 %collective-permute-start.5 = (f32[2,2,128]{2,1,0:T(2,128)S(1)}, f32[2,2,128]{2,1,0:T(2,128)S(1)}, u32[]{:S(2)}, u32[]{:S(2)}) collective-permute-start(f32[2,2,128]{2,1,0:T(2,128)S(1)} %get-tuple-element.78), channel_id=1, source_target_pairs={{0,16},{16,0},{32,48},{48,32},{64,80},{80,64},{96,112},{112,96},{1... | collective-permute-start | bytes 6152 | tf_op jit(solution)/shard_map/ppermute | solution.py:31
  39.0 0.1 fusion.72
  39.1 0.1 fusion.60
  39.1 0.1 maximum_bitcast_fusion.5
  39.2 0.2 fusion.38
  39.4 0.1 pad_maximum_fusion.12
  39.5 2.2 %collective-permute-done.6 = f32[2,2,128]{2,1,0:T(2,128)S(1)} collective-permute-done((f32[2,2,128]{2,1,0:T(2,128)S(1)}, f32[2,2,128]{2,1,0:T(2,128)S(1)}, u32[]{:S(2)}, u32[]{:S(2)}) %collective-permute-start.6) | collective-permute-done | bytes 2080 | tf_op jit(solution)/shard_map/ppermute | solution.py:26
  41.6 0.1 pad_maximum_fusion.4
  41.7 0.1 pad_maximum_fusion.15
  41.8 0.2 fusion.8
  42.1 0.1 broadcast_multiply_fusion.1
  42.2 3.0 %collective-permute-start.8 = (f32[2,2,128]{2,1,0:T(2,128)S(1)}, f32[2,2,128]{2,1,0:T(2,128)S(1)}, u32[]{:S(2)}, u32[]{:S(2)}) collective-permute-start(f32[2,2,128]{2,1,0:T(2,128)S(1)} %get-tuple-element.49), channel_id=1, source_target_pairs={{1,0},{2,1},{3,2},{4,3},{5,4},{6,5},{7,6},{8,7},{9,8},{10,9},{11,1... | collective-permute-start | bytes 6152 | tf_op jit(solution)/shard_map/ppermute | solution.py:20
  45.1 0.1 fusion.71
  45.2 0.1 fusion.70
  45.3 0.2 fusion.31
  45.5 1.9 %collective-permute-start.9 = (f32[2,2,128]{2,1,0:T(2,128)S(1)}, f32[2,2,128]{2,1,0:T(2,128)S(1)}, u32[]{:S(2)}, u32[]{:S(2)}) collective-permute-start(f32[2,2,128]{2,1,0:T(2,128)S(1)} %get-tuple-element.67), channel_id=1, source_target_pairs={{0,16},{16,0},{32,48},{48,32},{64,80},{80,64},{96,112},{112,96},{1... | collective-permute-start | bytes 6152 | tf_op jit(solution)/shard_map/ppermute | solution.py:31
  47.4 5.3 %collective-permute-start.10 = (f32[2,2,128]{2,1,0:T(2,128)S(1)}, f32[2,2,128]{2,1,0:T(2,128)S(1)}, u32[]{:S(2)}, u32[]{:S(2)}) collective-permute-start(f32[2,2,128]{2,1,0:T(2,128)S(1)} %get-tuple-element.66), channel_id=1, source_target_pairs={{0,1008},{16,32},{32,16},{48,64},{64,48},{80,96},{96,80},{112,128}... | collective-permute-start | bytes 6152 | tf_op jit(solution)/shard_map/ppermute | solution.py:26
  52.7 0.0 collective-permute-start.11
  52.7 0.1 maximum_bitcast_fusion.9
  52.8 0.2 fusion.40
  53.0 0.1 fusion.62
  53.1 0.1 pad_maximum_fusion.16
  53.2 1.9 %collective-permute-done.10 = f32[2,2,128]{2,1,0:T(2,128)S(1)} collective-permute-done((f32[2,2,128]{2,1,0:T(2,128)S(1)}, f32[2,2,128]{2,1,0:T(2,128)S(1)}, u32[]{:S(2)}, u32[]{:S(2)}) %collective-permute-start.10) | collective-permute-done | bytes 2080 | tf_op jit(solution)/shard_map/ppermute | solution.py:26
  55.1 0.1 pad_maximum_fusion.2
  55.1 0.1 pad_maximum_fusion.19
  55.2 0.2 fusion.10
  55.5 0.1 fusion.54
  55.6 0.2 shard_map.50
  55.8 17.4 %all_to_all.10 = f32[64,1,128]{2,1,0:T(1,128)S(1)} all-to-all(f32[64,1,128]{2,1,0:T(1,128)S(1)} %shard_map.50), channel_id=1, replica_groups=mesh['tz'=16,'tx'=4,'sy'=8,'sc'=2] {'tx','sy','sc'}, dimensions={0} | all-to-all | bytes 65536 | tf_op jit(solution)/shard_map/all_to_all | solution.py:254
  73.1 0.1 reduce_sum.349
  73.2 16.5 %all_to_all.11.gathered = f32[16,1,128]{2,1,0:T(1,128)S(1)} all-to-all(f32[16,1,128]{2,1,0:T(1,128)S(1)} %broadcast_in_dim.25), channel_id=1, replica_groups=mesh['tz'=16,'tx'=4,'sy'=8,'sc'=2] {'tz'}, dimensions={0} | all-to-all | bytes 16384 | tf_op jit(solution)/shard_map/all_to_all | solution.py:257
  89.7 0.8 shard_map.51
  (48 shorter events, 0.2 us)
Async XLA Ops:
  0.6 27.0 %copy-start = (bf16[1,1,2,2,4,64,128]{6,5,4,3,2,1,0:T(8,128)(2,1)S(1)}, bf16[1,1,2,2,4,64,128]{6,5,4,3,2,1,0:T(8,128)(2,1)}, u32[]{:S(2)}) copy-start(bf16[1,1,2,2,4,64,128]{6,5,4,3,2,1,0:T(8,128)(2,1)} %param.5) | copy-start | bytes 786436
  1.4 28.6 %collective-permute-start = (f32[2,2,128]{2,1,0:T(2,128)S(1)}, f32[2,2,128]{2,1,0:T(2,128)S(1)}, u32[]{:S(2)}, u32[]{:S(2)}) collective-permute-start(f32[2,2,128]{2,1,0:T(2,128)S(1)} %bitcast_convert_fusion), channel_id=1, source_target_pairs={{1,0},{2,1},{3,2},{4,3},{5,4},{6,5},{7,6},{8,7},{9,8},{10,9},{11,1... | collective-permute-start | bytes 6152 | tf_op jit(solution)/shard_map/ppermute | solution.py:20
  16.9 13.5 %collective-permute-start.3 = (f32[2,2,128]{2,1,0:T(2,128)S(1)}, f32[2,2,128]{2,1,0:T(2,128)S(1)}, u32[]{:S(2)}, u32[]{:S(2)}) collective-permute-start(f32[2,2,128]{2,1,0:T(2,128)S(1)} %pad_maximum_fusion.23), channel_id=1, source_target_pairs={{15,0},{0,1},{1,2},{2,3},{3,4},{4,5},{5,6},{6,7},{7,8},{8,9},{9,10... | collective-permute-start | bytes 6152 | tf_op jit(solution)/shard_map/ppermute | solution.py:20
  17.0 12.3 %collective-permute-start.2 = (f32[2,2,128]{2,1,0:T(2,128)S(1)}, f32[2,2,128]{2,1,0:T(2,128)S(1)}, u32[]{:S(2)}, u32[]{:S(2)}) collective-permute-start(f32[2,2,128]{2,1,0:T(2,128)S(1)} %get-tuple-element.55), channel_id=1, source_target_pairs={{0,1008},{16,32},{32,16},{48,64},{64,48},{80,96},{96,80},{112,128}... | collective-permute-start | bytes 6152 | tf_op jit(solution)/shard_map/ppermute | solution.py:26
  25.7 4.3 %collective-permute-start.1 = (f32[2,2,128]{2,1,0:T(2,128)S(1)}, f32[2,2,128]{2,1,0:T(2,128)S(1)}, u32[]{:S(2)}, u32[]{:S(2)}) collective-permute-start(f32[2,2,128]{2,1,0:T(2,128)S(1)} %get-tuple-element.54), channel_id=1, source_target_pairs={{0,16},{16,0},{32,48},{48,32},{64,80},{80,64},{96,112},{112,96},{1... | collective-permute-start | bytes 6152 | tf_op jit(solution)/shard_map/ppermute | solution.py:31
  28.2 0.8 copy-start.1
  30.5 11.1 %collective-permute-start.4 = (f32[2,2,128]{2,1,0:T(2,128)S(1)}, f32[2,2,128]{2,1,0:T(2,128)S(1)}, u32[]{:S(2)}, u32[]{:S(2)}) collective-permute-start(f32[2,2,128]{2,1,0:T(2,128)S(1)} %get-tuple-element.51), channel_id=1, source_target_pairs={{1,0},{2,1},{3,2},{4,3},{5,4},{6,5},{7,6},{8,7},{9,8},{10,9},{11,1... | collective-permute-start | bytes 6152 | tf_op jit(solution)/shard_map/ppermute | solution.py:20
  33.9 8.1 %collective-permute-start.7 = (f32[2,2,128]{2,1,0:T(2,128)S(1)}, f32[2,2,128]{2,1,0:T(2,128)S(1)}, u32[]{:S(2)}, u32[]{:S(2)}) collective-permute-start(f32[2,2,128]{2,1,0:T(2,128)S(1)} %get-tuple-element.17), channel_id=1, source_target_pairs={{15,0},{0,1},{1,2},{2,3},{3,4},{4,5},{5,6},{6,7},{7,8},{8,9},{9,10... | collective-permute-start | bytes 6152 | tf_op jit(solution)/shard_map/ppermute | solution.py:20
  34.0 7.6 %collective-permute-start.6 = (f32[2,2,128]{2,1,0:T(2,128)S(1)}, f32[2,2,128]{2,1,0:T(2,128)S(1)}, u32[]{:S(2)}, u32[]{:S(2)}) collective-permute-start(f32[2,2,128]{2,1,0:T(2,128)S(1)} %get-tuple-element.79), channel_id=1, source_target_pairs={{0,1008},{16,32},{32,16},{48,64},{64,48},{80,96},{96,80},{112,128}... | collective-permute-start | bytes 6152 | tf_op jit(solution)/shard_map/ppermute | solution.py:26
  37.0 4.6 %collective-permute-start.5 = (f32[2,2,128]{2,1,0:T(2,128)S(1)}, f32[2,2,128]{2,1,0:T(2,128)S(1)}, u32[]{:S(2)}, u32[]{:S(2)}) collective-permute-start(f32[2,2,128]{2,1,0:T(2,128)S(1)} %get-tuple-element.78), channel_id=1, source_target_pairs={{0,16},{16,0},{32,48},{48,32},{64,80},{80,64},{96,112},{112,96},{1... | collective-permute-start | bytes 6152 | tf_op jit(solution)/shard_map/ppermute | solution.py:31
  42.2 12.9 %collective-permute-start.8 = (f32[2,2,128]{2,1,0:T(2,128)S(1)}, f32[2,2,128]{2,1,0:T(2,128)S(1)}, u32[]{:S(2)}, u32[]{:S(2)}) collective-permute-start(f32[2,2,128]{2,1,0:T(2,128)S(1)} %get-tuple-element.49), channel_id=1, source_target_pairs={{1,0},{2,1},{3,2},{4,3},{5,4},{6,5},{7,6},{8,7},{9,8},{10,9},{11,1... | collective-permute-start | bytes 6152 | tf_op jit(solution)/shard_map/ppermute | solution.py:20
  45.5 7.7 %collective-permute-start.9 = (f32[2,2,128]{2,1,0:T(2,128)S(1)}, f32[2,2,128]{2,1,0:T(2,128)S(1)}, u32[]{:S(2)}, u32[]{:S(2)}) collective-permute-start(f32[2,2,128]{2,1,0:T(2,128)S(1)} %get-tuple-element.67), channel_id=1, source_target_pairs={{0,16},{16,0},{32,48},{48,32},{64,80},{80,64},{96,112},{112,96},{1... | collective-permute-start | bytes 6152 | tf_op jit(solution)/shard_map/ppermute | solution.py:31
  47.4 7.6 %collective-permute-start.10 = (f32[2,2,128]{2,1,0:T(2,128)S(1)}, f32[2,2,128]{2,1,0:T(2,128)S(1)}, u32[]{:S(2)}, u32[]{:S(2)}) collective-permute-start(f32[2,2,128]{2,1,0:T(2,128)S(1)} %get-tuple-element.66), channel_id=1, source_target_pairs={{0,1008},{16,32},{32,16},{48,64},{64,48},{80,96},{96,80},{112,128}... | collective-permute-start | bytes 6152 | tf_op jit(solution)/shard_map/ppermute | solution.py:26
  52.7 2.8 %collective-permute-start.11 = (f32[2,2,128]{2,1,0:T(2,128)S(1)}, f32[2,2,128]{2,1,0:T(2,128)S(1)}, u32[]{:S(2)}, u32[]{:S(2)}) collective-permute-start(f32[2,2,128]{2,1,0:T(2,128)S(1)} %get-tuple-element.16), channel_id=1, source_target_pairs={{15,0},{0,1},{1,2},{2,3},{3,4},{4,5},{5,6},{6,7},{7,8},{8,9},{9,10... | collective-permute-start | bytes 6152 | tf_op jit(solution)/shard_map/ppermute | solution.py:20
